TPU v7x, 32 devices: a whole 2x2x4 slice. The times are simulated.
32 devices in a mesh: dp: 4 (over z), row: 4 (over x, core), col: 2 (over y).
Axes of the slice: x: 2, y: 2, z: 4, core: 2. Of those that a mesh axis runs over, the one named last changes fastest.
Arguments:
- block_input: bfloat16 [2, 16384, 768], P(None, ('dp', 'row', 'col')), may hold values from -6 to 6
- segment_ids: int32 [2, 16384], P(None, ('dp', 'row', 'col')), may hold values from 0 to 127, never falling along the last dimension, each value on 1 to 512 neighbouring positions
- bucket: int32 [1023], replicated, may hold values from 0 to 31
- gain_attn: bfloat16 [768], P(('row', 'col')), may hold values from 0.5 to 1.5
- w_query: bfloat16 [768, 768], P('row', 'col'), may hold values from -0.0546875 to 0.0546875
- w_key: bfloat16 [768, 768], P('row', 'col'), may hold values from -0.21875 to 0.21875
- w_value: bfloat16 [768, 768], P('row', 'col'), may hold values from -0.21875 to 0.21875
- w_out: bfloat16 [768, 768], P('row', 'col'), may hold values from -0.875 to 0.875
- bias_table: float32 [32, 12], replicated, may hold values from -4 to 4
- gain_ffn: bfloat16 [768], P(('row', 'col')), may hold values from 0.5 to 1.5
- w_gate: bfloat16 [768, 2048], P('row', 'col'), may hold values from -0.21875 to 0.21875
- w_up: bfloat16 [768, 2048], P('row', 'col'), may hold values from -0.21875 to 0.21875
- w_down: bfloat16 [2048, 768], P('row', 'col'), may hold values from -0.125 to 0.125
- cotangent: bfloat16 [2, 16384, 768], P(None, ('dp', 'row', 'col')), may hold values from -6 to 6
Outputs:
- block_output: bfloat16 [2, 16384, 768], P(None, ('dp', 'row', 'col'))
- grad_input: bfloat16 [2, 16384, 768], P(None, ('dp', 'row', 'col'))
- grad_gain_attn: float32 [768], P(('row', 'col'))
- grad_query: float32 [768, 768], P('row', 'col')
- grad_key: float32 [768, 768], P('row', 'col')
- grad_value: float32 [768, 768], P('row', 'col')
- grad_out: float32 [768, 768], P('row', 'col')
- grad_table: float32 [32, 12], replicated
- grad_gain_ffn: float32 [768], P(('row', 'col'))
- grad_gate: float32 [768, 2048], P('row', 'col')
- grad_up: float32 [768, 2048], P('row', 'col')
- grad_down: float32 [2048, 768], P('row', 'col')
Inputs may be any that keep to these rules, and one draw needn't show every extreme that they name: `segment_ids`: segment ids never fall along the tokens of a micro-batch; a document has 1 to 512 tokens, one has exactly 512. Entry n is the bucket of a key standing n - 511 tokens after its query.
All inputs are finite; a program needn't handle non-finite values.
Results may differ from a plain program's by a relative error of at most 0.017.
Values may be sent and summed in bfloat16 or wider, within the bound.
A program may use at most 320 MiB of HBM per device.

v0:
```python
import jax
import jax.numpy as jnp
from jax import lax
from jax.sharding import PartitionSpec as P

H = 12
DH = 64


EPSILON = 1e-06
NEGATIVE = -1e30
PRECISE = lax.Precision.HIGHEST


def norm_scale(values, gain):
    mean_square = jnp.mean(values * values, axis=-1, keepdims=True)
    return values * lax.rsqrt(mean_square + EPSILON) * gain


def gated_gelu(gate_act, up_act):
    return jax.nn.gelu(gate_act, approximate=True) * up_act


def product(left, right):
    return jnp.dot(left, right, preferred_element_type=jnp.float32)


def left_product(left, right):
    return lax.dot_general(
        left, right, (((0,), (0,)), ((), ())), preferred_element_type=jnp.float32
    )


def right_product(left, right):
    return lax.dot_general(
        left, right, (((1,), (1,)), ((), ())), preferred_element_type=jnp.float32
    )


def make_offsets(bias_table, bucket):
    classes = jnp.arange(bias_table.shape[0], dtype=jnp.int32)
    onehot = (bucket[:, None] == classes[None, :]).astype(bias_table.dtype)
    looked = jnp.dot(onehot, bias_table, precision=PRECISE, preferred_element_type=jnp.float32)
    return jnp.pad(looked.T, ((0, 0), (0, 1)))


def bias_block(offsets, start_row, block_rows):
    head_count, twice_len = offsets.shape
    length = twice_len // 2
    tiled = jnp.tile(offsets, (1, block_rows))[:, : block_rows * (twice_len - 1)]
    skewed = tiled.reshape(head_count, block_rows, twice_len - 1)
    return lax.dynamic_slice_in_dim(skewed, length - 1 - start_row, length, 2)


def open_block(gathered, row_count, column_count):
    span_rows = gathered.shape[1]
    span_cols = gathered.shape[2]
    grid = gathered.reshape(row_count, column_count, span_rows, span_cols).transpose(0, 2, 1, 3)
    return grid.reshape(row_count * span_rows, column_count * span_cols)


def open_all(gathered, row_count, column_count):
    return tuple(
        (
            piece.reshape(-1) if piece.ndim == 2 else open_block(piece, row_count, column_count)
            for piece in gathered
        )
    )


def close_block(full, row_count, column_count):
    span_rows = full.shape[0] // row_count
    span_cols = full.shape[1] // column_count
    grid = full.reshape(row_count, span_rows, column_count, span_cols).transpose(0, 2, 1, 3)
    return grid.reshape(row_count * column_count, span_rows, span_cols)


def close_all(fulls, row_count, column_count):
    return tuple(
        (
            (
                full.reshape(row_count * column_count, -1)
                if full.ndim == 1
                else close_block(full, row_count, column_count)
            )
            for full in fulls
        )
    )


def add_all(totals, fresh):
    if totals is None:
        return fresh
    return tuple((older + newer for older, newer in zip(totals, fresh)))


def masked_scores(query_block, key_heads, segment_ids, bias_now):
    raw_scores = jnp.einsum(
        "qhd,khd->hqk", query_block, key_heads, preferred_element_type=jnp.float32
    )
    raw_scores = raw_scores + bias_now
    allowed = segment_ids[:, None] == segment_ids[None, :]
    return jnp.where(allowed[None], raw_scores, NEGATIVE)


def attend_forward(queries, keys_low, values_low, segment_ids, offsets):
    length = queries.shape[0]
    block_rows = min(512, length)
    query_heads = queries.reshape(length, H, DH)
    key_heads = keys_low.reshape(length, H, DH)
    value_heads = values_low.reshape(length, H, DH)

    def one_block(start_row):
        scores = masked_scores(
            query_heads, key_heads, segment_ids, bias_block(offsets, start_row, block_rows)
        )
        row_max = jnp.max(scores, axis=-1, keepdims=True)
        summed = jnp.sum(jnp.exp(scores - row_max), axis=-1, keepdims=True)
        log_total = row_max + jnp.log(summed)
        softmax_low = jnp.exp(scores - log_total).astype(jnp.bfloat16)
        attended = jnp.einsum(
            "hqk,khd->qhd", softmax_low, value_heads, preferred_element_type=jnp.float32
        )
        return (attended.reshape(block_rows, H * DH).astype(jnp.bfloat16), log_total)

    starts = jnp.arange(length // block_rows, dtype=jnp.int32) * block_rows
    attended, log_totals = lax.map(one_block, starts)
    return (attended.reshape(length, H * DH), log_totals)


def attend_backward(queries, keys_low, values_low, segment_ids, offsets, log_totals, d_attended):
    length = queries.shape[0]
    block_rows = min(512, length)
    query_heads = queries.reshape(length, H, DH)
    key_heads = keys_low.reshape(length, H, DH)
    value_heads = values_low.reshape(length, H, DH)
    grad_heads = d_attended.reshape(length, H, DH)

    def one_block(carry, packed):
        key_sum, value_sum, offset_sum = carry
        start_row, log_total = packed
        bias_now, bias_pull = jax.vjp(
            lambda table_row: bias_block(table_row, start_row, block_rows), offsets
        )
        scores = masked_scores(query_heads, key_heads, segment_ids, bias_now)
        softmax_f = jnp.exp(scores - log_total)
        softmax_low = softmax_f.astype(jnp.bfloat16)
        value_sum = value_sum + jnp.einsum(
            "hqk,qhd->khd", softmax_low, grad_heads, preferred_element_type=jnp.float32
        )
        d_softmax = jnp.einsum(
            "qhd,khd->hqk", grad_heads, value_heads, preferred_element_type=jnp.float32
        )
        inner = jnp.sum(softmax_f * d_softmax, axis=-1, keepdims=True)
        d_scores = (softmax_f * (d_softmax - inner)).astype(jnp.bfloat16)
        query_grad = jnp.einsum(
            "hqk,khd->qhd", d_scores, key_heads, preferred_element_type=jnp.float32
        )
        key_sum = key_sum + jnp.einsum(
            "hqk,qhd->khd", d_scores, query_heads, preferred_element_type=jnp.float32
        )
        offset_sum = offset_sum + bias_pull(d_scores.astype(jnp.float32))[0]
        return ((key_sum, value_sum, offset_sum), query_grad.astype(jnp.bfloat16))

    starts = jnp.arange(length // block_rows, dtype=jnp.int32) * block_rows
    zero_heads = jnp.zeros((length, H, DH), jnp.float32)
    initial = (zero_heads, zero_heads, jnp.zeros_like(offsets))
    (key_sum, value_sum, offset_sum), query_grads = lax.scan(
        one_block, initial, (starts, log_totals)
    )
    d_queries = query_grads.reshape(length, H * DH)
    d_keys = key_sum.reshape(length, H * DH).astype(jnp.bfloat16)
    d_values = value_sum.reshape(length, H * DH).astype(jnp.bfloat16)
    return (d_queries, d_keys, d_values, offset_sum)


def shards(
    block_input,
    segment_ids,
    bucket,
    gain_attn,
    w_query,
    w_key,
    w_value,
    w_out,
    bias_table,
    gain_ffn,
    w_gate,
    w_up,
    w_down,
    cotangent,
):
    row_count = lax.axis_size("row")
    column_count = lax.axis_size("col")
    first_gain = gain_attn[None]
    query_piece = w_query[None]
    key_piece = w_key[None]
    value_piece = w_value[None]
    out_piece = w_out[None]
    second_gain = gain_ffn[None]
    gate_piece = w_gate[None]
    up_piece = w_up[None]
    down_piece = w_down[None]
    offsets, offsets_pull = jax.vjp(lambda values: make_offsets(values, bucket), bias_table)
    totals = None
    shares = None
    offsets_total = jnp.zeros_like(offsets)
    outputs = []
    inputs_grads = []
    for batch_index in range(block_input.shape[0]):
        whole = open_all(
            (
                lax.all_gather(first_gain, ("row", "col"), axis=0, tiled=True),
                lax.all_gather(query_piece, ("row", "col"), axis=0, tiled=True),
                lax.all_gather(key_piece, ("row", "col"), axis=0, tiled=True),
                lax.all_gather(value_piece, ("row", "col"), axis=0, tiled=True),
                lax.all_gather(out_piece, ("row", "col"), axis=0, tiled=True),
                lax.all_gather(second_gain, ("row", "col"), axis=0, tiled=True),
                lax.all_gather(gate_piece, ("row", "col"), axis=0, tiled=True),
                lax.all_gather(up_piece, ("row", "col"), axis=0, tiled=True),
                lax.all_gather(down_piece, ("row", "col"), axis=0, tiled=True),
            ),
            row_count,
            column_count,
        )
        (
            gain_one,
            query_full,
            key_full,
            value_full,
            out_full,
            gain_two,
            gate_full,
            up_full,
            down_full,
        ) = whole
        segment_now = segment_ids[batch_index]
        inputs = block_input[batch_index].astype(jnp.float32)
        normed_f, pull_one = jax.vjp(norm_scale, inputs, gain_one.astype(jnp.float32))
        normed = normed_f.astype(jnp.bfloat16)
        queries = product(normed, query_full).astype(jnp.bfloat16)
        keys_low = product(normed, key_full).astype(jnp.bfloat16)
        values_low = product(normed, value_full).astype(jnp.bfloat16)
        attended, log_totals = attend_forward(queries, keys_low, values_low, segment_now, offsets)
        middle = inputs + product(attended, out_full)
        normed_two_f, pull_two = jax.vjp(norm_scale, middle, gain_two.astype(jnp.float32))
        normed_two = normed_two_f.astype(jnp.bfloat16)
        gate_act = product(normed_two, gate_full)
        up_act = product(normed_two, up_full)
        activated, active_pull = jax.vjp(gated_gelu, gate_act, up_act)
        hidden = activated.astype(jnp.bfloat16)
        result = middle + product(hidden, down_full)
        outputs.append(result.astype(jnp.bfloat16))
        whole = open_all(
            (
                lax.all_gather(first_gain, ("row", "col"), axis=0, tiled=True),
                lax.all_gather(query_piece, ("row", "col"), axis=0, tiled=True),
                lax.all_gather(key_piece, ("row", "col"), axis=0, tiled=True),
                lax.all_gather(value_piece, ("row", "col"), axis=0, tiled=True),
                lax.all_gather(out_piece, ("row", "col"), axis=0, tiled=True),
                lax.all_gather(second_gain, ("row", "col"), axis=0, tiled=True),
                lax.all_gather(gate_piece, ("row", "col"), axis=0, tiled=True),
                lax.all_gather(up_piece, ("row", "col"), axis=0, tiled=True),
                lax.all_gather(down_piece, ("row", "col"), axis=0, tiled=True),
            ),
            row_count,
            column_count,
        )
        (
            gain_one,
            query_full,
            key_full,
            value_full,
            out_full,
            gain_two,
            gate_full,
            up_full,
            down_full,
        ) = whole
        d_result = cotangent[batch_index]
        grad_down = left_product(hidden, d_result)
        d_hidden = right_product(d_result, down_full)
        d_gate, d_up = active_pull(d_hidden)
        d_gate = d_gate.astype(jnp.bfloat16)
        d_up = d_up.astype(jnp.bfloat16)
        grad_gate = left_product(normed_two, d_gate)
        grad_up = left_product(normed_two, d_up)
        d_normed_two = right_product(d_gate, gate_full) + right_product(d_up, up_full)
        d_middle_norm, grad_gain_two = pull_two(d_normed_two)
        d_middle = d_result.astype(jnp.float32) + d_middle_norm
        d_middle_low = d_middle.astype(jnp.bfloat16)
        grad_out = left_product(attended, d_middle_low)
        d_attended = right_product(d_middle_low, out_full).astype(jnp.bfloat16)
        d_queries, d_keys, d_values, d_offsets = attend_backward(
            queries, keys_low, values_low, segment_now, offsets, log_totals, d_attended
        )
        offsets_total = offsets_total + d_offsets
        grad_query = left_product(normed, d_queries)
        grad_key = left_product(normed, d_keys)
        grad_value = left_product(normed, d_values)
        d_normed = (
            right_product(d_queries, query_full)
            + right_product(d_keys, key_full)
            + right_product(d_values, value_full)
        )
        d_input_norm, grad_gain_one = pull_one(d_normed)
        inputs_grads.append((d_middle + d_input_norm).astype(jnp.bfloat16))
        fresh = (
            grad_gain_one,
            grad_query,
            grad_key,
            grad_value,
            grad_out,
            grad_gain_two,
            grad_gate,
            grad_up,
            grad_down,
        )
        totals = add_all(totals, fresh)
    pieces = close_all(totals, row_count, column_count)
    shares = (
        lax.psum_scatter(pieces[0], ("row", "col"), scatter_dimension=0, tiled=True),
        lax.psum_scatter(pieces[1], ("row", "col"), scatter_dimension=0, tiled=True),
        lax.psum_scatter(pieces[2], ("row", "col"), scatter_dimension=0, tiled=True),
        lax.psum_scatter(pieces[3], ("row", "col"), scatter_dimension=0, tiled=True),
        lax.psum_scatter(pieces[4], ("row", "col"), scatter_dimension=0, tiled=True),
        lax.psum_scatter(pieces[5], ("row", "col"), scatter_dimension=0, tiled=True),
        lax.psum_scatter(pieces[6], ("row", "col"), scatter_dimension=0, tiled=True),
        lax.psum_scatter(pieces[7], ("row", "col"), scatter_dimension=0, tiled=True),
        lax.psum_scatter(pieces[8], ("row", "col"), scatter_dimension=0, tiled=True),
    )
    reduced = (
        lax.psum(shares[0].astype(jnp.bfloat16), "dp").astype(jnp.float32),
        lax.psum(shares[1].astype(jnp.bfloat16), "dp").astype(jnp.float32),
        lax.psum(shares[2].astype(jnp.bfloat16), "dp").astype(jnp.float32),
        lax.psum(shares[3].astype(jnp.bfloat16), "dp").astype(jnp.float32),
        lax.psum(shares[4].astype(jnp.bfloat16), "dp").astype(jnp.float32),
        lax.psum(shares[5].astype(jnp.bfloat16), "dp").astype(jnp.float32),
        lax.psum(shares[6].astype(jnp.bfloat16), "dp").astype(jnp.float32),
        lax.psum(shares[7].astype(jnp.bfloat16), "dp").astype(jnp.float32),
        lax.psum(shares[8].astype(jnp.bfloat16), "dp").astype(jnp.float32),
    )
    reduced = tuple((piece.reshape(piece.shape[1:]) for piece in reduced))
    table_local = offsets_pull(offsets_total)[0]
    table_grad = lax.psum(table_local, ("dp", "row", "col"))
    return (
        jnp.stack(outputs),
        jnp.stack(inputs_grads),
        reduced[0],
        reduced[1],
        reduced[2],
        reduced[3],
        reduced[4],
        table_grad,
        reduced[5],
        reduced[6],
        reduced[7],
        reduced[8],
    )


def solution(mesh):
    placed = (
        P(None, ("dp", "row", "col"), None),
        P(None, ("dp", "row", "col")),
        P(),
        P(("row", "col")),
        P("row", "col"),
        P("row", "col"),
        P("row", "col"),
        P("row", "col"),
        P(),
        P(("row", "col")),
        P("row", "col"),
        P("row", "col"),
        P("row", "col"),
        P(None, ("dp", "row", "col"), None),
    )
    return jax.shard_map(
        shards,
        mesh=mesh,
        in_specs=placed,
        out_specs=(
            P(None, ("dp", "row", "col"), None),
            P(None, ("dp", "row", "col"), None),
            P(("row", "col")),
            P("row", "col"),
            P("row", "col"),
            P("row", "col"),
            P("row", "col"),
            P(),
            P(("row", "col")),
            P("row", "col"),
            P("row", "col"),
            P("row", "col"),
        ),
        check_vma=False,
    )
```

profile of v0, /device:TPU:0, one launch (start us, length us, event | category | flops | bytes accessed | tf_op | source)
XLA Modules:
  0.0 890.0 jit_solution(13271986183534080764)
XLA Ops:
  15.6 15.2 %all-reduce.10 = (bf16[768]{0:T(1024)(128)(2,1)S(1)}, bf16[768]{0:T(1024)(128)(2,1)S(1)}) all-reduce(bf16[768]{0:T(1024)(128)(2,1)S(1)} %dynamic-update-slice, bf16[768]{0:T(1024)(128)(2,1)S(1)} %dynamic-update-slice.1), channel_id=2, replica_groups=mesh['dp'=4,'row'=4,'col'=2] {'row','col'}, use_global_device_ids=true, to_apply=%add.5 | all-reduce | flops 1536 | bytes 6144
  31.8 11.6 %tile.44 = f32[12,512,1024]{2,1,0:T(8,128)} broadcast(f32[12,1024]{1,0:T(8,128)S(1)} %pad.23), dimensions={0,2} | broadcast | bytes 25214976 | tf_op jit(solution)/shard_map/while/body/eval_jaxpr/tile | solution.py:50
  43.4 11.0 %pad.33 = f32[16,512,1024]{2,1,0:T(8,128)S(1)} pad(f32[12,512,1024]{2,1,0:T(8,128)} %tile.44, f32[]{:T(128)} %constant.113.clone.1), padding=0_4x0_0x0_0 | pad | bytes 58720260
  54.4 39.7 %copy.137 = f32[2,8,512,1024]{3,1,2,0:T(8,128)} copy(f32[2,8,512,1024]{3,2,1,0:T(8,128)S(1)} %bitcast.301) | data formatting | bytes 67108864
  94.1 22.8 %slice.37 = f32[12,523776]{1,0:T(8,128)} slice(f32[12,524288]{1,0:T(8,128)} %bitcast.302), slice={[0:12], [0:523776]} | slice | bytes 50282496 | tf_op jit(solution)/shard_map/while/body/eval_jaxpr/slice | solution.py:50
  116.8 51.6 %reshape.674 = f32[12,512,1023]{2,1,0:T(8,128)} reshape(f32[12,523776]{1,0:T(8,128)} %slice.37) | data formatting | bytes 50282496 | tf_op jit(solution)/shard_map/while/body/eval_jaxpr/reshape | solution.py:51
  168.5 13.9 %dynamic_slice.25 = f32[12,512,512]{2,1,0:T(8,128)} slice(f32[12,512,1023]{2,1,0:T(8,128)} %reshape.674), slice={[0:12], [0:512], [511:1023]} | slice | bytes 25165824 | tf_op jit(solution)/shard_map/while/body/eval_jaxpr/dynamic_slice | solution.py:52
  182.4 12.8 %copy.131 = f32[12,512,512]{1,2,0:T(8,128)} copy(f32[12,512,512]{2,1,0:T(8,128)} %dynamic_slice.25) | data formatting | bytes 25165824
  217.1 6.6 fusion.116
  236.6 6.9 fusion.52
  245.6 6.5 fusion.115
  261.1 5.4 copy.99
  269.2 5.3 copy.100
  284.1 5.3 copy.101
  293.2 6.5 multiply_convert_fusion.3
  310.4 6.5 multiply_convert_fusion.2
  327.6 12.3 %multiply_reduce_fusion = (f32[12,512]{1,0:T(8,128)S(1)}, f32[12,512,512]{1,2,0:T(8,128)}) fusion(f32[12,512,512]{1,2,0:T(8,128)} %copy-done.3, f32[12,512]{1,0:T(8,128)S(1)} %log_add_fusion, bf16[512,12,64]{0,2,1:T(8,128)(2,1)} %bitcast.330, bf16[512,12,64]{0,2,1:T(8,128)(2,1)} %bitcast.328), kind=kOutput, calls=%fused_computation.5 | convolution fusion | flops 412084224 | bytes 26787840 | tf_op jit(solution)/shard_map/while/body/eval_jaxpr/qhd,khd->hqk/dot_general | solution.py:151
  339.9 7.4 multiply_convert_fusion
  355.2 12.3 %multiply_reduce_fusion.1 = (f32[12,512]{1,0:T(8,128)S(1)}, f32[12,512,512]{1,2,0:T(8,128)}) fusion(f32[12,512,512]{1,2,0:T(8,128)} %copy-done.2, f32[12,512]{1,0:T(8,128)S(1)} %log_add_fusion.1, bf16[512,12,64]{0,2,1:T(8,128)(2,1)} %bitcast.332, bf16[512,12,64]{0,2,1:T(8,128)(2,1)} %bitcast.327), kind=kOutput, calls=%fused_computation.7 | convolution fusion | flops 412084224 | bytes 26787840 | tf_op jit(solution)/shard_map/while/body/eval_jaxpr/qhd,khd->hqk/dot_general | solution.py:151
  367.5 7.0 multiply_convert_fusion.1
  388.7 5.0 convolution_convert_fusion.10
  395.7 5.2 convolution_convert_fusion.8
  411.4 7.0 fusion.55
  420.3 6.6 fusion.61
  459.1 9.2 %reshape.716 = f32[4,192,2,1024]{3,2,1,0:T(2,128)} reshape(f32[768,2048]{1,0:T(8,128)} %convolution_add_fusion.2) | data formatting | bytes 12582912 | tf_op jit(solution)/shard_map/reshape | solution.py:74
  468.3 7.4 copy.120
  476.1 8.7 copy.133
  488.5 4.7 convolution_add_fusion.1
  493.2 9.2 %reshape.720 = f32[4,192,2,1024]{3,2,1,0:T(2,128)} reshape(f32[768,2048]{1,0:T(8,128)} %convolution_add_fusion.1) | data formatting | bytes 12582912 | tf_op jit(solution)/shard_map/reshape | solution.py:74
  502.4 7.5 copy.121
  509.9 10.8 %dynamic_update_slice.24.clone = bf16[12,512,1023]{2,1,0:T(8,128)(2,1)} pad(bf16[12,512,512]{2,1,0:T(8,128)(2,1)} %copy.133, bf16[]{:T(256)} %constant.125.clone.1), padding=0_0x0_0x511_0 | pad | bytes 18862082 | tf_op jit(solution)/shard_map/while/body/eval_jaxpr/transpose(jvp())/dynamic_update_slice | solution.py:52
  520.7 35.0 %reshape.711 = bf16[12,523776]{1,0:T(8,128)(2,1)} reshape(bf16[12,512,1023]{2,1,0:T(8,128)(2,1)} %dynamic_update_slice.24.clone) | data formatting | bytes 25141248 | tf_op jit(solution)/shard_map/while/body/eval_jaxpr/transpose(jvp())/reshape | solution.py:51
  555.8 18.6 %pad_convert_fusion = f32[12,524288]{1,0:T(8,128)} fusion(bf16[12,523776]{1,0:T(8,128)(2,1)} %reshape.711), kind=kLoop, calls=%fused_computation.2 | loop fusion | flops 6291456 | bytes 37736448 | tf_op jit(solution)/shard_map/while/body/eval_jaxpr/transpose(jvp())/reshape | solution.py:50
  574.4 9.0 %copy.132 = bf16[12,512,512]{2,1,0:T(8,128)(2,1)} copy(bf16[12,512,512]{1,2,0:T(8,128)(2,1)} %copy-done.4) | data formatting | bytes 12582912
  587.3 4.7 convolution_add_fusion
  592.0 8.5 reshape.724
  600.5 5.9 copy.122
  606.3 10.7 %dynamic_update_slice.23.clone = bf16[12,512,1023]{2,1,0:T(8,128)(2,1)} pad(bf16[12,512,512]{2,1,0:T(8,128)(2,1)} %copy.132, bf16[]{:T(256)} %constant.125.clone.1), padding=0_0x0_0x511_0 | pad | bytes 18862082 | tf_op jit(solution)/shard_map/while/body/eval_jaxpr/transpose(jvp())/dynamic_update_slice | solution.py:52
  617.1 35.8 %reshape.708 = bf16[12,523776]{1,0:T(8,128)(2,1)} reshape(bf16[12,512,1023]{2,1,0:T(8,128)(2,1)} %dynamic_update_slice.23.clone) | data formatting | bytes 25141248 | tf_op jit(solution)/shard_map/while/body/eval_jaxpr/transpose(jvp())/reshape | solution.py:51
  653.0 18.8 %pad_convert_fusion.1 = f32[12,524288]{1,0:T(8,128)} fusion(bf16[12,523776]{1,0:T(8,128)(2,1)} %reshape.708), kind=kLoop, calls=%fused_computation.3 | loop fusion | flops 6291456 | bytes 37736448 | tf_op jit(solution)/shard_map/while/body/eval_jaxpr/transpose(jvp())/reshape | solution.py:50
  681.1 13.5 %all-reduce.9 = (bf16[8,96]{1,0:T(8,128)(2,1)S(1)}, bf16[8,96]{1,0:T(8,128)(2,1)S(1)}) all-reduce(f32[8,96]{1,0:T(8,128)S(1)} %add.268, f32[8,96]{1,0:T(8,128)S(1)} %add.275), channel_id=11, replica_groups=mesh['dp'=4,'row'=4,'col'=2] {'row','col'}, use_global_device_ids=true, to_apply=%region_16.17.clone | all-reduce | flops 1536 | bytes 9216
  695.2 12.1 %all-reduce.11 = (bf16[96]{0:T(256)(128)(2,1)S(1)}, bf16[96]{0:T(256)(128)(2,1)S(1)}) all-reduce(bf16[96]{0:T(256)(128)(2,1)S(1)} %get-tuple-element.189, bf16[96]{0:T(256)(128)(2,1)S(1)} %get-tuple-element.190), channel_id=1, replica_groups=mesh['dp'=4,'row'=4,'col'=2] {'dp'}, use_global_device_ids=true, to_apply=%region_17.18 | all-reduce | flops 192 | bytes 768 | tf_op jit(solution)/shard_map/psum | solution.py:333
  707.8 28.8 %copy.143 = f32[2,8,512,1024]{3,2,1,0:T(8,128)S(1)} copy(f32[2,8,512,1024]{3,1,2,0:T(8,128)} %bitcast.299) | data formatting | bytes 67108864
  736.6 32.1 %copy.142 = f32[2,8,512,1024]{3,2,1,0:T(8,128)} copy(f32[2,8,512,1024]{3,1,2,0:T(8,128)} %bitcast.300) | data formatting | bytes 67108864
  773.9 10.1 %slice_reduce_fusion = (f32[12,1024]{1,0:T(8,128)S(1)}, f32[12,1024]{1,0:T(8,128)S(1)}) fusion(f32[16,512,1024]{2,1,0:T(8,128)S(1)} %bitcast.303, f32[16,512,1024]{2,1,0:T(8,128)} %bitcast.304), kind=kLoop, calls=%fused_computation | loop fusion | flops 12558336 | bytes 50429952 | tf_op jit(solution)/shard_map/while/body/eval_jaxpr/transpose(jvp())/reduce_sum | solution.py:50
  796.9 40.6 %psum.75 = f32[32,12]{0,1:T(8,128)} all-reduce(f32[32,12]{0,1:T(8,128)S(1)} %fusion.81), channel_id=1, replica_groups=mesh['dp'=4,'row'=4,'col'=2] {'dp','row','col'}, use_global_device_ids=true, to_apply=%region_28.29 | all-reduce | flops 384 | bytes 3072 | tf_op jit(solution)/shard_map/psum | solution.py:345
  837.6 4.7 fusion.64
  846.8 25.9 %all-reduce.15.cloned.1.call-done = (bf16[192,384]{1,0:T(8,128)(2,1)}, bf16[192,384]{1,0:T(8,128)(2,1)}, bf16[192,384]{1,0:T(8,128)(2,1)}, bf16[192,384]{1,0:T(8...) async-done(((bf16[192,384]{1,0:T(8,128)(2,1)}, bf16[192,384]{1,0:T(8,128)(2,1)}, bf16[192,384]{1,0:T(8,128)(2,1)}, ...) | async-done | bytes 1769488 | tf_op jit(solution)/shard_map/psum | solution.py:334
  (358 shorter events, 211.4 us)
Async XLA Ops:
  7.2 24.1 %copy-start = (f32[32,12]{0,1:T(8,128)S(1)}, f32[32,12]{0,1:T(8,128)}, u32[]{:S(2)}) copy-start(f32[32,12]{0,1:T(8,128)} %param.22) | copy-start | bytes 4612
  7.2 23.7 %copy-start.6 = (bf16[2,512,768]{2,1,0:T(8,128)(2,1)S(1)}, bf16[2,512,768]{2,1,0:T(8,128)(2,1)}, u32[]{:S(2)}) copy-start(bf16[2,512,768]{2,1,0:T(8,128)(2,1)} %param.14) | copy-start | bytes 4718596
  7.2 24.1 %copy-start.87 = (s32[1023]{0:T(1024)S(1)}, s32[1023]{0:T(1024)}, u32[]{:S(2)}) copy-start(s32[1023]{0:T(1024)} %param.16) | copy-start | bytes 12280
  7.2 189.8 %all-gather.17.cloned.1.call-start = ((), (), s32[]{:S(2)}) async-start(), calls=%async_computation.14 | async-start | bytes 1327104 | tf_op jit(solution)/shard_map/all_gather | solution.py:216
  8.0 191.8 %all-gather.19.cloned.1.call-start = ((), (), s32[]{:S(2)}) async-start(), calls=%async_computation.15 | async-start | bytes 1327104 | tf_op jit(solution)/shard_map/all_gather | solution.py:214
  8.7 200.2 %all-gather.21.cloned.1.call-start = ((), (), s32[]{:S(2)}) async-start(), calls=%async_computation.16 | async-start | bytes 1327104 | tf_op jit(solution)/shard_map/all_gather | solution.py:215
  9.4 221.6 %all-gather.23.cloned.1.call-start = ((), (), s32[]{:S(2)}) async-start(), calls=%async_computation.17 | async-start | bytes 1327104 | tf_op jit(solution)/shard_map/all_gather | solution.py:217
  10.0 251.1 %all-gather.25.cloned.1.call-start = ((), (), s32[]{:S(2)}) async-start(), calls=%async_computation.18 | async-start | bytes 3538944 | tf_op jit(solution)/shard_map/all_gather | solution.py:219
  10.6 258.6 %all-gather.27.cloned.1.call-start = ((), (), s32[]{:S(2)}) async-start(), calls=%async_computation.19 | async-start | bytes 3538944 | tf_op jit(solution)/shard_map/all_gather | solution.py:220
  11.2 272.9 %all-gather.29.cloned.1.call-start = ((), (), s32[]{:S(2)}) async-start(), calls=%async_computation.20 | async-start | bytes 3538944 | tf_op jit(solution)/shard_map/all_gather | solution.py:221
  11.9 772.0 %reduce-scatter.8.cloned.1.call-start = ((), (), s32[]{:S(2)}) async-start(), calls=%async_computation.7 | async-start | bytes 2654208 | tf_op jit(solution)/shard_map/reduce_scatter | solution.py:323
  31.3 12.1 %copy-start.82 = (f32[512]{0:T(512)}, f32[512]{0:T(512)S(1)}, u32[]{:S(2)}) copy-start(f32[512]{0:T(512)S(1)} %get-tuple-element.119) | copy-start | bytes 6148
  31.3 164.8 %copy-start.80 = (f32[512]{0:T(512)}, f32[512]{0:T(512)S(1)}, u32[]{:S(2)}) copy-start(f32[512]{0:T(512)S(1)} %get-tuple-element.118) | copy-start | bytes 6148
  182.4 12.8 %copy-start.86 = (s32[2,512]{1,0:T(2,128)S(1)}, s32[2,512]{1,0:T(2,128)}, u32[]{:S(2)}) copy-start(s32[2,512]{1,0:T(2,128)} %param.15) | copy-start | bytes 12292
  199.7 6.6 copy-start.40
  215.4 8.4 copy-start.18
  217.1 6.7 copy-start.11
  231.0 14.6 %copy-start.13 = (bf16[512,768]{0,1:T(8,128)(2,1)}, bf16[512,768]{0,1:T(8,128)(2,1)S(1)}, u32[]{:S(2)}) copy-start(bf16[512,768]{0,1:T(8,128)(2,1)S(1)} %copy.104) | copy-start | bytes 2359300
  236.6 7.0 copy-start.15
  236.6 7.0 copy-start.69
  261.0 19.3 %copy-start.23 = (bf16[512,768]{1,0:T(8,128)(2,1)}, bf16[512,768]{1,0:T(8,128)(2,1)S(1)}, u32[]{:S(2)}) copy-start(bf16[512,768]{1,0:T(8,128)(2,1)S(1)} %multiply_convert_fusion.7) | copy-start | bytes 2359300
  290.0 20.4 %copy-start.45 = (bf16[256,8,2,384]{3,1,2,0:T(8,128)(2,1)}, bf16[256,8,2,384]{3,1,2,0:T(8,128)(2,1)S(1)}, u32[]{:S(2)}) copy-start(bf16[256,8,2,384]{3,1,2,0:T(8,128)(2,1)S(1)} %copy.141) | copy-start | bytes 9437188
  293.2 6.5 copy-start.47
  323.5 116.6 %copy-start.7 = (f32[512,768]{1,0:T(8,128)}, f32[512,768]{1,0:T(8,128)S(1)}, u32[]{:S(2)}) copy-start(f32[512,768]{1,0:T(8,128)S(1)} %get-tuple-element.166) | copy-start | bytes 4718596
  327.6 12.3 %slice-start.3 = ((s8[12582912]{0:T(1024)(128)(4,1)}), s8[4194304]{0:T(1024)(128)(4,1)S(1)}, s32[]{:S(2)}) async-start(s8[12582912]{0:T(1024)(128)(4,1)} %bitcast.297), calls=%async_computation.25 | async-start | bytes 8388608
  327.6 12.3 %slice-start.4 = ((s8[12582912]{0:T(1024)(128)(4,1)}), s8[4194304]{0:T(1024)(128)(4,1)S(1)}, s32[]{:S(2)}) async-start(s8[12582912]{0:T(1024)(128)(4,1)} %bitcast.297), calls=%async_computation.26 | async-start | bytes 8388608
  327.6 12.3 %slice-start.5 = ((s8[12582912]{0:T(1024)(128)(4,1)}), s8[4194304]{0:T(1024)(128)(4,1)S(1)}, s32[]{:S(2)}) async-start(s8[12582912]{0:T(1024)(128)(4,1)} %bitcast.297), calls=%async_computation.27 | async-start | bytes 8388608
  339.9 7.5 copy-start.14
  355.2 12.3 %slice-start = ((s8[12582912]{0:T(1024)(128)(4,1)}), s8[4194304]{0:T(1024)(128)(4,1)S(1)}, s32[]{:S(2)}) async-start(s8[12582912]{0:T(1024)(128)(4,1)} %bitcast.295), calls=%async_computation.22 | async-start | bytes 8388608
  355.2 12.3 %slice-start.1 = ((s8[12582912]{0:T(1024)(128)(4,1)}), s8[4194304]{0:T(1024)(128)(4,1)S(1)}, s32[]{:S(2)}) async-start(s8[12582912]{0:T(1024)(128)(4,1)} %bitcast.295), calls=%async_computation.23 | async-start | bytes 8388608
  355.2 12.3 %slice-start.2 = ((s8[12582912]{0:T(1024)(128)(4,1)}), s8[4194304]{0:T(1024)(128)(4,1)S(1)}, s32[]{:S(2)}) async-start(s8[12582912]{0:T(1024)(128)(4,1)} %bitcast.295), calls=%async_computation.24 | async-start | bytes 8388608
  367.5 7.0 copy-start.12
  388.5 397.1 %reduce-scatter.10.cloned.1.call-start = ((), (), s32[]{:S(2)}) async-start(), calls=%async_computation.8 | async-start | bytes 2654208 | tf_op jit(solution)/shard_map/reduce_scatter | solution.py:324
  411.3 375.9 %reduce-scatter.12.cloned.1.call-start = ((), (), s32[]{:S(2)}) async-start(), calls=%async_computation.9 | async-start | bytes 2654208 | tf_op jit(solution)/shard_map/reduce_scatter | solution.py:325
  437.4 351.5 %reduce-scatter.14.cloned.1.call-start = ((), (), s32[]{:S(2)}) async-start(), calls=%async_computation.10 | async-start | bytes 2654208 | tf_op jit(solution)/shard_map/reduce_scatter | solution.py:326
  449.8 340.8 %reduce-scatter.16.cloned.1.call-start = ((), (), s32[]{:S(2)}) async-start(), calls=%async_computation.11 | async-start | bytes 7077888 | tf_op jit(solution)/shard_map/reduce_scatter | solution.py:328
  475.7 316.8 %reduce-scatter.18.cloned.1.call-start = ((), (), s32[]{:S(2)}) async-start(), calls=%async_computation.12 | async-start | bytes 7077888 | tf_op jit(solution)/shard_map/reduce_scatter | solution.py:329
  555.7 238.8 %reduce-scatter.20.cloned.1.call-start = ((), (), s32[]{:S(2)}) async-start(), calls=%async_computation.13 | async-start | bytes 7077888 | tf_op jit(solution)/shard_map/reduce_scatter | solution.py:330
  574.4 9.0 %copy-start.30 = (bf16[2,512,768]{2,1,0:T(8,128)(2,1)S(1)}, bf16[2,512,768]{2,1,0:T(8,128)(2,1)}, u32[]{:S(2)}) copy-start(bf16[2,512,768]{2,1,0:T(8,128)(2,1)} %param.27) | copy-start | bytes 4718596
  652.9 18.9 %copy-start.26 = (bf16[12,64,512]{2,1,0:T(8,128)(2,1)S(1)}, bf16[12,64,512]{2,1,0:T(8,128)(2,1)}, u32[]{:S(2)}) copy-start(bf16[12,64,512]{2,1,0:T(8,128)(2,1)} %convolution_convert_fusion.9) | copy-start | bytes 2359300
  652.9 219.8 %all-reduce.15.cloned.1.call-start = ((), (), s32[]{:S(2)}) async-start(), calls=%async_computation.21 | async-start | bytes 3538944 | tf_op jit(solution)/shard_map/psum | solution.py:334
  653.0 18.9 %copy-start.66 = (bf16[96,8,2,384]{3,1,2,0:T(8,128)(2,1)S(1)}, bf16[96,8,2,384]{3,1,2,0:T(8,128)(2,1)}, u32[]{:S(2)}) copy-start(bf16[96,8,2,384]{3,1,2,0:T(8,128)(2,1)} %copy-done.65) | copy-start | bytes 3538948
  736.6 32.7 %copy-start.39 = (bf16[512,2048]{1,0:T(8,128)(2,1)S(1)}, bf16[512,2048]{1,0:T(8,128)(2,1)}, u32[]{:S(2)}) copy-start(bf16[512,2048]{1,0:T(8,128)(2,1)} %get-tuple-element.162) | copy-start | bytes 6291460
  736.6 32.7 %copy-start.64 = (f32[512,768]{1,0:T(8,128)S(1)}, f32[512,768]{1,0:T(8,128)}, u32[]{:S(2)}) copy-start(f32[512,768]{1,0:T(8,128)} %get-tuple-element.179) | copy-start | bytes 4718596
  792.5 45.0 %copy-start.35 = (f32[512,768]{1,0:T(8,128)S(1)}, f32[512,768]{1,0:T(8,128)}, u32[]{:S(2)}) copy-start(f32[512,768]{1,0:T(8,128)} %get-tuple-element.177) | copy-start | bytes 4718596
  872.7 8.6 copy-start.79
  872.7 9.6 %copy-start.78 = (bf16[512,384]{1,0:T(8,128)(2,1)S(1)}, bf16[512,384]{1,0:T(8,128)(2,1)}, u32[]{:S(2)}) copy-start(bf16[512,384]{1,0:T(8,128)(2,1)} %get-tuple-element.144) | copy-start | bytes 1179652
  876.0 7.2 copy-start.1
  (64 other events, 172.2 us)
Sparse Core Ops, SparseCore 0:
  9.9 26.9 all-gather.16
  38.8 23.9 all-gather.18
  64.6 24.0 all-gather.20
  90.5 24.0 all-gather.22
  116.3 32.3 all-gather.24
  150.4 32.3 all-gather.26
  184.6 32.3 all-gather.28
  388.6 42.8 reduce-scatter.7
  435.3 42.4 reduce-scatter.9
  481.0 42.4 reduce-scatter.11
  527.2 42.4 reduce-scatter.13
  573.0 61.7 reduce-scatter.15
  638.5 62.1 reduce-scatter.17
  704.0 61.7 reduce-scatter.19
  796.6 76.0 all-reduce.14
where the time goes:
time: 896 us; the launch traced here: 890 us
  local copies, waits for them, and re-layouts  483 us (54%)
  matrix products  181 us (20%)
  other arithmetic  97.4 us (11%)
  blocking collectives  81.5 us (9%)
  waiting for transfers between devices  30.4 us (3%)
  between operations  16.1 us (2%)
    unnamed x213, local copies, waits for them, and re-layouts  176 us
    reshape x3, local copies, waits for them, and re-layouts, bias_block(): skewed = tiled.reshape(head_count, block_rows, twice_len - 1)  122 us
    reshape x7, local copies, waits for them, and re-layouts, close_block(): full.reshape(row_count, span_rows, column_count, span_cols)  42.6 us
    psum x1, blocking collectives, shards(): table_grad = lax.psum(table_local, ('dp', 'row', 'col'))  40.6 us
    dot_general x14, matrix products, left_product(): lax.dot_general(left, right, (((0,), (0,)), ((), ())), preferred_element_...  40 us
    reshape x2, other arithmetic, bias_block(): tiled = jnp.tile(offsets, (1, block_rows))[:, :block_rows * (twice_len - 1)]  37.4 us
    dot_general x14, matrix products, product(): return jnp.dot(left, right, preferred_element_type=jnp.float32)  34 us
    transpose x7, local copies, waits for them, and re-layouts, close_block(): full.reshape(row_count, span_rows, column_count, span_cols)  33.9 us
  transfers between devices with their start and end apart: 15, of which 1 were waited for; matrix products, arithmetic and copies ran while one was open for 71% of the time, Pallas kernels for 0%

commit v1 on v0

v1 whole, which is shorter than its diff:
```python
import functools
import types

import jax
import jax.numpy as jnp
from jax import lax
from jax.experimental import pallas as pl
from jax.experimental.pallas import tpu as pltpu
from jax.sharding import PartitionSpec as P

F32 = jnp.float32
BF = jnp.bfloat16
EPSILON = 1e-06
NEGATIVE = -1e30
PRECISE = lax.Precision.HIGHEST


def nn(left, right):
    return lax.dot_general(left, right, (((1,), (0,)), ((), ())), preferred_element_type=F32)


def nt(left, right):
    return lax.dot_general(left, right, (((1,), (1,)), ((), ())), preferred_element_type=F32)


def rows_of(index, size):
    return pl.ds(pl.multiple_of(index * size, size), size)


def loop(count, body):
    lax.fori_loop(0, count, lambda index, carry: (body(index), carry)[1], 0)


def norm_in(s, rb):
    def body(i):
        r = rows_of(i, rb)
        x = s.x[r, :].astype(F32)
        scale = lax.rsqrt(jnp.mean(x * x, axis=-1, keepdims=True) + EPSILON)
        n = (x * scale * s.gain[0:1, :]).astype(BF)
        s.a[r, :] = n
        s.n1t[:, r] = n.T

    loop(s.tokens // rb, body)


def masks(s):
    for m in range(s.micro):
        row = s.seg[m : m + 1, :].astype(F32)
        column = jnp.broadcast_to(row, (128, s.length)).T
        for i in range(s.length // 128):
            same = column == row[:, 128 * i : 128 * (i + 1)]
            s.mask[m, :, 128 * i : 128 * (i + 1)] = jnp.where(same, 0.0, NEGATIVE)


def offset_rows(s):
    classes = lax.broadcasted_iota(jnp.int32, (s.buckets, 2 * s.length), 0)
    onehot = (s.bucket[0:1, :] == classes).astype(F32)
    s.offs[...] = lax.dot_general(
        s.table_t[...], onehot, (((1,), (0,)), ((), ())), precision=PRECISE, preferred_element_type=F32
    )


def project(s, which, rb):
    weight, out, out_t = ((s.wq, s.q, None), (s.wk, s.k, s.kt), (s.wv, s.v, s.vt))[which]

    def body(i):
        r = rows_of(i, rb)
        p = nn(s.a[r, :], weight[...]).astype(BF)
        out[r, :] = p
        if out_t is not None:
            out_t[:, r] = p.T

    loop(s.tokens // rb, body)


def half_masks(dtype):
    lane = lax.broadcasted_iota(jnp.int32, (1, 128), 1)
    return [(lane < 64).astype(dtype), (lane >= 64).astype(dtype)]


def attend_pair(s, pair):
    length, wide = s.length, s.wide
    blocks = length // 128
    cols = rows_of(pair, 128)
    keep = half_masks(BF)
    for sub in range(2):
        head = 2 * pair + sub
        row = jnp.broadcast_to(s.offs[pl.ds(head, 1), :], (128, 2 * length))
        s.toep[...] = pltpu.roll(row, 2 * length - 127, 1, stride=1, stride_axis=0)
        hr = rows_of(head, 64)
        for m in range(s.micro):
            mr = slice(m * length, (m + 1) * length)
            key = s.k[mr, cols] * keep[sub]
            vt = s.vt[hr, mr]
            for b in range(length // wide):
                ir = slice(m * length + b * wide, m * length + (b + 1) * wide)
                il = slice(b * wide, (b + 1) * wide)
                scores = nt(key, s.q[ir, cols])
                bias = jnp.concatenate(
                    [s.toep[:, 128 * (blocks - 1 - j) + b * wide : 128 * (blocks - 1 - j) + (b + 1) * wide] for j in range(blocks)],
                    axis=0,
                )
                scores = scores + bias + s.mask[m, :, il]
                top = jnp.max(scores, axis=0, keepdims=True)
                e = jnp.exp(scores - top)
                low = (e * (1.0 / jnp.sum(e, axis=0, keepdims=True))).astype(BF)
                s.p[head * s.micro + m, :, il] = low
                s.ot[hr, ir] = nn(vt, low).astype(BF)


def turn(s, source, target, cb):
    def body(i):
        r = rows_of(i, cb)
        target[r, :] = source[:, r].T

    loop(s.tokens // cb, body)


def turn_back(s, source, target, cb):
    def body(i):
        r = rows_of(i, cb)
        target[:, r] = source[r, :].T

    loop(s.tokens // cb, body)


def out_project(s, rb):
    def body(i):
        r = rows_of(i, rb)
        att = s.ot[:, r].T
        mid = s.x[r, :].astype(F32) + nn(att, s.wo[...])
        s.mid[r, :] = mid
        s.y[r, :] = mid
        scale = lax.rsqrt(jnp.mean(mid * mid, axis=-1, keepdims=True) + EPSILON)
        n = (mid * scale * s.gain[1:2, :]).astype(BF)
        s.a[r, :] = n
        s.n2t[:, r] = n.T
        s.dn[r, :] = jnp.zeros_like(mid)
        s.ct[:, r] = s.c[r, :].T

    loop(s.tokens // rb, body)


C0 = 0.7978845608028654
C1 = 0.044715


def ffn_tile(s, tile, ft, rb, gb):
    cols = rows_of(tile, ft)

    def forward(i):
        r = rows_of(i, rb)
        n = s.a[r, :]
        cot = s.c[r, :]
        gate = nn(n, s.wg[:, cols])
        up = nn(n, s.wu[:, cols])
        dh = nt(cot, s.wd[cols, :])
        square = gate * gate
        t = jnp.tanh(gate * (C0 + (C0 * C1) * square))
        half = 0.5 + 0.5 * t
        act = gate * half
        slope = half + (0.5 * gate) * (1.0 - t * t) * (C0 + (3.0 * C0 * C1) * square)
        hid = (act * up).astype(BF)
        dg = (dh * up * slope).astype(BF)
        du = (dh * act).astype(BF)
        s.hid[r, :] = hid
        s.dg[r, :] = dg
        s.du[r, :] = du
        s.y[r, :] += nn(hid, s.wd[cols, :])
        s.dn[r, :] += nt(dg, s.wg[:, cols]) + nt(du, s.wu[:, cols])

    loop(s.tokens // rb, forward)

    def grads(i):
        r = rows_of(i, gb)
        s.wd[cols, r] = nn(s.ct[r, :], s.hid[...]).astype(BF).T
        s.wg[r, cols] = nn(s.n2t[r, :], s.dg[...]).astype(BF)
        s.wu[r, cols] = nn(s.n2t[r, :], s.du[...]).astype(BF)

    loop(s.width // gb, grads)


def ffn_close(s, rb):
    s.gsum[...] = jnp.zeros_like(s.gsum)

    def body(i):
        r = rows_of(i, rb)
        mid = s.mid[r, :]
        dn = s.dn[r, :]
        scale = lax.rsqrt(jnp.mean(mid * mid, axis=-1, keepdims=True) + EPSILON)
        gdn = dn * s.gain[1:2, :]
        dot = jnp.mean(gdn * mid, axis=-1, keepdims=True)
        dmid = s.c[r, :].astype(F32) + scale * gdn - mid * (scale * scale * scale * dot)
        s.gsum[1:2, :] += jnp.sum(dn * mid * scale, axis=0, keepdims=True)
        s.dn[r, :] = dmid
        s.a[r, :] = dmid.astype(BF)
        s.c[r, :] = s.y[r, :].astype(BF)

    loop(s.tokens // rb, body)


def out_backward(s, rb, gb):
    def body(i):
        r = rows_of(i, rb)
        d = nt(s.a[r, :], s.wo[...]).astype(BF)
        s.do[r, :] = d
        s.dot[:, r] = d.T

    loop(s.tokens // rb, body)

    def grads(i):
        r = rows_of(i, gb)
        s.wo[r, :] = nn(s.ot[r, :], s.a[...]).astype(BF)

    loop(s.width // gb, grads)


def attend_back(s, pair):
    length, wide = s.length, s.wide
    blocks = length // 128
    cols = rows_of(pair, 128)
    keep = half_masks(BF)
    lane = lax.broadcasted_iota(jnp.int32, (1, 128), 1) < 64
    parts = {}
    for sub in range(2):
        head = 2 * pair + sub
        hr = rows_of(head, 64)
        s.toep[...] = jnp.zeros_like(s.toep)
        for m in range(s.micro):
            mr = slice(m * length, (m + 1) * length)
            value = s.v[mr, cols] * keep[sub]
            kt = s.kt[hr, mr]
            for b in range(length // wide):
                ir = slice(m * length + b * wide, m * length + (b + 1) * wide)
                il = slice(b * wide, (b + 1) * wide)
                dp = nt(value, s.do[ir, cols])
                inner = jnp.sum(s.dot[hr, ir].astype(F32) * s.ot[hr, ir].astype(F32), axis=0, keepdims=True)
                ds = s.p[head * s.micro + m, :, il].astype(F32) * (dp - inner)
                for j in range(blocks):
                    at = 128 * (blocks - 1 - j) + b * wide
                    s.toep[:, at : at + wide] += ds[128 * j : 128 * (j + 1), :]
                low = ds.astype(BF)
                s.ds[:, il] = low
                s.dqt[hr, ir] = nn(kt, low).astype(BF)
            parts[sub, m, 0] = nn(s.ds[...], s.q[mr, cols])
            parts[sub, m, 1] = nn(s.p[head * s.micro + m, :, :], s.do[mr, cols])
            if sub == 1:
                s.k[mr, cols] = jnp.where(lane, parts[0, m, 0], parts[1, m, 0]).astype(BF)
                s.v[mr, cols] = jnp.where(lane, parts[0, m, 1], parts[1, m, 1]).astype(BF)
        fold = s.toep[...]
        rows = 64
        while rows >= 8:
            fold = fold[:rows, :] + pltpu.roll(fold[rows:, :], 2 * length - rows, 1)
            rows //= 2
        for r in range(8):
            s.goff[r, pl.ds(head, 1), :] = fold[r : r + 1, :]


def table_grad(s):
    total = None
    for r in range(8):
        part = pltpu.roll(s.goff[r, :, :], 127 - r, 1)
        total = part if total is None else total + part
    classes = lax.broadcasted_iota(jnp.int32, (s.buckets, 2 * s.length), 0)
    onehot = (s.bucket[0:1, :] == classes).astype(F32)
    return lax.dot_general(
        total, onehot, (((1,), (1,)), ((), ())), precision=PRECISE, preferred_element_type=F32
    )


def qkv_back_input(s, rb):
    def body(i):
        r = rows_of(i, rb)
        dn = nt(s.q[r, :], s.wq[...]) + nt(s.k[r, :], s.wk[...]) + nt(s.v[r, :], s.wv[...])
        x = s.x[r, :].astype(F32)
        scale = lax.rsqrt(jnp.mean(x * x, axis=-1, keepdims=True) + EPSILON)
        gdn = dn * s.gain[0:1, :]
        dot = jnp.mean(gdn * x, axis=-1, keepdims=True)
        s.gsum[0:1, :] += jnp.sum(dn * x * scale, axis=0, keepdims=True)
        s.x[r, :] = (s.dn[r, :] + scale * gdn - x * (scale * scale * scale * dot)).astype(BF)

    loop(s.tokens // rb, body)


def weight_back(s, which, grad, gb):
    weight = (s.wq, s.wk, s.wv)[which]

    def body(i):
        r = rows_of(i, gb)
        weight[r, :] = nn(s.n1t[r, :], grad[...]).astype(BF)

    loop(s.width // gb, body)


MESH = pl.DeviceIdType.MESH
NAMES = ("wq", "wk", "wv", "wo", "wg", "wu", "wd")


def place(s):
    s.z, s.row, s.col = lax.axis_index("dp"), lax.axis_index("row"), lax.axis_index("col")
    s.core, s.xx = lax.rem(s.row, 2), lax.div(s.row, 2)
    s.row_p = 2 * s.xx + 1 - s.core
    s.row_x = 2 * (1 - s.xx) + s.core
    s.row_px = 2 * (1 - s.xx) + 1 - s.core
    s.col_y = 1 - s.col
    s.to_p = (s.z, s.row_p, s.col)
    s.to_x = (s.z, s.row_x, s.col)
    s.to_y = (s.z, s.row, s.col_y)
    s.me = 2 * s.row + s.col
    s.plane = [(s.z, lax.rem(s.row + (i // 2), 4), lax.rem(s.col + i % 2, 2)) for i in range(1, 8)]
    s.stack = [(lax.rem(s.z + i, 4), s.row, s.col) for i in range(1, 4)]


def greet(s):
    barrier = pltpu.get_barrier_semaphore()
    for peer in s.plane + s.stack:
        pl.semaphore_signal(barrier, inc=1, device_id=peer, device_id_type=MESH)
    pl.semaphore_wait(barrier, 10)


def block(s, w, row, col, half=None):
    full = getattr(s, NAMES[w])
    rb, cb = full.shape[0] // 4, full.shape[1] // 2
    size = rb if half is None else rb // 2
    start = row * rb + (0 if half is None else half * (rb // 2))
    return full.at[pl.ds(pl.multiple_of(start, size), size), pl.ds(pl.multiple_of(col * cb, cb), cb)]


def strip(s, w, row, half=None):
    full = getattr(s, NAMES[w])
    rb = full.shape[0] // 4
    size = rb if half is None else rb // 2
    start = row * rb + (0 if half is None else half * (rb // 2))
    return full.at[pl.ds(pl.multiple_of(start, size), size), :]


def send(s, family, w, kind, src, dst, peer):
    return pltpu.make_async_remote_copy(
        src_ref=src, dst_ref=dst, send_sem=getattr(s, family + "_send").at[w, kind],
        recv_sem=getattr(s, family + "_recv").at[w, kind], device_id=peer, device_id_type=MESH)


def ag_copy(s, w, kind):
    piece = getattr(s, NAMES[w] + "_in")
    b = lambda r, c, h=None: block(s, w, r, c, h)
    own = b(s.row, s.col)
    if kind == 0:
        return send(s, "ag", w, 0, piece, own, s.to_x)
    if kind == 1:
        return send(s, "ag", w, 1, piece, own, s.to_y)
    if kind == 2:
        return send(s, "ag", w, 2, piece, own, s.to_p)
    if kind == 3:
        return send(s, "ag", w, 3, b(s.row_x, s.col), b(s.row_x, s.col), s.to_p)
    if kind == 4:
        return send(s, "ag", w, 4, b(s.row, s.col_y), b(s.row, s.col_y), s.to_p)
    if kind == 5:
        return send(s, "ag", w, 5, b(s.row_x, s.col, 0), b(s.row_x, s.col, 0), s.to_y)
    if kind == 6:
        return send(s, "ag", w, 6, b(s.row, s.col_y, 1), b(s.row, s.col_y, 1), s.to_x)
    return send(s, "ag", w, kind, b(s.row_x, s.col_y, kind - 7), b(s.row_x, s.col_y, kind - 7), s.to_p)


def ag_arrive(s, w, kind):
    b = lambda r, c, h=None: block(s, w, r, c, h)
    where = [
        lambda: b(s.row_x, s.col), lambda: b(s.row, s.col_y), lambda: b(s.row_p, s.col), lambda: b(s.row_px, s.col),
        lambda: b(s.row_p, s.col_y), lambda: b(s.row_x, s.col_y, 0), lambda: b(s.row_x, s.col_y, 1),
        lambda: b(s.row_px, s.col_y, 0), lambda: b(s.row_px, s.col_y, 1)][kind]()
    send(s, "ag", w, kind, where, where, s.to_p).wait_recv()


def ag_open(s, w):
    for kind in range(3):
        ag_copy(s, w, kind).start()
    pltpu.make_async_copy(getattr(s, NAMES[w] + "_in"), block(s, w, s.row, s.col), s.ag_own.at[w]).start()


def ag_relay(s, w):
    ag_arrive(s, w, 0)
    ag_copy(s, w, 5).start()
    ag_copy(s, w, 3).start()
    ag_arrive(s, w, 1)
    ag_copy(s, w, 6).start()
    ag_copy(s, w, 4).start()


def ag_corner(s, w):
    for kind in (5, 6):
        ag_arrive(s, w, kind)
        ag_copy(s, w, kind + 2).start()


def ag_close(s, w):
    for kind in (2, 3, 4, 7, 8):
        ag_arrive(s, w, kind)
    pltpu.make_async_copy(getattr(s, NAMES[w] + "_in"), block(s, w, s.row, s.col), s.ag_own.at[w]).wait()


def ag_sent(s, w):
    for kind in range(9):
        ag_copy(s, w, kind).wait_send()


def gain_copies(s):
    return [
        pltpu.make_async_remote_copy(
            src_ref=s.gain_in, dst_ref=s.gain_slots.at[s.me], send_sem=s.gain_send.at[i], recv_sem=s.gain_recv.at[s.me],
            device_id=peer, device_id_type=MESH)
        for i, peer in enumerate(s.plane)]


def gain_open(s):
    for copy in gain_copies(s):
        copy.start()


def gain_close(s):
    total = s.gain_in[...]
    for i in range(1, 8):
        slot = 2 * lax.rem(s.row + (i // 2), 4) + lax.rem(s.col + i % 2, 2)
        pltpu.make_async_remote_copy(
            src_ref=s.gain_in, dst_ref=s.gain_slots.at[slot], send_sem=s.gain_send.at[i - 1], recv_sem=s.gain_recv.at[slot],
            device_id=s.plane[i - 1], device_id_type=MESH).wait_recv()
        total = total + s.gain_slots[slot]
    s.gain[...] = total
    for copy in gain_copies(s):
        copy.wait_send()


def small_open(s, family, slots, peers, me):
    slots[me] = s.small[...]
    for i, peer in enumerate(peers):
        pltpu.make_async_remote_copy(
            src_ref=s.small, dst_ref=slots.at[me], send_sem=getattr(s, family + "_send").at[i],
            recv_sem=getattr(s, family + "_recv").at[me], device_id=peer, device_id_type=MESH).start()


def small_close(s, family, slots, peers, ids, me):
    for i, (peer, slot) in enumerate(zip(peers, ids)):
        copy = pltpu.make_async_remote_copy(
            src_ref=s.small, dst_ref=slots.at[slot], send_sem=getattr(s, family + "_send").at[i],
            recv_sem=getattr(s, family + "_recv").at[slot], device_id=peer, device_id_type=MESH)
        copy.wait_recv()
        copy.wait_send()
    total = slots[0]
    for i in range(1, len(ids) + 1):
        total = total + slots[i]
    s.small[...] = total


def plane_ids(s):
    return [2 * lax.rem(s.row + (i // 2), 4) + lax.rem(s.col + i % 2, 2) for i in range(1, 8)]


def stack_ids(s):
    return [lax.rem(s.z + i, 4) for i in range(1, 4)]


def rs_buf(s, name, w):
    return getattr(s, f"{name}{w}")


def rs_copy(s, w, kind):
    n = lambda name: rs_buf(s, name, w)
    if kind in (0, 1):
        return send(s, "rs", w, kind, strip(s, w, 2 * kind + 1 - s.core), n("pr").at[kind], s.to_p)
    if kind == 2:
        return send(s, "rs", w, 2, strip(s, w, s.row_x, 0), n("xa"), s.to_x)
    if kind in (3, 4):
        return send(s, "rs", w, kind, block(s, w, 2 * (kind - 3) + s.core, s.col_y, 1), n("yb").at[kind - 3], s.to_y)
    if kind == 5:
        return send(s, "rs", w, 5, block(s, w, s.row, s.col_y, 0), n("ya"), s.to_y)
    if kind == 6:
        return send(s, "rs", w, 6, block(s, w, s.row_x, s.col, 1), n("xb"), s.to_x)
    low = s.z - 1
    if kind == 7:
        return send(s, "rs", w, 7, block(s, w, s.row, s.col), n("zi"), (s.z_in, s.row, s.col))
    if kind == 8:
        return send(s, "rs", w, 8, block(s, w, s.row, s.col, 1 - low), n("zx"), (3 - s.z, s.row, s.col))
    if kind == 9:
        return send(s, "rs", w, 9, block(s, w, s.row, s.col, low), block(s, w, s.row_p, s.col, low), (3 - s.z, s.row, s.col))
    if kind == 10:
        return send(s, "rs", w, 10, block(s, w, s.row, s.col, low), block(s, w, s.row_p, s.col, low), (s.z_out, s.row, s.col))
    return send(s, "rs", w, 11, block(s, w, s.row_p, s.col, 1 - low), block(s, w, s.row_p, s.col, 1 - low), (s.z_out, s.row, s.col))


def rs_arrive(s, w, kind):
    n = lambda name: rs_buf(s, name, w)
    low = s.z - 1
    where = [
        lambda: n("pr").at[0], lambda: n("pr").at[1], lambda: n("xa"), lambda: n("yb").at[0], lambda: n("yb").at[1],
        lambda: n("ya"), lambda: n("xb"), lambda: n("zi"), lambda: n("zx"),
        lambda: block(s, w, s.row_p, s.col, 1 - low),
        lambda: block(s, w, s.row_p, s.col, s.z_in - 1),
        lambda: block(s, w, s.row_p, s.col, 2 - s.z_in)][kind]()
    send(s, "rs", w, kind, where, where, s.to_p).wait_recv()


def add_into(target, source, step):
    rows = target.shape[0]
    step = min(step, rows)

    def body(i):
        r = rows_of(i, step)
        target[r, :] = (target[r, :].astype(F32) + source[r, :].astype(F32)).astype(BF)

    loop(rows // step, body)


def rs_1(s, w):
    rs_copy(s, w, 0).start()
    rs_copy(s, w, 1).start()


def rs_2(s, w):
    for i in range(2):
        rs_arrive(s, w, i)
        add_into(strip(s, w, 2 * i + s.core), rs_buf(s, "pr", w).at[i], 32)
    rs_copy(s, w, 2).start()
    rs_copy(s, w, 3).start()
    rs_copy(s, w, 4).start()


def rs_3(s, w):
    rs_arrive(s, w, 2)
    add_into(strip(s, w, s.row, 0), rs_buf(s, "xa", w), 32)
    rs_copy(s, w, 5).start()
    for i in range(2):
        rs_arrive(s, w, 3 + i)
        add_into(block(s, w, 2 * i + s.core, s.col, 1), rs_buf(s, "yb", w).at[i], 32)
    rs_copy(s, w, 6).start()


def rs_4(s, w):
    rs_arrive(s, w, 5)
    add_into(block(s, w, s.row, s.col, 0), rs_buf(s, "ya", w), 32)
    rs_arrive(s, w, 6)
    add_into(block(s, w, s.row, s.col, 1), rs_buf(s, "xb", w), 32)
    for kind in range(7):
        rs_copy(s, w, kind).wait_send()

    @pl.when(s.outer)
    def _():
        rs_copy(s, w, 7).start()


def rs_5(s, w):
    @pl.when(s.inner)
    def _():
        rs_arrive(s, w, 7)
        add_into(block(s, w, s.row, s.col), rs_buf(s, "zi", w), 32)
        rs_copy(s, w, 8).start()


def rs_6(s, w):
    @pl.when(s.inner)
    def _():
        rs_arrive(s, w, 8)
        mine = block(s, w, s.row, s.col, s.z - 1)
        add_into(mine, rs_buf(s, "zx", w), 32)
        rs_copy(s, w, 9).start()
        rs_copy(s, w, 10).start()
        done = block(s, w, s.row_p, s.col, s.z - 1)
        done[...] = mine[...]


def rs_7(s, w):
    @pl.when(s.inner)
    def _():
        rs_arrive(s, w, 9)
        rs_copy(s, w, 11).start()
        for kind in (8, 9, 10):
            rs_copy(s, w, kind).wait_send()

    @pl.when(s.outer)
    def _():
        rs_arrive(s, w, 10)
        rs_copy(s, w, 7).wait_send()


def rs_8(s, w):
    @pl.when(s.inner)
    def _():
        rs_copy(s, w, 11).wait_send()

    @pl.when(s.outer)
    def _():
        rs_arrive(s, w, 11)


def rs_out(s, w):
    return pltpu.make_async_copy(block(s, w, s.row_p, s.col), getattr(s, NAMES[w] + "_out"), s.out_sems.at[w])


PIECES = ("w_query", "w_key", "w_value", "w_out", "w_gate", "w_up", "w_down")
Q, K, V, O, G, U, D = range(7)


def at_step(index, steps):
    for number, todo in enumerate(steps):
        if todo:

            @pl.when(index == number)
            def _():
                for act, weight in todo:
                    act(weight)


def layer(cfg, *refs):
    s = types.SimpleNamespace(**cfg)
    for name, ref in zip(cfg["names"], refs):
        setattr(s, name, ref)
    s.gsum = s.small.at[0:2]
    s.dqt = s.vt
    comm = s.comm
    load_x = pltpu.make_async_copy(s.x_in, s.x, s.io_sems.at[0])
    load_c = pltpu.make_async_copy(s.c_in, s.c, s.io_sems.at[1])
    load_x.start()
    load_c.start()
    if comm:
        place(s)
        s.inner = jnp.logical_and(s.z >= 1, s.z <= 2)
        s.outer = jnp.logical_not(s.inner)
        s.z_in, s.z_out = 1 + lax.div(s.z, 2), 3 * lax.div(s.z, 2)
        greet(s)
        gain_open(s)
        for w in (Q, K, V):
            ag_open(s, w)
    else:
        weights = [pltpu.make_async_copy(getattr(s, n + "_in"), getattr(s, n), s.out_sems.at[i]) for i, n in enumerate(NAMES)]
        for copy in weights:
            copy.start()
        s.gain[...] = s.gain_in[...]
    s.small[...] = jnp.zeros_like(s.small)
    offset_rows(s)
    opened = lambda w: comm and ag_open(s, w)
    relay = lambda w: comm and ag_relay(s, w)
    corner = lambda w: comm and ag_corner(s, w)
    close = lambda w: comm and ag_close(s, w)

    def forward(act, n2t, mid, y, ct, mask):
        s.act, s.n2t, s.mid, s.y, s.ct, s.mask = act, n2t, mid, y, ct, mask
        s.hid, s.dg, s.du = (act.at[:, i * s.ft : (i + 1) * s.ft] for i in range(3))
        masks(s)
        load_x.wait()
        load_c.wait()
        if comm:
            gain_close(s)
        else:
            for copy in weights:
                copy.wait()
        norm_in(s, 128)
        for w in (Q, K, V):
            relay(w)
        opened(O)
        for w in (Q, K, V):
            corner(w)
        opened(G)
        for w in (Q, K, V):
            close(w)
            project(s, w, 256)
        plan = [[], [(relay, O), (opened, U)], [(corner, O), (relay, G), (opened, D)], [(corner, G)], [(relay, U)], [(corner, U), (relay, D)]]

        def pair_step(p):
            if comm:
                at_step(p, plan)
            attend_pair(s, p)

        loop(s.heads // 2, pair_step)
        close(O)
        out_project(s, 256)
        corner(D)
        for w in (G, U, D):
            close(w)
        if comm:
            for w in range(7):
                ag_sent(s, w)
        loop(s.hidden // s.ft, lambda t: ffn_tile(s, t, s.ft, 256, 256))
        ffn_close(s, 128)

    tw = (s.tokens, s.width)
    wt = (s.width, s.tokens)
    pl.run_scoped(
        forward, pltpu.VMEM((s.tokens, 3 * s.ft), BF), pltpu.VMEM(wt, BF), pltpu.VMEM(tw, F32), pltpu.VMEM(tw, F32), pltpu.VMEM(wt, BF),
        pltpu.VMEM((s.micro, s.length, s.length), F32))

    put_y = pltpu.make_async_copy(s.c, s.y_out, s.io_sems.at[0])
    put_x = pltpu.make_async_copy(s.x, s.gi_out, s.io_sems.at[1])
    put_y.start()

    def backward(dot, *bufs):
        s.do, s.dot = s.c, dot
        for name, ref in zip(s.rs_names, bufs):
            setattr(s, name, ref)
        step = lambda fn: (lambda w: comm and fn(s, w))
        r1, r2, r3, r4, r5, r6, r7, r8 = map(step, (rs_1, rs_2, rs_3, rs_4, rs_5, rs_6, rs_7, rs_8))
        if comm:
            for peer in (s.to_p, s.to_x, s.to_y) + tuple(s.stack):
                pl.semaphore_signal(s.ready, inc=1, device_id=peer, device_id_type=MESH)
            pl.semaphore_wait(s.ready, 6)
        for w in (D, G, U):
            r1(w)
        put_y.wait()
        out_backward(s, 256, 256)
        r1(O)
        plan = [
            [(r2, D)], [(r2, G), (r3, D)], [(r2, U), (r3, G), (r4, D)], [(r2, O), (r3, U), (r4, G), (r5, D)],
            [(r3, O), (r4, U), (r5, G), (r6, D)], [(r4, O), (r5, U), (r6, G), (r7, D)]]

        def pair_step(p):
            if comm:
                at_step(p, plan)
            attend_back(s, p)

        loop(s.heads // 2, pair_step)
        for act, w in ((r5, O), (r6, U), (r7, G), (r8, D)):
            act(w)
        s.small[2 : 2 + s.heads, 0 : s.buckets] = table_grad(s)
        turn(s, s.dqt, s.q, 256)
        qkv_back_input(s, 256)
        put_x.start()
        if comm:
            small_open(s, "near", s.near_slots, s.plane, s.me)
        for act, w in ((r6, O), (r7, U), (r8, G)):
            act(w)
        for w, grad in ((Q, s.q), (K, s.k), (V, s.v)):
            weight_back(s, w, grad, 256)
            r1(w)
        for act, w in ((r7, O), (r8, U)):
            act(w)
        if comm:
            small_close(s, "near", s.near_slots, s.plane, plane_ids(s), s.me)
            small_open(s, "far", s.far_slots, s.stack, s.z)
        for act in (r2, r3, r4, r5, r6, r7, r8):
            for w in (Q, K, V):
                act(w)
            if act is r3:
                r8(O)
        if comm:
            small_close(s, "far", s.far_slots, s.stack, stack_ids(s), s.z)
            outs = [rs_out(s, w) for w in range(7)]
        else:
            outs = [pltpu.make_async_copy(getattr(s, n), getattr(s, n + "_out"), s.out_sems.at[i]) for i, n in enumerate(NAMES)]
        for copy in outs:
            copy.start()
        for copy in outs:
            copy.wait()

    bufs = [pltpu.VMEM(shape, BF) for shape in s.rs_shapes]
    pl.run_scoped(backward, pltpu.VMEM(wt, BF), *bufs)
    put_x.wait()
    s.small_out[...] = s.small[...]


def call_layer(comm, x, c, weights, gain, seg, bucket, table_t, full):
    tokens, width = x.shape
    micro, length = seg.shape
    heads, buckets = table_t.shape
    hidden = full[G][1]
    ft = 512
    vm, sem = pltpu.VMEM, pltpu.SemaphoreType.DMA
    tw, wt = (tokens, width), (width, tokens)
    scratch = dict(
        x=vm(tw, BF), c=vm(tw, BF), **{n: vm(shape, BF) for n, shape in zip(NAMES, full)},
        a=vm(tw, BF), n1t=vm(wt, BF), q=vm(tw, BF), k=vm(tw, BF), v=vm(tw, BF), kt=vm(wt, BF), vt=vm(wt, BF), ot=vm(wt, BF),
        dn=vm(tw, F32), toep=vm((128, 2 * length), F32), ds=vm((length, length), BF), p=vm((heads * micro, length, length), BF),
        offs=vm((heads, 2 * length), F32), goff=vm((8, heads, 2 * length), F32), gain=vm((8, width), F32), small=vm((16, width), F32),
        io_sems=sem((2,)), out_sems=sem((7,)),
    )
    rs_names, rs_shapes = [], []
    if comm:
        scratch.update(
            gain_slots=vm((8, 8, width), F32), near_slots=vm((8, 16, width), F32), far_slots=vm((4, 16, width), F32),
            ag_send=sem((7, 9)), ag_recv=sem((7, 9)), ag_own=sem((7,)), rs_send=sem((7, 12)), rs_recv=sem((7, 12)),
            gain_send=sem((7,)), gain_recv=sem((8,)), near_send=sem((7,)), near_recv=sem((8,)), far_send=sem((3,)), far_recv=sem((4,)),
            ready=pltpu.SemaphoreType.REGULAR,
        )
        for w, (rows, columns) in enumerate(full):
            rb, cb, hb = rows // 4, columns // 2, rows // 8
            for name, shape in (("pr", (2, rb, columns)), ("xa", (hb, columns)), ("yb", (2, hb, cb)), ("ya", (hb, cb)), ("xb", (hb, cb)), ("zi", (rb, cb)), ("zx", (hb, cb))):
                rs_names.append(f"{name}{w}")
                rs_shapes.append(shape)
    ins = ["x_in", "c_in"] + [n + "_in" for n in NAMES] + ["gain_in", "seg", "bucket", "table_t"]
    outs = ["y_out", "gi_out"] + [n + "_out" for n in NAMES] + ["small_out"]
    cfg = dict(
        comm=comm, tokens=tokens, width=width, micro=micro, length=length, hidden=hidden, heads=heads, buckets=buckets, ft=ft, wide=256,
        rs_names=rs_names, rs_shapes=rs_shapes, names=ins + outs + list(scratch))
    far, near = pl.BlockSpec(memory_space=pl.ANY), pl.BlockSpec(memory_space=pltpu.VMEM)
    sh = jax.ShapeDtypeStruct
    params = dict(vmem_limit_bytes=67043328)
    if comm:
        params.update(collective_id=0, has_side_effects=True)
    return pl.pallas_call(
        functools.partial(layer, cfg),
        out_shape=[sh(tw, BF)] * 2 + [sh(w.shape, BF) for w in weights] + [sh((16, width), F32)],
        in_specs=[far] * 9 + [near] * 4, out_specs=[far] * 9 + [near], scratch_shapes=list(scratch.values()),
        compiler_params=pltpu.CompilerParams(**params),
    )(x, c, *weights, gain, seg, bucket, table_t)


def open_block(gathered, row_count, column_count):
    _, rows, columns = gathered.shape
    grid = gathered.reshape(row_count, column_count, rows, columns).transpose(0, 2, 1, 3)
    return grid.reshape(row_count * rows, column_count * columns)


def close_block(full, row_count, column_count):
    rows, columns = full.shape[0] // row_count, full.shape[1] // column_count
    grid = full.reshape(row_count, rows, column_count, columns).transpose(0, 2, 1, 3)
    return grid.reshape(row_count * column_count, rows, columns)


def shards(block_input, segment_ids, bucket, gain_attn, w_query, w_key, w_value, w_out, bias_table, gain_ffn, w_gate, w_up, w_down, cotangent):
    row_count, column_count = lax.axis_size("row"), lax.axis_size("col")
    micro, length, width = block_input.shape
    tokens = micro * length
    pieces = [w_query, w_key, w_value, w_out, w_gate, w_up, w_down]
    full = [(p.shape[0] * row_count, p.shape[1] * column_count) for p in pieces]
    fits = row_count == 4 and column_count == 2 and lax.axis_size("dp") == 4
    mine = (lax.axis_index("row") * column_count + lax.axis_index("col")) * gain_attn.shape[0]
    turned = jnp.pad(bucket[::-1], (0, 1), constant_values=-1)[None]
    gains = jnp.stack([gain_attn, gain_ffn]).astype(F32)
    x, c = block_input.reshape(tokens, width), cotangent.reshape(tokens, width)
    plane = ("row", "col")
    if fits:
        gains = lax.dynamic_update_slice(jnp.zeros((8, width), F32), gains, (0, mine))
        weights = pieces
    else:
        gains = jnp.pad(lax.all_gather(gains, plane, axis=1, tiled=True), ((0, 6), (0, 0)))
        weights = [open_block(lax.all_gather(p[None], plane, axis=0, tiled=True), row_count, column_count) for p in pieces]
    out = call_layer(fits, x, c, weights, gains, segment_ids, turned, bias_table.T, full)
    y, grad_in, grads, small = out[0], out[1], out[2:9], out[9]
    if not fits:
        small = lax.psum(small, ("dp",) + plane)
        grads = [lax.psum_scatter(close_block(g, row_count, column_count), plane, scatter_dimension=0, tiled=True)[0] for g in grads]
        grads = [lax.psum(g, "dp") for g in grads]
    gain_one, gain_two = (lax.dynamic_slice(small, (i, mine), (1, gain_attn.shape[0]))[0] for i in range(2))
    gq, gk, gv, go, gg, gu, gd = (g.astype(F32) for g in grads)
    table = small[2 : 2 + bias_table.shape[1], : bias_table.shape[0]].T
    return (
        y.reshape(block_input.shape), grad_in.reshape(block_input.shape), gain_one, gq, gk, gv, go, table, gain_two, gg, gu, gd)


def solution(mesh):
    whole = P(None, ("dp", "row", "col"), None)
    split, gain = P("row", "col"), P(("row", "col"))
    return jax.shard_map(
        shards, mesh=mesh,
        in_specs=(whole, P(None, ("dp", "row", "col")), P(), gain, split, split, split, split, P(), gain, split, split, split, whole),
        out_specs=(whole, whole, gain, split, split, split, split, P(), gain, split, split, split),
        check_vma=False)
```

time: 896 us -> 254 us (0.28)
  local copies, waits for them, and re-layouts: 483 us -> 9.21 us
  Pallas kernels: 0 us -> 235 us
  matrix products: 181 us -> 0 us
  other arithmetic: 97.4 us -> 8.55 us
  blocking collectives: 81.5 us -> 0 us
  waiting for transfers between devices: 30.4 us -> 0 us
  between operations: 16.1 us -> 0.69 us
    pallas_call x0 -> x1, Pallas kernels: none -> 235 us  [call_layer(): pl.pallas_call(functools.partial(layer, cfg), out_shape=[sh(tw, BF)] * 2...]
    reshape x18 -> x0, local copies, waits for them, and re-layouts: 192 us -> none  [the longest x3 122 us: bias_block(): skewed = tiled.reshape(head_count, block_rows, twice_len - 1)]
    dot_general x56 -> x0, matrix products: 181 us -> none  [the longest x14 40 us: left_product(): lax.dot_general(left, right, (((0,), (0,)), ((), ())), preferred_element_...]
    unnamed x213 -> x18, local copies, waits for them, and re-layouts: 176 us -> 3.97 us
    reshape x18 -> x0, other arithmetic: 61.4 us -> none  [the longest x2 37.4 us: bias_block(): tiled = jnp.tile(offsets, (1, block_rows))[:, :block_rows * (twice_len - 1)]]
    psum x2 -> x0, blocking collectives: 52.8 us -> none  [the longest x1 40.6 us: shards(): table_grad = lax.psum(table_local, ('dp', 'row', 'col'))]
    transpose x7 -> x1, local copies, waits for them, and re-layouts: 33.9 us -> 1.3 us  [shards(): table = small[2:2 + bias_table.shape[1], :bias_table.shape[0]].T]
    unnamed x2 -> x0, blocking collectives: 28.7 us -> none
  transfers between devices with their start and end apart: 15 -> 0, of which waited for: 1 -> 0; matrix products, arithmetic and copies ran while one was open for 71% -> 0% of each run, Pallas kernels for 0% -> 0%
where the time goes in v1:
time: 254 us; the launch traced here: 253 us
  Pallas kernels  235 us (93%)
  local copies, waits for them, and re-layouts  9.21 us (4%)
  other arithmetic  8.55 us (3%)
    pallas_call x1, Pallas kernels, call_layer(): pl.pallas_call(functools.partial(layer, cfg), out_shape=[sh(tw, BF)] * 2...  235 us
    convert_element_type x7, other arithmetic, shards(): gq, gk, gv, go, gg, gu, gd = (g.astype(F32) for g in grads)  7.87 us

profile of v1, /device:TPU:0, one launch (start us, length us, event | category | flops | bytes accessed | tf_op | source)
XLA Modules:
  0.0 253.3 jit_solution(10162428306341362851)
XLA Ops:
  0.7 0.7 maximum_convert_fusion
  1.3 0.6 broadcast_in_dim.6
  1.9 1.4 dynamic_update_slice.3.refs_9_
  3.3 0.8 reverse
  4.1 0.1 slice.5
  4.1 0.6 pad.4
  4.7 234.8 %shard_map.229 = (bf16[1024,768]{1,0:T(8,128)(2,1)}, bf16[1024,768]{1,0:T(8,128)(2,1)}, bf16[192,384]{1,0:T(8,128)(2,1)}, bf16[192,384]{1,0:T(8,128)(2,1)}, bf16...) custom-call(bf16[1024,768]{1,0:T(8,128)(2,1)} %bitcast.17, ...), custom_call_target="tpu_custom_call" | custom-call | tf_op jit(solution)/shard_map/pallas_call | solution.py:794
  239.6 0.0 copy-start.2
  239.6 1.4 dynamic-slice_bitcast_fusion
  240.9 1.3 slice_bitcast_fusion
  242.2 0.0 copy-start.6
  242.2 2.0 convert_element_type.29
  244.2 0.0 copy-start.5
  244.2 0.0 copy-start.4
  244.2 0.0 copy-start.3
  244.2 2.0 convert_element_type.30
  246.3 0.0 copy-start.1
  246.3 0.0 copy-done.2
  246.3 0.9 convert_element_type.31
  247.2 0.0 copy-done.6
  247.2 0.7 convert_element_type.25
  247.9 0.0 copy-done.5
  247.9 0.7 convert_element_type.26
  248.7 0.0 copy-done.4
  248.7 0.7 convert_element_type.27
  249.4 0.0 copy-done.3
  249.4 0.7 convert_element_type.28
  250.1 0.0 copy-done.1
  250.1 0.0 copy-start
  250.1 1.1 copy.29
  251.3 0.8 copy-done
  252.1 1.1 copy.30
Async XLA Ops:
  239.6 6.7 %copy-start.2 = (bf16[512,384]{1,0:T(8,128)(2,1)S(1)}, bf16[512,384]{1,0:T(8,128)(2,1)}, u32[]{:S(2)}) copy-start(bf16[512,384]{1,0:T(8,128)(2,1)} %get-tuple-element.31) | copy-start | bytes 1179652
  242.2 5.0 %copy-start.6 = (bf16[192,384]{1,0:T(8,128)(2,1)S(1)}, bf16[192,384]{1,0:T(8,128)(2,1)}, u32[]{:S(2)}) copy-start(bf16[192,384]{1,0:T(8,128)(2,1)} %get-tuple-element.25) | copy-start | bytes 442372
  244.2 3.7 %copy-start.5 = (bf16[192,384]{1,0:T(8,128)(2,1)S(1)}, bf16[192,384]{1,0:T(8,128)(2,1)}, u32[]{:S(2)}) copy-start(bf16[192,384]{1,0:T(8,128)(2,1)} %get-tuple-element.26) | copy-start | bytes 442372
  244.2 4.4 %copy-start.4 = (bf16[192,384]{1,0:T(8,128)(2,1)S(1)}, bf16[192,384]{1,0:T(8,128)(2,1)}, u32[]{:S(2)}) copy-start(bf16[192,384]{1,0:T(8,128)(2,1)} %get-tuple-element.27) | copy-start | bytes 442372
  244.2 5.2 %copy-start.3 = (bf16[192,384]{1,0:T(8,128)(2,1)S(1)}, bf16[192,384]{1,0:T(8,128)(2,1)}, u32[]{:S(2)}) copy-start(bf16[192,384]{1,0:T(8,128)(2,1)} %get-tuple-element.28) | copy-start | bytes 442372
  246.3 3.9 %copy-start.1 = (bf16[1024,768]{1,0:T(8,128)(2,1)S(1)}, bf16[1024,768]{1,0:T(8,128)(2,1)}, u32[]{:S(2)}) copy-start(bf16[1024,768]{1,0:T(8,128)(2,1)} %get-tuple-element.22) | copy-start | bytes 4718596
  250.1 2.0 copy-start

commit v2 on v1

v2 whole, which is shorter than its diff:
```python
import functools
import types

import jax
import jax.numpy as jnp
from jax import lax
from jax.experimental import pallas as pl
from jax.experimental.pallas import tpu as pltpu
from jax.sharding import PartitionSpec as P

F32 = jnp.float32
BF = jnp.bfloat16
EPSILON = 1e-06
NEGATIVE = -1e30
PRECISE = lax.Precision.HIGHEST
MESH = pl.DeviceIdType.MESH
CHUNKS = 2
GELU_0 = 0.7978845608028654
GELU_1 = 0.044715


def contract(left, right, dims, **more):
    return lax.dot_general(left, right, ((dims[:1], dims[1:]), ((), ())), preferred_element_type=F32, **more)


def nn(left, right):
    return contract(left, right, (1, 0))


def nt(left, right):
    return contract(left, right, (1, 1))


def rows_of(index, size):
    return pl.ds(pl.multiple_of(index * size, size), size)


def loop(count, body):
    lax.fori_loop(0, count, lambda index, carry: (body(index), carry)[1], 0)


def bucket_classes(s):
    return (s.turned[...] == lax.broadcasted_iota(jnp.int32, (s.buckets, 2 * s.length), 0)).astype(F32)


def offset_rows(s):
    twice = 2 * s.length
    s.turned[...] = jnp.full((1, twice), -1, jnp.int32)
    s.turned[:, 0 : twice - 1] = s.bucket[...]
    flip = (lax.broadcasted_iota(jnp.int32, (128, 128), 0) + lax.broadcasted_iota(jnp.int32, (128, 128), 1) == 127).astype(BF)
    parts = [nn(s.turned[:, i : i + 128].astype(F32).astype(BF), flip) for i in range(0, twice, 128)]
    turned = jnp.concatenate(parts[::-1], axis=1)
    s.turned[...] = pltpu.roll(turned, twice - 1, 1).astype(jnp.int32)
    s.offs[...] = contract(s.table[...], bucket_classes(s), (1, 0), precision=PRECISE)


def masks(s):
    for m in range(s.micro):
        row = s.seg[m : m + 1, :].astype(F32)
        column = jnp.broadcast_to(row, (128, s.length)).T
        for i in range(0, s.length, 128):
            s.mask[m, :, i : i + 128] = jnp.where(column == row[:, i : i + 128], 0.0, NEGATIVE)


def norm_in(s, rb):
    def body(i):
        r = rows_of(i, rb)
        x = s.x[r, :].astype(F32)
        scale = lax.rsqrt(jnp.mean(x * x, axis=-1, keepdims=True) + EPSILON)
        n = (x * scale * s.gain[0:1, :]).astype(BF)
        s.a[r, :] = n
        s.n1t[:, r] = n.T

    loop(s.tokens // rb, body)


def spot(s, pair):
    half = s.heads // 4
    return 2 * (pair % half) + pair // half


def project(s, which, rb):
    weight, out, out_t = ((s.wq, s.q, None), (s.wk, s.k, s.kt), (s.wv, s.v, s.vt))[which]

    def body(i):
        r = rows_of(i, rb)
        p = nn(s.a[r, :], weight[...]).astype(BF)
        for pair in range(s.heads // 2):
            at = 128 * spot(s, pair)
            out[r, at : at + 128] = p[:, 128 * pair : 128 * (pair + 1)]
        if out_t is not None:
            out_t[:, r] = p.T

    loop(s.tokens // rb, body)


def half_masks(dtype):
    lane = lax.broadcasted_iota(jnp.int32, (1, 128), 1)
    return [(lane < 64).astype(dtype), (lane >= 64).astype(dtype)]


def attend_pair(s, i):
    length = s.length
    blocks = length // 128
    pair = lax.div(i, 2) + (s.heads // 4) * lax.rem(i, 2)
    here = rows_of(i, 128)
    keep = half_masks(BF)
    for sub in range(2):
        head = 2 * pair + sub
        hr = rows_of(head, 64)
        row = jnp.broadcast_to(s.offs[pl.ds(head, 1), :], (128, 2 * length))
        s.toep[...] = pltpu.roll(row, 2 * length - 127, 1, stride=1, stride_axis=0)
        for m in range(s.micro):
            mr = slice(m * length, (m + 1) * length)
            scores = nt(s.k[mr, here] * keep[sub], s.q[mr, here])
            bias = jnp.concatenate([s.toep[:, 128 * j : 128 * j + length] for j in reversed(range(blocks))], axis=0)
            scores = scores + bias + s.mask[m]
            e = jnp.exp(scores - jnp.max(scores, axis=0, keepdims=True))
            low = (e * (1.0 / jnp.sum(e, axis=0, keepdims=True))).astype(BF)
            s.p[rows_of((2 * i + sub) * s.micro + m, length), :] = low
            s.ot[hr, mr] = nn(s.vt[hr, mr], low).astype(BF)


def out_project(s, rb):
    def body(i):
        r = rows_of(i, rb)
        mid = s.x[r, :].astype(F32) + nn(s.ot[:, r].T, s.wo[...])
        s.mid[r, :] = mid
        s.y[r, :] = mid
        scale = lax.rsqrt(jnp.mean(mid * mid, axis=-1, keepdims=True) + EPSILON)
        n = (mid * scale * s.gain[1:2, :]).astype(BF)
        s.k[r, :] = n
        s.n2t[:, r] = n.T
        s.dn[r, :] = jnp.zeros_like(mid)
        s.ct[:, r] = s.c[r, :].T

    loop(s.tokens // rb, body)


def ffn_rows(s, tile, ft, rb):
    cols = rows_of(tile, ft)

    def forward(i):
        r = rows_of(i, rb)
        n = s.k[r, :]
        gate = nn(n, s.wg[:, cols])
        up = nn(n, s.wu[:, cols])
        dh = nt(s.c[r, :], s.wd[cols, :])
        square = gate * gate
        t = jnp.tanh(gate * (GELU_0 + (GELU_0 * GELU_1) * square))
        half = 0.5 + 0.5 * t
        act = gate * half
        slope = half + (0.5 * gate) * (1.0 - t * t) * (GELU_0 + (3.0 * GELU_0 * GELU_1) * square)
        hid = (act * up).astype(BF)
        dg = (dh * up * slope).astype(BF)
        du = (dh * act).astype(BF)
        s.hid[r, :] = hid
        s.dg[r, :] = dg
        s.du[r, :] = du
        s.y[r, :] += nn(hid, s.wd[cols, :])
        s.dn[r, :] += nt(dg, s.wg[:, cols]) + nt(du, s.wu[:, cols])

    loop(s.tokens // rb, forward)


def ffn_grads(s, tile, ft, gb):
    cols = rows_of(tile, ft)

    def grads(i):
        r = rows_of(i, gb)
        s.wd[cols, r] = nn(s.ct[r, :], s.hid[...]).astype(BF).T
        s.wg[r, cols] = nn(s.n2t[r, :], s.dg[...]).astype(BF)
        s.wu[r, cols] = nn(s.n2t[r, :], s.du[...]).astype(BF)

    loop(s.width // gb, grads)


def ffn_close(s, rb):
    def body(i):
        r = rows_of(i, rb)
        mid = s.mid[r, :]
        dn = s.dn[r, :]
        scale = lax.rsqrt(jnp.mean(mid * mid, axis=-1, keepdims=True) + EPSILON)
        gdn = dn * s.gain[1:2, :]
        dot = jnp.mean(gdn * mid, axis=-1, keepdims=True)
        dmid = s.c[r, :].astype(F32) + scale * gdn - mid * (scale * scale * scale * dot)
        s.small[1:2, :] += jnp.sum(dn * mid * scale, axis=0, keepdims=True)
        s.dn[r, :] = dmid
        s.k[r, :] = dmid.astype(BF)
        s.c[r, :] = s.y[r, :].astype(BF)

    loop(s.tokens // rb, body)


def out_backward(s, rb):
    def body(i):
        r = rows_of(i, rb)
        d = nt(s.k[r, :], s.wo[...]).astype(BF)
        s.do[r, :] = d
        s.dot[:, r] = d.T

    loop(s.tokens // rb, body)


def out_grads(s, gb):
    def grads(i):
        r = rows_of(i, gb)
        s.wo[r, :] = nn(s.ot[r, :], s.k[...]).astype(BF)

    loop(s.width // gb, grads)


def attend_back(s, i):
    length = s.length
    blocks = length // 128
    pair = lax.div(i, 2) + (s.heads // 4) * lax.rem(i, 2)
    here, natural = rows_of(i, 128), rows_of(pair, 128)
    keep = half_masks(BF)
    left = lax.broadcasted_iota(jnp.int32, (1, 128), 1) < 64
    parts = {}
    for sub in range(2):
        head = 2 * pair + sub
        hr = rows_of(head, 64)
        for m in range(s.micro):
            mr = slice(m * length, (m + 1) * length)
            pr = rows_of((2 * i + sub) * s.micro + m, length)
            dp = nt(s.v[mr, here] * keep[sub], s.do[mr, natural])
            inner = jnp.sum(s.dot[hr, mr].astype(F32) * s.ot[hr, mr].astype(F32), axis=0, keepdims=True)
            ds = s.p[pr, :].astype(F32) * (dp - inner)
            if m == 0:
                s.toep[...] = jnp.zeros_like(s.toep)
            for j in range(blocks):
                at = 128 * (blocks - 1 - j)
                s.toep[:, at : at + length] += ds[128 * j : 128 * (j + 1), :]
            low = ds.astype(BF)
            s.ds[...] = low
            parts[sub, m, 2] = nn(s.kt[hr, mr], low)
            parts[sub, m, 0] = nn(s.ds[...], s.q[mr, here])
            parts[sub, m, 1] = nn(s.p[pr, :], s.do[mr, natural])
            if sub == 1:
                s.k[mr, here] = jnp.where(left, parts[0, m, 0], parts[1, m, 0]).astype(BF)
                s.v[mr, here] = jnp.where(left, parts[0, m, 1], parts[1, m, 1]).astype(BF)
                s.q[mr, here] = jnp.concatenate([parts[0, m, 2], parts[1, m, 2]], axis=0).astype(BF).T
        fold = s.toep[...]
        rows = 64
        while rows >= 8:
            fold = fold[:rows, :] + pltpu.roll(fold[rows:, :], 2 * length - rows, 1)
            rows //= 2
        for r in range(8):
            s.goff[r, pl.ds(head, 1), :] = fold[r : r + 1, :]


def slab(s, chunk, side):
    start = chunk * (4 * s.micro * s.length) + side * s.width
    return pl.ds(pl.multiple_of(start, 128), s.width)


def chunk_grads(s, chunk, gb):
    cols = rows_of(chunk, 256)

    def body(i):
        r = rows_of(i, gb)
        for w, grad in enumerate((s.q, s.k, s.v)):
            g = nn(s.n1t[r, :], grad[:, cols]).astype(BF)
            for side in range(2):
                start = chunk * (4 * s.micro * s.length) + side * s.width + i * gb
                s.p[pl.ds(pl.multiple_of(start, gb & -gb), gb), 128 * w : 128 * (w + 1)] = g[:, 128 * side : 128 * (side + 1)]

    loop(s.width // gb, body)


def table_grad(s):
    total = None
    for r in range(8):
        part = pltpu.roll(s.goff[r, :, :], 127 - r, 1)
        total = part if total is None else total + part
    return contract(total, bucket_classes(s), (1, 1), precision=PRECISE)


def qkv_back_input(s, rb):
    order = [spot(s, pair) for pair in range(s.heads // 2)]

    def body(i):
        r = rows_of(i, rb)
        dn = None
        for grad, weight in ((s.q, s.wq), (s.k, s.wk), (s.v, s.wv)):
            part = nt(jnp.concatenate([grad[r, 128 * at : 128 * (at + 1)] for at in order], axis=1), weight[...])
            dn = part if dn is None else dn + part
        x = s.x[r, :].astype(F32)
        scale = lax.rsqrt(jnp.mean(x * x, axis=-1, keepdims=True) + EPSILON)
        gdn = dn * s.gain[0:1, :]
        dot = jnp.mean(gdn * x, axis=-1, keepdims=True)
        s.small[0:1, :] += jnp.sum(dn * x * scale, axis=0, keepdims=True)
        s.x[r, :] = (s.dn[r, :] + scale * gdn - x * (scale * scale * scale * dot)).astype(BF)

    loop(s.tokens // rb, body)


OUT = 3


def ffn_unit(part, which):
    return 4 + 3 * part + which


def place(s):
    s.z, s.row, s.col = lax.axis_index("dp"), lax.axis_index("row"), lax.axis_index("col")
    s.core, s.xx = lax.rem(s.row, 2), lax.div(s.row, 2)
    s.row_p = 2 * s.xx + 1 - s.core
    s.row_x = 2 * (1 - s.xx) + s.core
    s.row_px = 2 * (1 - s.xx) + 1 - s.core
    s.col_y = 1 - s.col
    s.to_p, s.to_x = (s.z, s.row_p, s.col), (s.z, s.row_x, s.col)
    s.to_y, s.to_xy = (s.z, s.row, s.col_y), (s.z, s.row_x, s.col_y)
    s.me = 2 * s.row + s.col
    s.plane = [(s.z, lax.rem(s.row + (i // 2), 4), lax.rem(s.col + i % 2, 2)) for i in range(1, 8)]
    s.stack = [(lax.rem(s.z + i, 4), s.row, s.col) for i in range(1, 4)]
    s.plane_ids = [2 * row + col for _, row, col in s.plane]
    s.stack_ids = [z for z, _, _ in s.stack]
    s.inner = jnp.logical_and(s.z >= 1, s.z <= 2)
    s.outer = jnp.logical_not(s.inner)
    s.z_in, s.z_out = 1 + lax.div(s.z, 2), 3 * lax.div(s.z, 2)


def greet(s):
    barrier = pltpu.get_barrier_semaphore()
    for peer in s.plane + s.stack:
        pl.semaphore_signal(barrier, inc=1, device_id=peer, device_id_type=MESH)
    pl.semaphore_wait(barrier, len(s.plane) + len(s.stack))


def unit_shape(s, unit):
    rb, cb = s.width // 4, s.width // 2
    if unit <= OUT:
        return rb, cb
    part = s.hidden // CHUNKS
    return (part // 4, cb) if (unit - 4) % 3 == 2 else (rb, part // 2)


def span(start, size):
    return pl.ds(pl.multiple_of(start, size & -size), size)


def block(s, unit, row, col, half=None, grad=False):
    rb, cb = unit_shape(s, unit)
    size = rb if half is None else rb // 2
    down = row * rb + (0 if half is None else half * size)
    if unit < OUT and grad:
        return s.p.at[span(unit * (4 * s.micro * s.length) + col * s.width + down, size), 0:cb]
    if unit <= OUT:
        return (s.wq, s.wk, s.wv, s.wo)[unit].at[span(down, size), span(col * cb, cb)]
    part, which = divmod(unit - 4, 3)
    offset = part * (s.hidden // CHUNKS)
    if which == 2:
        return s.wd.at[span(offset + down, size), span(col * cb, cb)]
    return (s.wg, s.wu)[which].at[span(down, size), span(offset + col * cb, cb)]


def send(s, family, unit, kind, src, dst, peer):
    return pltpu.make_async_remote_copy(
        src_ref=src, dst_ref=dst, send_sem=getattr(s, family + "_send").at[unit, kind],
        recv_sem=getattr(s, family + "_recv").at[unit, kind], device_id=peer, device_id_type=MESH)


def own_source(s, unit, half=None):
    rb, cb = unit_shape(s, unit)
    if unit <= OUT:
        piece, start = s.pieces[unit], 0
    else:
        part, which = divmod(unit - 4, 3)
        if which < 2:
            return block(s, unit, s.row, s.col, half)
        piece, start = s.pieces[6], part * rb
    if half is None:
        return piece.at[start : start + rb, :]
    return piece.at[start + half * (rb // 2) : start + (half + 1) * (rb // 2), :]


def own_copies(s, unit):
    rb, cb = unit_shape(s, unit)
    own = block(s, unit, s.row, s.col)
    part, which = divmod(unit - 4, 3)
    if unit <= OUT or which == 2:
        return [pltpu.make_async_copy(own_source(s, unit), own, s.own_sems.at[unit, 0])]
    piece, half = s.pieces[4 + which], cb // 2
    size = s.hidden // 4
    offset = part * (s.hidden // CHUNKS)
    mine = (s.wg, s.wu)[which]
    return [
        pltpu.make_async_copy(
            piece.at[:, i * size + part * half : i * size + (part + 1) * half],
            mine.at[span(s.row * rb, rb), span(offset + s.col * cb + i * half, half)], s.own_sems.at[unit, i])
        for i in range(2)]


def ag_copy(s, unit, kind):
    b = functools.partial(block, s, unit)
    if kind < 3:
        return send(s, "ag", unit, kind, own_source(s, unit), b(s.row, s.col), (s.to_x, s.to_y, s.to_p)[kind])
    there, peer = [
        (b(s.row_x, s.col, 0), s.to_y), (b(s.row, s.col_y, 1), s.to_x), (b(s.row_x, s.col), s.to_p), (b(s.row, s.col_y), s.to_p),
        (b(s.row_x, s.col_y, 0), s.to_p), (b(s.row_x, s.col_y, 1), s.to_p)][kind - 3]
    return send(s, "ag", unit, kind, there, there, peer)


def ag_arrive(s, unit, kind):
    b = functools.partial(block, s, unit)
    where = [
        b(s.row_x, s.col), b(s.row, s.col_y), b(s.row_p, s.col), b(s.row_x, s.col_y, 0), b(s.row_x, s.col_y, 1),
        b(s.row_px, s.col), b(s.row_p, s.col_y), b(s.row_px, s.col_y, 0), b(s.row_px, s.col_y, 1)][kind]
    send(s, "ag", unit, kind, where, where, s.to_p).wait_recv()


def shuffled(unit):
    return unit > OUT and (unit - 4) % 3 < 2


def own_wait(s, unit):
    for copy in own_copies(s, unit):
        copy.wait()


def ag_open(s, unit):
    if shuffled(unit):
        own_wait(s, unit)
    for kind in range(3):
        ag_copy(s, unit, kind).start()


def ag_relay(s, unit):
    for kind in range(2):
        ag_arrive(s, unit, kind)
        ag_copy(s, unit, kind + 3).start()
        ag_copy(s, unit, kind + 5).start()


def ag_corner(s, unit):
    for kind in (3, 4):
        ag_arrive(s, unit, kind)
        ag_copy(s, unit, kind + 4).start()


def ag_close(s, unit):
    if not shuffled(unit):
        own_wait(s, unit)
    for kind in (2, 5, 6, 7, 8):
        ag_arrive(s, unit, kind)


def ag_sent(s, unit):
    for kind in range(9):
        ag_copy(s, unit, kind).wait_send()


def swap_copy(s, family, i, peer, slot):
    slots = getattr(s, family + "_slots")
    return pltpu.make_async_remote_copy(
        src_ref=getattr(s, family + "_from"), dst_ref=slots.at[slot], send_sem=getattr(s, family + "_send").at[i],
        recv_sem=getattr(s, family + "_recv").at[slot], device_id=peer, device_id_type=MESH)


def swap_open(s, family, peers, me):
    getattr(s, family + "_slots")[me] = getattr(s, family + "_from")[...]
    for i, peer in enumerate(peers):
        swap_copy(s, family, i, peer, me).start()


def swap_wait(s, family, peers, ids):
    for i, (peer, slot) in enumerate(zip(peers, ids)):
        copy = swap_copy(s, family, i, peer, slot)
        copy.wait_recv()
        copy.wait_send()


def swap_close(s, family, peers, ids):
    swap_wait(s, family, peers, ids)
    slots = getattr(s, family + "_slots")
    total = slots[0]
    for i in range(1, len(ids) + 1):
        total = total + slots[i]
    return total


def small_rows(s):
    return 2 * (s.width // 128) + s.heads


def small_pack(s, table):
    wide = s.width // 128
    for i in range(2):
        for j in range(wide):
            s.near_from[i * wide + j : i * wide + j + 1, :] = s.small[i : i + 1, 128 * j : 128 * (j + 1)]
    s.near_from[2 * wide : 2 * wide + s.heads, 0 : s.buckets] = table


def rs_copy(s, unit, kind):
    b = functools.partial(block, s, unit, grad=True)
    n = lambda name: getattr(s, f"{name}{unit}")
    low = s.z - 1
    if kind < 4:
        x, col = divmod(kind, 2)
        return send(s, "rs", unit, kind, b(2 * x + 1 - s.core, col), n("pr").at[x, col], s.to_p)
    if kind < 6:
        return send(s, "rs", unit, kind, b(s.row_x, kind - 4, 0), n("xa").at[kind - 4], s.to_x)
    if kind < 8:
        return send(s, "rs", unit, kind, b(2 * (kind - 6) + s.core, s.col_y, 1), n("yb").at[kind - 6], s.to_y)
    up, side = (s.z_out, s.row, s.col), (3 - s.z, s.row, s.col)
    src, dst, peer = [
        lambda: (b(s.row, s.col_y, 0), n("ya"), s.to_y),
        lambda: (b(s.row_x, s.col, 1), n("xb"), s.to_x),
        lambda: (b(s.row, s.col), n("zi"), (s.z_in, s.row, s.col)),
        lambda: (b(s.row, s.col, 1 - low), n("zx"), side),
        lambda: (b(s.row, s.col, low), b(s.row_p, s.col, low), side),
        lambda: (b(s.row, s.col, low), b(s.row_p, s.col, low), up),
        lambda: (b(s.row_p, s.col, 1 - low), b(s.row_p, s.col, 1 - low), up)][kind - 8]()
    return send(s, "rs", unit, kind, src, dst, peer)


def rs_arrive(s, unit, kind):
    b = functools.partial(block, s, unit, grad=True)
    n = lambda name: getattr(s, f"{name}{unit}")
    if kind < 4:
        where = n("pr").at[kind // 2, kind % 2]
    elif kind < 6:
        where = n("xa").at[kind - 4]
    elif kind < 8:
        where = n("yb").at[kind - 6]
    elif kind < 12:
        where = n(("ya", "xb", "zi", "zx")[kind - 8])
    else:
        where = b(s.row_p, s.col, (2 - s.z, s.z_in - 1, 2 - s.z_in)[kind - 12])
    send(s, "rs", unit, kind, where, where, s.to_p).wait_recv()
    return where


def add_into(target, source):
    rows = target.shape[0]
    step = 32 if rows % 32 == 0 else 16

    def body(i):
        r = rows_of(i, step)
        target[r, :] = (target[r, :].astype(F32) + source[r, :].astype(F32)).astype(BF)

    loop(rows // step, body)


def rs_1(s, unit):
    for kind in range(4):
        rs_copy(s, unit, kind).start()


def rs_2(s, unit):
    b = functools.partial(block, s, unit, grad=True)
    for kind in range(4):
        x, col = divmod(kind, 2)
        add_into(b(2 * x + s.core, col), rs_arrive(s, unit, kind))
    for kind in range(4, 8):
        rs_copy(s, unit, kind).start()


def rs_3(s, unit):
    b = functools.partial(block, s, unit, grad=True)
    for col in range(2):
        add_into(b(s.row, col, 0), rs_arrive(s, unit, 4 + col))
    rs_copy(s, unit, 8).start()
    for x in range(2):
        add_into(b(2 * x + s.core, s.col, 1), rs_arrive(s, unit, 6 + x))
    rs_copy(s, unit, 9).start()


def rs_4(s, unit):
    b = functools.partial(block, s, unit, grad=True)
    for half in range(2):
        add_into(b(s.row, s.col, half), rs_arrive(s, unit, 8 + half))
    for kind in range(10):
        rs_copy(s, unit, kind).wait_send()

    @pl.when(s.outer)
    def _():
        rs_copy(s, unit, 10).start()


def rs_5(s, unit):
    @pl.when(s.inner)
    def _():
        add_into(block(s, unit, s.row, s.col, grad=True), rs_arrive(s, unit, 10))
        rs_copy(s, unit, 11).start()


def rs_6(s, unit):
    @pl.when(s.inner)
    def _():
        mine = block(s, unit, s.row, s.col, s.z - 1, grad=True)
        add_into(mine, rs_arrive(s, unit, 11))
        rs_copy(s, unit, 12).start()
        rs_copy(s, unit, 13).start()
        done = block(s, unit, s.row_p, s.col, s.z - 1, grad=True)
        done[...] = mine[...]


def rs_7(s, unit):
    @pl.when(s.inner)
    def _():
        rs_arrive(s, unit, 12)
        rs_copy(s, unit, 14).start()
        for kind in (11, 12, 13):
            rs_copy(s, unit, kind).wait_send()

    @pl.when(s.outer)
    def _():
        rs_arrive(s, unit, 13)
        rs_copy(s, unit, 10).wait_send()


def rs_8(s, unit):
    @pl.when(s.inner)
    def _():
        rs_copy(s, unit, 14).wait_send()

    @pl.when(s.outer)
    def _():
        rs_arrive(s, unit, 14)

    rs_out(s, unit).start()


def rs_out(s, unit):
    return pltpu.make_async_copy(block(s, unit, s.row_p, s.col, grad=True), s.unit_out[unit], s.out_sems.at[unit])


NAMES = ("wq", "wk", "wv", "wo", "wg", "wu", "wd")
STEPS = (rs_1, rs_2, rs_3, rs_4, rs_5, rs_6, rs_7, rs_8)
G0, U0, D0, G1, U1, D1 = (ffn_unit(part, which) for part in range(2) for which in range(3))
UNITS = OUT + 1 + 3 * CHUNKS
EARLY = (G0, U0, D0)


class Reducer:
    def __init__(self, s):
        self.s, self.done = s, {unit: 0 for unit in range(UNITS)}

    def plan(self, *units):
        todo = []
        for unit in units:
            todo.append((STEPS[self.done[unit]], unit))
            self.done[unit] += 1
        return todo

    def run(self, *units):
        act_all(self.s, self.plan(*units))


def act_all(s, todo):
    for act, unit in todo if s.comm else ():
        act(s, unit)


def at_step(s, index, steps):
    for number, todo in enumerate(steps):
        if todo and s.comm:

            @pl.when(index == number)
            def _():
                act_all(s, todo)


def gather(*names):
    kinds = dict(o=ag_open, r=ag_relay, c=ag_corner, x=ag_close, s=ag_sent)
    return [(kinds[kind], unit) for kind, unit in names]


def gains_in(s):
    for i, gain in enumerate((s.gain_one, s.gain_two)):
        if s.comm:
            s.gain_from[i : i + 1, 0 : gain.shape[1]] = gain[...].astype(F32)
        else:
            s.gain[i : i + 1, :] = gain[...].astype(F32)


def gains_spread(s):
    swap_wait(s, "gain", s.plane, s.plane_ids)
    count = s.gain_one.shape[1]
    wide = (128, s.width)
    lane, spot = lax.broadcasted_iota(jnp.int32, wide, 0), lax.broadcasted_iota(jnp.int32, wide, 1)
    total = None
    for i in range(8):
        part = nn(s.gain_slots[i].astype(BF), jnp.logical_and(spot == lane + count * i, lane < count).astype(BF))
        total = part if total is None else total + part
    s.gain[...] = total


def layer(cfg, *refs):
    s = types.SimpleNamespace(**cfg)
    for name, ref in zip(cfg["names"], refs):
        setattr(s, name, ref)
    s.pieces = [getattr(s, n + "_in") for n in NAMES]
    comm = s.comm
    load_x = pltpu.make_async_copy(s.x_in, s.x, s.io_sems.at[0])
    load_c = pltpu.make_async_copy(s.c_in, s.c, s.io_sems.at[1])
    load_x.start()
    load_c.start()
    Q, K, V, O = range(4)
    if comm:
        place(s)
        s.unit_out = [getattr(s, f"unit{u}_out") for u in range(UNITS)]
        greet(s)
        for unit in range(UNITS):
            for copy in own_copies(s, unit):
                copy.start()
        act_all(s, gather(("o", Q), ("o", K)))
        s.gain_from[...] = jnp.zeros_like(s.gain_from)
        gains_in(s)
        swap_open(s, "gain", s.plane, s.me)
    else:
        weights = [pltpu.make_async_copy(piece, getattr(s, n), s.load_sems.at[i]) for i, (n, piece) in enumerate(zip(NAMES, s.pieces))]
        for copy in weights:
            copy.start()
        gains_in(s)
    s.small[...] = jnp.zeros_like(s.small)
    s.near_from[...] = jnp.zeros_like(s.near_from)
    offset_rows(s)
    tw, wt = (s.tokens, s.width), (s.width, s.tokens)
    vm = pltpu.VMEM

    def attention(a, mask):
        s.a, s.mask = a, mask
        masks(s)
        load_x.wait()
        if comm:
            gains_spread(s)
        else:
            for copy in weights:
                copy.wait()
        norm_in(s, 128)
        act_all(s, gather(("r", Q), ("o", V), ("r", K), ("c", Q), ("o", O), ("r", V), ("c", K), ("o", G0), ("x", Q)))
        project(s, Q, 256)
        act_all(s, gather(("c", V), ("x", K)))
        project(s, K, 256)
        act_all(s, gather(("r", O), ("o", U0), ("x", V)))
        project(s, V, 256)
        plan = [
            gather(("c", O), ("r", G0)), gather(("o", D0)), gather(("c", G0), ("r", U0), ("o", G1)), gather(("c", U0)),
            gather(("r", D0), ("o", U1)), gather(("c", D0), ("r", G1), ("o", D1))]

        def step(i):
            at_step(s, i, plan)
            attend_pair(s, i)

        loop(s.heads // 2, step)

    pl.run_scoped(attention, vm(tw, BF), vm((s.micro, s.length, s.length), F32))
    reducer = Reducer(s)
    reduce = reducer.run
    s.n2t = s.vt

    def feed(act, mid, y, ct):
        s.mid, s.y, s.ct = mid, y, ct
        s.hid, s.dg, s.du = (act.at[:, i * s.ft : (i + 1) * s.ft] for i in range(3))
        load_c.wait()
        act_all(s, gather(("x", O)))
        out_project(s, 256)
        act_all(s, gather(("c", G1), ("r", U1), ("x", G0), ("x", U0), ("x", D0)))
        plan = reducer.plan
        ahead, amid = [[], gather(("c", U1), ("r", D1))], [gather(*[("s", u) for u in EARLY]), gather(("c", D1))]
        ahead.append(gather(("x", G1), ("x", U1), ("x", D1)) + plan(G0, U0, D0))
        amid.append(gather(*[("s", u) for u in (G1, U1, D1)]) + plan(G0, U0))
        ahead.append(plan(G0, D0))
        amid.append(plan(U0, G0))

        def step(t):
            at_step(s, t, ahead)
            ffn_rows(s, t, s.ft, 256)
            at_step(s, t, amid)
            ffn_grads(s, t, s.ft, s.gb)

        loop(s.hidden // s.ft, step)
        ffn_close(s, 128)

    pl.run_scoped(feed, vm((s.tokens, 3 * s.ft), BF), vm(tw, F32), vm(tw, F32), vm(wt, BF))
    put_y = pltpu.make_async_copy(s.c, s.y_out, s.io_sems.at[0])
    put_x = pltpu.make_async_copy(s.x, s.gi_out, s.io_sems.at[1])
    put_y.start()

    def back(dot, *bufs):
        s.do, s.dot = s.c, dot
        for name, ref in zip(s.rs_names, bufs):
            setattr(s, name, ref)
        if comm:
            for peer in [s.to_p, s.to_x, s.to_y] + s.stack:
                pl.semaphore_signal(s.ready, inc=1, device_id=peer, device_id_type=MESH)
            pl.semaphore_wait(s.ready, 6)
        reduce(G1, U1, D1, D0, U0, G0)
        put_y.wait()
        out_backward(s, 256)
        act_all(s, gather(("s", Q), ("s", K), ("s", V), ("s", O)))
        out_grads(s, 256)
        reduce(O, G1, D0, U0, G0)
        plan = reducer.plan
        reducer.done.update({0: 1, 1: 1, 2: 1})
        ahead = [
            plan(U1, G1), plan(D1, D0, U0, G0), plan(U1, G1, O, D0, U0, G0), plan(D1, G1, U1, U0, 0), plan(O, G1, U1, D1, D0),
            plan(O, G1, U1, D1, D0, 0, 1)]

        def step(i):
            at_step(s, i, ahead)
            attend_back(s, i)

            @pl.when(lax.rem(i, 2) == 1)
            def _():
                chunk = lax.div(i, 2)
                chunk_grads(s, chunk, 384)
                at_step(s, chunk, [[(rs_1, unit)] for unit in range(3)])

        loop(s.heads // 2, step)
        reduce(2, 1, 0, O, D1, U1, G1)
        table = table_grad(s)
        qkv_back_input(s, 256)
        put_x.start()
        small_pack(s, table)
        if comm:
            swap_open(s, "near", s.plane, s.me)
            left = lambda: [u for u in (2, 1, 0, O, D1, U1, G1) + EARLY if reducer.done[u] < 8]
            reduce(*left())
            s.far_from[...] = swap_close(s, "near", s.plane, s.plane_ids)
            swap_open(s, "far", s.stack, s.z)
            while left():
                reduce(*left())
            s.small_out[...] = swap_close(s, "far", s.stack, s.stack_ids)
            for unit in range(UNITS):
                rs_out(s, unit).wait()
        else:
            s.small_out[...] = s.near_from[...]
            outs = [pltpu.make_async_copy(getattr(s, n), getattr(s, n + "_out"), s.load_sems.at[i + 3]) for i, n in enumerate(NAMES[3:])]
            for copy in outs:
                copy.start()
            for copy in outs:
                copy.wait()
            half = s.heads // 4
            for w, n in enumerate(NAMES[:3]):
                for pair in range(s.heads // 2):
                    copy = pltpu.make_async_copy(
                        s.p.at[slab(s, pair % half, pair // half), 128 * w : 128 * (w + 1)],
                        getattr(s, n + "_out").at[:, 128 * pair : 128 * (pair + 1)], s.load_sems.at[w])
                    copy.start()
                    copy.wait()

    pl.run_scoped(back, vm(wt, BF), *[vm(shape, BF) for shape in s.rs_shapes])
    put_x.wait()


def call_layer(comm, x, c, weights, gains, seg, bucket, table, full):
    tokens, width = x.shape
    micro, length = seg.shape
    heads, buckets = table.shape
    hidden = full[4][1]
    ft, vm, sem = 512, pltpu.VMEM, pltpu.SemaphoreType.DMA
    tw, wt, tiny = (tokens, width), (width, tokens), (2 * (width // 128) + heads, 128)
    s = types.SimpleNamespace(
        comm=comm, tokens=tokens, width=width, micro=micro, length=length, hidden=hidden, heads=heads, buckets=buckets, ft=ft, gb=256,
        rs_names=[], rs_shapes=[])
    scratch = dict(
        x=vm(tw, BF), c=vm(tw, BF), **{n: vm(shape, BF) for n, shape in zip(NAMES, full)},
        n1t=vm(wt, BF), q=vm(tw, BF), k=vm(tw, BF), v=vm(tw, BF), kt=vm(wt, BF), vt=vm(wt, BF), ot=vm(wt, BF),
        dn=vm(tw, F32), toep=vm((128, 2 * length), F32), ds=vm((length, length), BF), p=vm((heads * micro * length, length), BF),
        offs=vm((heads, 2 * length), F32), goff=vm((8, heads, 2 * length), F32), gain=vm((8, width), F32), small=vm((2, width), F32), near_from=vm(tiny, F32),
        turned=vm((1, 2 * length), jnp.int32), io_sems=sem((2,)), load_sems=sem((7,)), out_sems=sem((UNITS,)),
    )
    out_shape = [(tw, BF)] * 2
    if comm:
        scratch.update(
            gain_from=vm((8, 128), F32), far_from=vm(tiny, F32),
            gain_slots=vm((8, 8, 128), F32), near_slots=vm((8, *tiny), F32), far_slots=vm((4, *tiny), F32),
            ag_send=sem((UNITS, 9)), ag_recv=sem((UNITS, 9)), own_sems=sem((UNITS, 2)), rs_send=sem((UNITS, 15)), rs_recv=sem((UNITS, 15)),
            gain_send=sem((7,)), gain_recv=sem((8,)), near_send=sem((7,)), near_recv=sem((8,)), far_send=sem((3,)), far_recv=sem((4,)),
            ready=pltpu.SemaphoreType.REGULAR,
        )
        for unit in range(UNITS):
            rb, cb = unit_shape(s, unit)
            hb = rb // 2
            shapes = dict(pr=(2, 2, rb, cb), xa=(2, hb, cb), yb=(2, hb, cb), ya=(hb, cb), xb=(hb, cb), zi=(rb, cb), zx=(hb, cb))
            for name, shape in shapes.items():
                if unit in EARLY:
                    scratch[f"{name}{unit}"] = vm(shape, BF)
                else:
                    s.rs_names.append(f"{name}{unit}")
                    s.rs_shapes.append(shape)
            out_shape.append(((rb, cb), BF))
        grad_names = [f"unit{unit}_out" for unit in range(UNITS)]
    else:
        out_shape += [(shape, BF) for shape in full]
        grad_names = [n + "_out" for n in NAMES]
    ins = ["x_in", "c_in"] + [n + "_in" for n in NAMES] + ["gain_one", "gain_two", "seg", "bucket", "table"]
    outs = ["y_out", "gi_out"] + grad_names + ["small_out"]
    out_shape.append((tiny, F32))
    names = ins + outs + list(scratch)
    far, near = pl.BlockSpec(memory_space=pl.ANY), pl.BlockSpec(memory_space=pltpu.VMEM)
    params = dict(vmem_limit_bytes=67043328)
    if comm:
        params.update(collective_id=0, has_side_effects=True)

    def body(*refs):
        cfg = dict(vars(s), names=names)
        layer(cfg, *refs)

    return pl.pallas_call(
        body, out_shape=[jax.ShapeDtypeStruct(*o) for o in out_shape],
        in_specs=[far] * 9 + [near] * 5, out_specs=[far] * (len(outs) - 1) + [near], scratch_shapes=list(scratch.values()),
        compiler_params=pltpu.CompilerParams(**params),
    )(x, c, *weights, *gains, seg, bucket, table)


def finish_kernel(cfg, *refs):
    s = types.SimpleNamespace(**cfg)
    small, srcs, outs = refs[0], refs[1 : 3 + UNITS], refs[3 + UNITS : 3 + UNITS + 12]
    bufs = refs[15 + UNITS : 15 + 2 + 2 * UNITS]
    wide, (in_sems, out_sems) = refs[17 + 2 * UNITS : -2], refs[-2:]
    loads = [pltpu.make_async_copy(src, buf, in_sems.at[i]) for i, (src, buf) in enumerate(zip(srcs, bufs))]
    for i in list(range(2, len(loads))) + [0, 1]:
        loads[i].start()
    row, col = lax.axis_index("row"), lax.axis_index("col")
    y, gi, gain_one, gq, gk, gv, go, table, gain_two, gg, gu, gd = outs
    rows = s.width // 128
    at = lax.rem(s.width - s.gain_count * (2 * row + col), s.width)
    for i, out in enumerate((gain_one, gain_two)):
        full = jnp.concatenate([small[i * rows + j : i * rows + j + 1, :] for j in range(rows)], axis=1)
        out[...] = pltpu.roll(jnp.broadcast_to(full, (8, s.width)), at, 1)[0:1, 0 : s.gain_count]
    table[...] = small[2 * rows : 2 * rows + s.heads, 0 : s.buckets]
    units = bufs[2:]
    stores = []

    def leave(buf, out):
        stores.append(pltpu.make_async_copy(buf, out, out_sems.at[len(stores)]))
        stores[-1].start()

    wq, wk, wv, wo, wg, wu, wd = wide
    for unit in range(3):
        loads[2 + unit].wait()
        for w, buf in enumerate((wq, wk, wv)):
            buf[:, 128 * unit : 128 * (unit + 1)] = units[unit][:, 128 * w : 128 * (w + 1)].astype(F32)
    for buf, out in ((wq, gq), (wk, gk), (wv, gv)):
        leave(buf, out)
    loads[2 + OUT].wait()
    wo[...] = units[OUT][...].astype(F32)
    leave(wo, go)
    for which, buf, out in ((0, wg, gg), (1, wu, gu), (2, wd, gd)):
        for part in range(CHUNKS):
            unit = ffn_unit(part, which)
            loads[2 + unit].wait()
            rows, cols = units[unit].shape
            if which == 2:
                buf[part * rows : (part + 1) * rows, :] = units[unit][...].astype(F32)
            else:
                size = buf.shape[1] // 2
                for i in range(2):
                    at = i * size + part * (cols // 2)
                    buf[:, at : at + cols // 2] = units[unit][:, i * (cols // 2) : (i + 1) * (cols // 2)].astype(F32)
        leave(buf, out)
    for i, out in enumerate((y, gi)):
        loads[i].wait()
        leave(bufs[i], out)
    for copy in stores:
        copy.wait()


def finish(small, arrays, gain_count, heads, buckets, blocks):
    vm, sh = pltpu.VMEM, jax.ShapeDtypeStruct
    far, near = pl.BlockSpec(memory_space=pl.ANY), pl.BlockSpec(memory_space=pltpu.VMEM)
    y, gi = arrays[:2]
    b = [sh(shape, F32) for shape in blocks]
    gain = sh((1, gain_count), F32)
    cfg = dict(width=y.shape[1], gain_count=gain_count, heads=heads, buckets=buckets)
    return pl.pallas_call(
        functools.partial(finish_kernel, cfg),
        out_shape=[sh(y.shape, BF), sh(gi.shape, BF), gain, *b[:4], sh((heads, buckets), F32), gain, *b[4:]],
        in_specs=[near] + [far] * len(arrays), out_specs=[far, far, near, far, far, far, far, near, near, far, far, far],
        scratch_shapes=[vm(a.shape, BF) for a in arrays] + [vm(shape, F32) for shape in blocks]
        + [pltpu.SemaphoreType.DMA((len(arrays),)), pltpu.SemaphoreType.DMA((9,))],
        compiler_params=pltpu.CompilerParams(vmem_limit_bytes=67043328),
    )(small, *arrays)


def open_block(gathered, row_count, column_count):
    _, rows, columns = gathered.shape
    grid = gathered.reshape(row_count, column_count, rows, columns).transpose(0, 2, 1, 3)
    return grid.reshape(row_count * rows, column_count * columns)


def close_block(full, row_count, column_count):
    rows, columns = full.shape[0] // row_count, full.shape[1] // column_count
    grid = full.reshape(row_count, rows, column_count, columns).transpose(0, 2, 1, 3)
    return grid.reshape(row_count * column_count, rows, columns)


def shards(block_input, segment_ids, bucket, gain_attn, w_query, w_key, w_value, w_out, bias_table, gain_ffn, w_gate, w_up, w_down, cotangent):
    row_count, column_count = lax.axis_size("row"), lax.axis_size("col")
    micro, length, width = block_input.shape
    tokens, gain_count = micro * length, gain_attn.shape[0]
    buckets, heads = bias_table.shape
    pieces = [w_query, w_key, w_value, w_out, w_gate, w_up, w_down]
    full = [(p.shape[0] * row_count, p.shape[1] * column_count) for p in pieces]
    fits = row_count == 4 and column_count == 2 and lax.axis_size("dp") == 4
    x, c = block_input.reshape(tokens, width), cotangent.reshape(tokens, width)
    gains = [gain_attn[None], gain_ffn[None]]
    plane = ("row", "col")
    if fits:
        out = call_layer(True, x, c, pieces, gains, segment_ids, bucket[None], bias_table.T, full)
        y, gi, one, gq, gk, gv, go, table, two, gg, gu, gd = finish(
            out[-1], out[:-1], gain_count, heads, buckets, [p.shape for p in pieces])
        return y.reshape(block_input.shape), gi.reshape(block_input.shape), one[0], gq, gk, gv, go, table.T, two[0], gg, gu, gd
    gains = [lax.all_gather(g, plane, axis=1, tiled=True) for g in gains]
    weights = [open_block(lax.all_gather(p[None], plane, axis=0, tiled=True), row_count, column_count) for p in pieces]
    out = call_layer(False, x, c, weights, gains, segment_ids, bucket[None], bias_table.T, full)
    y, gi, grads, small = out[0], out[1], out[2:9], out[9]
    small = lax.psum(small, ("dp",) + plane)
    grads = [lax.psum_scatter(close_block(g, row_count, column_count), plane, scatter_dimension=0, tiled=True)[0] for g in grads]
    gq, gk, gv, go, gg, gu, gd = (lax.psum(g, "dp").astype(F32) for g in grads)
    mine = (lax.axis_index("row") * column_count + lax.axis_index("col")) * gain_count
    one, two = (lax.dynamic_slice(small[i * (width // 128) : (i + 1) * (width // 128)].reshape(-1), (mine,), (gain_count,)) for i in range(2))
    table = small[2 * (width // 128) :, :buckets].T
    return y.reshape(block_input.shape), gi.reshape(block_input.shape), one, gq, gk, gv, go, table, two, gg, gu, gd


def solution(mesh):
    whole = P(None, ("dp", "row", "col"), None)
    split, gain = P("row", "col"), P(("row", "col"))
    return jax.shard_map(
        shards, mesh=mesh,
        in_specs=(whole, P(None, ("dp", "row", "col")), P(), gain, split, split, split, split, P(), gain, split, split, split, whole),
        out_specs=(whole, whole, gain, split, split, split, split, P(), gain, split, split, split),
        check_vma=False)
```

time: 254 us -> 193 us (0.76)
  Pallas kernels: 235 us -> 192 us
  local copies, waits for them, and re-layouts: 9.21 us -> 0 us
  other arithmetic: 8.55 us -> 0 us
    pallas_call x1 -> x2, Pallas kernels: 235 us -> 192 us  [the longest x1 185 us: call_layer(): pl.pallas_call(body, out_shape=[jax.ShapeDtypeStruct(*o) for o in out_sha...]
    convert_element_type x8 -> x0, other arithmetic: 8.55 us -> none  [the longest x7 7.87 us: shards(): gq, gk, gv, go, gg, gu, gd = (g.astype(F32) for g in grads)]
    unnamed x18 -> x0, local copies, waits for them, and re-layouts: 3.97 us -> none
where the time goes in v2:
time: 193 us; the launch traced here: 192 us
  Pallas kernels  192 us (99%)
    pallas_call x1, Pallas kernels, call_layer(): pl.pallas_call(body, out_shape=[jax.ShapeDtypeStruct(*o) for o in out_sha...  185 us
    pallas_call x1, Pallas kernels, finish(): pl.pallas_call(functools.partial(finish_kernel, cfg), out_shape=[sh(y.sha...  6.45 us

profile of v2, /device:TPU:0, one launch (start us, length us, event | category | flops | bytes accessed | tf_op | source)
XLA Modules:
  0.0 192.3 jit_solution(12021083228388653037)
XLA Ops:
  0.6 185.1 %shard_map.229 = (bf16[1024,768]{1,0:T(8,128)(2,1)}, bf16[1024,768]{1,0:T(8,128)(2,1)}, bf16[192,384]{1,0:T(8,128)(2,1)}, bf16[192,384]{1,0:T(8,128)(2,1)}, bf16...) custom-call(bf16[1024,768]{1,0:T(8,128)(2,1)} %bitcast.11, ...), custom_call_target="tpu_custom_call" | custom-call | tf_op jit(solution)/shard_map/pallas_call | solution.py:905
  185.7 6.5 %shard_map.230 = (bf16[1024,768]{1,0:T(8,128)(2,1)}, bf16[1024,768]{1,0:T(8,128)(2,1)}, f32[1,96]{1,0:T(1,128)}, f32[192,384]{1,0:T(8,128)}, f32[192,384]{1,0:T(...) custom-call(f32[24,128]{1,0:T(8,128)} %get-tuple-element.37.refs_0_,, ...), custom_call_target="tpu_custom_call" | custom-call | tf_op jit(solution)/shard_map/pallas_call | solution.py:972

commit v3 on v2

--- a/solution.py
+++ b/solution.py
@@ -14,7 +14,7 @@
 NEGATIVE = -1e30
 PRECISE = lax.Precision.HIGHEST
 MESH = pl.DeviceIdType.MESH
-CHUNKS = 2
+CHUNKS = 4
 GELU_0 = 0.7978845608028654
 GELU_1 = 0.044715
 
@@ -79,17 +79,18 @@
     return 2 * (pair % half) + pair // half
 
 
-def project(s, which, rb):
+def project(s, which, side, rb):
     weight, out, out_t = ((s.wq, s.q, None), (s.wk, s.k, s.kt), (s.wv, s.v, s.vt))[which]
+    wide = s.width // 2
+    cols = pl.ds(pl.multiple_of(side * wide, 128), wide)
 
     def body(i):
         r = rows_of(i, rb)
-        p = nn(s.a[r, :], weight[...]).astype(BF)
-        for pair in range(s.heads // 2):
-            at = 128 * spot(s, pair)
-            out[r, at : at + 128] = p[:, 128 * pair : 128 * (pair + 1)]
+        p = nn(s.a[r, :], weight[:, cols]).astype(BF)
+        for j in range(s.heads // 4):
+            out[r, rows_of(2 * j + side, 128)] = p[:, 128 * j : 128 * (j + 1)]
         if out_t is not None:
-            out_t[:, r] = p.T
+            out_t[cols, r] = p.T
 
     loop(s.tokens // rb, body)
 
@@ -99,13 +100,14 @@
     return [(lane < 64).astype(dtype), (lane >= 64).astype(dtype)]
 
 
-def attend_pair(s, i):
+def attend_pair(s, side, late, j):
     length = s.length
     blocks = length // 128
-    pair = lax.div(i, 2) + (s.heads // 4) * lax.rem(i, 2)
+    pair, i = (s.heads // 4) * side + j, 2 * j + side
     here = rows_of(i, 128)
     keep = half_masks(BF)
     for sub in range(2):
+        s.hook("attend", late + 2 * j + sub)
         head = 2 * pair + sub
         hr = rows_of(head, 64)
         row = jnp.broadcast_to(s.offs[pl.ds(head, 1), :], (128, 2 * length))
@@ -113,7 +115,7 @@
         for m in range(s.micro):
             mr = slice(m * length, (m + 1) * length)
             scores = nt(s.k[mr, here] * keep[sub], s.q[mr, here])
-            bias = jnp.concatenate([s.toep[:, 128 * j : 128 * j + length] for j in reversed(range(blocks))], axis=0)
+            bias = jnp.concatenate([s.toep[:, 128 * b : 128 * b + length] for b in reversed(range(blocks))], axis=0)
             scores = scores + bias + s.mask[m]
             e = jnp.exp(scores - jnp.max(scores, axis=0, keepdims=True))
             low = (e * (1.0 / jnp.sum(e, axis=0, keepdims=True))).astype(BF)
@@ -141,6 +143,7 @@
     cols = rows_of(tile, ft)
 
     def forward(i):
+        s.hook("feed", 5 * tile + i)
         r = rows_of(i, rb)
         n = s.k[r, :]
         gate = nn(n, s.wg[:, cols])
@@ -194,6 +197,7 @@
 
 def out_backward(s, rb):
     def body(i):
+        s.hook("outback", i)
         r = rows_of(i, rb)
         d = nt(s.k[r, :], s.wo[...]).astype(BF)
         s.do[r, :] = d
@@ -219,6 +223,7 @@
     left = lax.broadcasted_iota(jnp.int32, (1, 128), 1) < 64
     parts = {}
     for sub in range(2):
+        s.hook("back", 2 * i + sub)
         head = 2 * pair + sub
         hr = rows_of(head, 64)
         for m in range(s.micro):
@@ -281,6 +286,7 @@
     order = [spot(s, pair) for pair in range(s.heads // 2)]
 
     def body(i):
+        s.hook("input", i + 1)
         r = rows_of(i, rb)
         dn = None
         for grad, weight in ((s.q, s.wq), (s.k, s.wk), (s.v, s.wv)):
@@ -440,11 +446,21 @@
         ag_copy(s, unit, kind + 4).start()
 
 
-def ag_close(s, unit):
+def ag_near(s, unit):
     if not shuffled(unit):
         own_wait(s, unit)
-    for kind in (2, 5, 6, 7, 8):
+    for kind in (2, 5):
         ag_arrive(s, unit, kind)
+
+
+def ag_far(s, unit):
+    for kind in (6, 7, 8):
+        ag_arrive(s, unit, kind)
+
+
+def ag_close(s, unit):
+    ag_near(s, unit)
+    ag_far(s, unit)
 
 
 def ag_sent(s, unit):
@@ -493,10 +509,23 @@
     s.near_from[2 * wide : 2 * wide + s.heads, 0 : s.buckets] = table
 
 
+DIRECT = 2
+
+
+def quarter(s, unit, row, index):
+    rb, cb = unit_shape(s, unit)
+    return s.p.at[span(unit * (4 * s.micro * s.length) + s.col * s.width + row * rb + index * (rb // 4), rb // 4), 0:cb]
+
+
 def rs_copy(s, unit, kind):
     b = functools.partial(block, s, unit, grad=True)
     n = lambda name: getattr(s, f"{name}{unit}")
     low = s.z - 1
+    if unit == DIRECT and kind >= 10:
+        peer, there = s.stack[(kind - 10) % 3], s.stack_ids[(kind - 10) % 3]
+        if kind < 13:
+            return send(s, "rs", unit, kind, quarter(s, unit, s.row, there), n("zq").at[kind - 10], peer)
+        return send(s, "rs", unit, kind, quarter(s, unit, s.row, s.z), quarter(s, unit, s.row_p, s.z), peer)
     if kind < 4:
         x, col = divmod(kind, 2)
         return send(s, "rs", unit, kind, b(2 * x + 1 - s.core, col), n("pr").at[x, col], s.to_p)
@@ -519,7 +548,11 @@
 def rs_arrive(s, unit, kind):
     b = functools.partial(block, s, unit, grad=True)
     n = lambda name: getattr(s, f"{name}{unit}")
-    if kind < 4:
+    if unit == DIRECT and kind >= 13:
+        where = quarter(s, unit, s.row_p, lax.rem(s.z + 4 - (kind - 12), 4))
+    elif unit == DIRECT and kind >= 10:
+        where = n("zq").at[kind - 10]
+    elif kind < 4:
         where = n("pr").at[kind // 2, kind % 2]
     elif kind < 6:
         where = n("xa").at[kind - 4]
@@ -539,7 +572,7 @@
 
     def body(i):
         r = rows_of(i, step)
-        target[r, :] = (target[r, :].astype(F32) + source[r, :].astype(F32)).astype(BF)
+        target[r, :] = target[r, :] + source[r, :]
 
     loop(rows // step, body)
 
@@ -574,6 +607,10 @@
         add_into(b(s.row, s.col, half), rs_arrive(s, unit, 8 + half))
     for kind in range(10):
         rs_copy(s, unit, kind).wait_send()
+    if unit == DIRECT:
+        for kind in (11, 10, 12):
+            rs_copy(s, unit, kind).start()
+        return
 
     @pl.when(s.outer)
     def _():
@@ -581,6 +618,15 @@
 
 
 def rs_5(s, unit):
+    if unit == DIRECT:
+        mine = quarter(s, unit, s.row, s.z)
+        for kind in (10, 12, 11):
+            add_into(mine, rs_arrive(s, unit, kind))
+        for kind in (14, 13, 15):
+            rs_copy(s, unit, kind).start()
+        quarter(s, unit, s.row_p, s.z)[...] = mine[...]
+        return
+
     @pl.when(s.inner)
     def _():
         add_into(block(s, unit, s.row, s.col, grad=True), rs_arrive(s, unit, 10))
@@ -588,6 +634,14 @@
 
 
 def rs_6(s, unit):
+    if unit == DIRECT:
+        for kind in (13, 15, 14):
+            rs_arrive(s, unit, kind)
+        for kind in range(10, 16):
+            rs_copy(s, unit, kind).wait_send()
+        rs_out(s, unit).start()
+        return
+
     @pl.when(s.inner)
     def _():
         mine = block(s, unit, s.row, s.col, s.z - 1, grad=True)
@@ -628,45 +682,95 @@
     return pltpu.make_async_copy(block(s, unit, s.row_p, s.col, grad=True), s.unit_out[unit], s.out_sems.at[unit])
 
 
+PLAN = {
+    ("start", 0): (("o", 0), ("o", 1), ("o", 2)),
+    ("project", 0): (("r", 0), ("n", 0), ("o", 3)),
+    ("project", 1): (("r", 1), ("n", 1)),
+    ("project", 2): (("o", 4), ("r", 2), ("n", 2), ("c", 0)),
+    ("attend", 0): (("o", 5),),
+    ("attend", 1): (("r", 3),),
+    ("attend", 2): (("c", 1), ("o", 6)),
+    ("attend", 4): (("r", 4), ("o", 7)),
+    ("attend", 5): (("c", 2),),
+    ("project", 3): (("r", 5), ("f", 0), ("o", 8)),
+    ("project", 4): (("c", 3), ("f", 1)),
+    ("project", 5): (("o", 9), ("r", 6), ("f", 2)),
+    ("attend", 6): (("c", 4), ("o", 10)),
+    ("attend", 7): (("r", 7),),
+    ("attend", 8): (("c", 5),),
+    ("attend", 9): (("o", 11),),
+    ("attend", 10): (("r", 8),),
+    ("attend", 11): (("r", 9),),
+    ("feed_in", 0): (("c", 6), ("o", 12), ("x", 3)),
+    ("feed", 0): (("c", 7), ("r", 10), ("r", 11), ("o", 13), ("x", 4), ("x", 5), ("x", 6)),
+    ("feed", 1): (("c", 8), ("c", 9), ("o", 14), ("o", 15), ("r", 12)),
+    ("feed", 4): (("c", 10), ("c", 11)),
+    ("feed", 5): (("r", 13), ("r", 14), (1, 4), (1, 5), (1, 6), ("x", 7), ("x", 8), ("x", 9)),
+    ("feed", 6): (("c", 12), ("r", 15), (2, 4)),
+    ("feed", 9): (("c", 13), ("c", 14), (2, 5), (2, 6)),
+    ("feed", 10): (("c", 15), (3, 4), (1, 7), (1, 8), (1, 9), ("x", 10), ("x", 11), ("x", 12)),
+    ("feed", 11): ((3, 5), (2, 7), (2, 8), (3, 6)),
+    ("feed", 14): ((4, 4), (2, 9), (4, 5)),
+    ("feed", 15): ((3, 7), ("x", 13), ("x", 14), ("x", 15)),
+    ("feed", 16): ((5, 4), (4, 6), (3, 8), (3, 9), (5, 5)),
+    ("feed", 19): ((4, 7),),
+    ("close", 0): ((6, 4), (6, 5), (5, 6), (4, 8), (4, 9)),
+    ("outback", 0): ((5, 7), (1, 10), (1, 11), (1, 12), (1, 13), (1, 14), (1, 15)),
+    ("outback", 1): ((7, 4),),
+    ("outback", 2): ((7, 5),),
+    ("outback", 3): ((6, 6), (5, 8), (2, 10), (2, 11), (6, 7)),
+    ("outgrad", 0): ((5, 9), (2, 12), (2, 13), (8, 4)),
+    ("outgrad", 1): ((1, 3), (8, 5), (7, 6), (2, 14), (2, 15)),
+    ("back", 1): ((7, 7), (6, 8), (3, 10)),
+    ("back", 2): ((6, 9), (3, 11), (2, 3), (8, 6)),
+    ("back", 3): ((3, 12),),
+    ("chunk", 0): ((1, 0), (8, 7), (7, 8), (7, 9), (3, 13), (3, 14)),
+    ("back", 5): ((3, 15),),
+    ("back", 6): ((4, 10), (4, 11), (2, 0)),
+    ("back", 7): ((8, 8), (8, 9)),
+    ("chunk", 1): ((1, 1), (4, 12), (4, 13), (3, 3), (5, 10), (4, 14)),
+    ("back", 9): ((5, 11), (4, 15)),
+    ("back", 10): ((2, 1),),
+    ("back", 11): ((6, 10), (5, 12), (4, 3), (3, 0)),
+    ("chunk", 2): ((1, 2), (6, 11), (5, 13), (5, 14), (7, 10)),
+    ("input", 1): ((3, 1), (6, 12), (5, 15)),
+    ("input", 2): ((4, 0), (2, 2)),
+    ("input", 3): ((7, 11), (5, 3), (8, 10), (6, 13)),
+    ("input", 4): ((6, 14), (4, 1), (7, 12)),
+    ("tail", 0): ((6, 15), (8, 11), (5, 0), (3, 2), (6, 3), (7, 13), (7, 14), (8, 12), (7, 15), (5, 1), (4, 2), (6, 0), (8, 13), (7, 3), (8, 14), (6, 1), (8, 15), (8, 3), (5, 2), (7, 0), (7, 1), (8, 0), (8, 1), (6, 2)),
+}
+
+
 NAMES = ("wq", "wk", "wv", "wo", "wg", "wu", "wd")
-STEPS = (rs_1, rs_2, rs_3, rs_4, rs_5, rs_6, rs_7, rs_8)
-G0, U0, D0, G1, U1, D1 = (ffn_unit(part, which) for part in range(2) for which in range(3))
 UNITS = OUT + 1 + 3 * CHUNKS
-EARLY = (G0, U0, D0)
-
-
-class Reducer:
-    def __init__(self, s):
-        self.s, self.done = s, {unit: 0 for unit in range(UNITS)}
-
-    def plan(self, *units):
-        todo = []
-        for unit in units:
-            todo.append((STEPS[self.done[unit]], unit))
-            self.done[unit] += 1
-        return todo
-
-    def run(self, *units):
-        act_all(self.s, self.plan(*units))
+EARLY = tuple(range(4, 10))
+ACTS = {"o": ag_open, "r": ag_relay, "c": ag_corner, "x": ag_close, "n": ag_near, "f": ag_far, 1: rs_1, 2: rs_2, 3: rs_3, 4: rs_4, 5: rs_5, 6: rs_6, 7: rs_7, 8: rs_8}
 
 
 def act_all(s, todo):
     for act, unit in todo if s.comm else ():
-        act(s, unit)
-
-
-def at_step(s, index, steps):
-    for number, todo in enumerate(steps):
-        if todo and s.comm:
-
-            @pl.when(index == number)
-            def _():
+        ACTS[act](s, unit)
+
+
+def hook(s, phase, index):
+    entries = sorted((number, todo) for (name, number), todo in PLAN.items() if name == phase)
+    if not s.comm:
+        return
+    if isinstance(index, int):
+        for number, todo in entries:
+            if number == index:
                 act_all(s, todo)
-
-
-def gather(*names):
-    kinds = dict(o=ag_open, r=ag_relay, c=ag_corner, x=ag_close, s=ag_sent)
-    return [(kinds[kind], unit) for kind, unit in names]
+        return
+
+    def pick(some):
+        if len(some) == 1:
+            pl.when(index == some[0][0])(functools.partial(act_all, s, some[0][1]))
+        elif some:
+            middle = len(some) // 2
+            pl.when(index < some[middle][0])(lambda: pick(some[:middle]))
+            pl.when(index >= some[middle][0])(lambda: pick(some[middle:]))
+
+    pick(entries)
 
 
 def gains_in(s):
@@ -695,10 +799,14 @@
         setattr(s, name, ref)
     s.pieces = [getattr(s, n + "_in") for n in NAMES]
     comm = s.comm
+    s.hook = functools.partial(hook, s)
     load_x = pltpu.make_async_copy(s.x_in, s.x, s.io_sems.at[0])
     load_c = pltpu.make_async_copy(s.c_in, s.c, s.io_sems.at[1])
-    load_x.start()
-    load_c.start()
+    tiny_loads = [
+        pltpu.make_async_copy(getattr(s, name + "_in"), getattr(s, name), s.tiny_sems.at[i])
+        for i, name in enumerate(("gain_one", "gain_two", "seg", "bucket", "table"))]
+    for copy in tiny_loads + [load_x, load_c]:
+        copy.start()
     Q, K, V, O = range(4)
     if comm:
         place(s)
@@ -707,7 +815,9 @@
         for unit in range(UNITS):
             for copy in own_copies(s, unit):
                 copy.start()
-        act_all(s, gather(("o", Q), ("o", K)))
+        s.hook("start", 0)
+        for copy in tiny_loads:
+            copy.wait()
         s.gain_from[...] = jnp.zeros_like(s.gain_from)
         gains_in(s)
         swap_open(s, "gain", s.plane, s.me)
@@ -715,6 +825,8 @@
         weights = [pltpu.make_async_copy(piece, getattr(s, n), s.load_sems.at[i]) for i, (n, piece) in enumerate(zip(NAMES, s.pieces))]
         for copy in weights:
             copy.start()
+        for copy in tiny_loads:
+            copy.wait()
         gains_in(s)
     s.small[...] = jnp.zeros_like(s.small)
     s.near_from[...] = jnp.zeros_like(s.near_from)
@@ -722,8 +834,8 @@
     tw, wt = (s.tokens, s.width), (s.width, s.tokens)
     vm = pltpu.VMEM
 
-    def attention(a, mask):
-        s.a, s.mask = a, mask
+    def attention(a, mask, toep):
+        s.a, s.mask, s.toep = a, mask, toep
         masks(s)
         load_x.wait()
         if comm:
@@ -732,48 +844,40 @@
             for copy in weights:
                 copy.wait()
         norm_in(s, 128)
-        act_all(s, gather(("r", Q), ("o", V), ("r", K), ("c", Q), ("o", O), ("r", V), ("c", K), ("o", G0), ("x", Q)))
-        project(s, Q, 256)
-        act_all(s, gather(("c", V), ("x", K)))
-        project(s, K, 256)
-        act_all(s, gather(("r", O), ("o", U0), ("x", V)))
-        project(s, V, 256)
-        plan = [
-            gather(("c", O), ("r", G0)), gather(("o", D0)), gather(("c", G0), ("r", U0), ("o", G1)), gather(("c", U0)),
-            gather(("r", D0), ("o", U1)), gather(("c", D0), ("r", G1), ("o", D1))]
-
-        def step(i):
-            at_step(s, i, plan)
-            attend_pair(s, i)
-
-        loop(s.heads // 2, step)
-
-    pl.run_scoped(attention, vm(tw, BF), vm((s.micro, s.length, s.length), F32))
-    reducer = Reducer(s)
-    reduce = reducer.run
+        pairs = s.heads // 4
+        for part in range(2):
+            side = (s.col if part == 0 else s.col_y) if comm else part
+            for w in (Q, K, V):
+                s.hook("project", 3 * part + w)
+                project(s, w, side, 256)
+            loop(pairs, functools.partial(attend_pair, s, side, 2 * pairs * part))
+
+    skew = vm((128, 2 * s.length), F32)
+    pl.run_scoped(attention, vm(tw, BF), vm((s.micro, s.length, s.length), F32), skew)
     s.n2t = s.vt
 
     def feed(act, mid, y, ct):
         s.mid, s.y, s.ct = mid, y, ct
         s.hid, s.dg, s.du = (act.at[:, i * s.ft : (i + 1) * s.ft] for i in range(3))
         load_c.wait()
-        act_all(s, gather(("x", O)))
+        s.hook("feed_in", 0)
         out_project(s, 256)
-        act_all(s, gather(("c", G1), ("r", U1), ("x", G0), ("x", U0), ("x", D0)))
-        plan = reducer.plan
-        ahead, amid = [[], gather(("c", U1), ("r", D1))], [gather(*[("s", u) for u in EARLY]), gather(("c", D1))]
-        ahead.append(gather(("x", G1), ("x", U1), ("x", D1)) + plan(G0, U0, D0))
-        amid.append(gather(*[("s", u) for u in (G1, U1, D1)]) + plan(G0, U0))
-        ahead.append(plan(G0, D0))
-        amid.append(plan(U0, G0))
 
         def step(t):
-            at_step(s, t, ahead)
-            ffn_rows(s, t, s.ft, 256)
-            at_step(s, t, amid)
+            ffn_rows(s, t, s.ft, s.rb)
+            s.hook("feed", 5 * t + 4)
+            if comm:
+                for part in range(CHUNKS):
+
+                    @pl.when(t == part)
+                    def _():
+                        for which in range(3):
+                            ag_sent(s, ffn_unit(part, which))
+
             ffn_grads(s, t, s.ft, s.gb)
 
         loop(s.hidden // s.ft, step)
+        s.hook("close", 0)
         ffn_close(s, 128)
 
     pl.run_scoped(feed, vm((s.tokens, 3 * s.ft), BF), vm(tw, F32), vm(tw, F32), vm(wt, BF))
@@ -781,55 +885,48 @@
     put_x = pltpu.make_async_copy(s.x, s.gi_out, s.io_sems.at[1])
     put_y.start()
 
-    def back(dot, *bufs):
-        s.do, s.dot = s.c, dot
+    def back(toep, ds, goff, *bufs):
+        s.toep, s.ds, s.goff = toep, ds, goff
+        s.do, s.dot = s.c, s.vt
         for name, ref in zip(s.rs_names, bufs):
             setattr(s, name, ref)
         if comm:
             for peer in [s.to_p, s.to_x, s.to_y] + s.stack:
                 pl.semaphore_signal(s.ready, inc=1, device_id=peer, device_id_type=MESH)
             pl.semaphore_wait(s.ready, 6)
-        reduce(G1, U1, D1, D0, U0, G0)
         put_y.wait()
         out_backward(s, 256)
-        act_all(s, gather(("s", Q), ("s", K), ("s", V), ("s", O)))
+        s.hook("outgrad", 0)
+        if comm:
+            for unit in range(4):
+                ag_sent(s, unit)
         out_grads(s, 256)
-        reduce(O, G1, D0, U0, G0)
-        plan = reducer.plan
-        reducer.done.update({0: 1, 1: 1, 2: 1})
-        ahead = [
-            plan(U1, G1), plan(D1, D0, U0, G0), plan(U1, G1, O, D0, U0, G0), plan(D1, G1, U1, U0, 0), plan(O, G1, U1, D1, D0),
-            plan(O, G1, U1, D1, D0, 0, 1)]
+        s.hook("outgrad", 1)
 
         def step(i):
-            at_step(s, i, ahead)
             attend_back(s, i)
 
             @pl.when(lax.rem(i, 2) == 1)
             def _():
-                chunk = lax.div(i, 2)
-                chunk_grads(s, chunk, 384)
-                at_step(s, chunk, [[(rs_1, unit)] for unit in range(3)])
+                chunk_grads(s, lax.div(i, 2), 384)
+                s.hook("chunk", lax.div(i, 2))
 
         loop(s.heads // 2, step)
-        reduce(2, 1, 0, O, D1, U1, G1)
+        s.hook("input", 0)
         table = table_grad(s)
         qkv_back_input(s, 256)
         put_x.start()
         small_pack(s, table)
         if comm:
             swap_open(s, "near", s.plane, s.me)
-            left = lambda: [u for u in (2, 1, 0, O, D1, U1, G1) + EARLY if reducer.done[u] < 8]
-            reduce(*left())
             s.far_from[...] = swap_close(s, "near", s.plane, s.plane_ids)
             swap_open(s, "far", s.stack, s.z)
-            while left():
-                reduce(*left())
-            s.small_out[...] = swap_close(s, "far", s.stack, s.stack_ids)
+            s.hook("tail", 0)
+            s.small_sum[...] = swap_close(s, "far", s.stack, s.stack_ids)
             for unit in range(UNITS):
                 rs_out(s, unit).wait()
         else:
-            s.small_out[...] = s.near_from[...]
+            s.small_sum[...] = s.near_from[...]
             outs = [pltpu.make_async_copy(getattr(s, n), getattr(s, n + "_out"), s.load_sems.at[i + 3]) for i, n in enumerate(NAMES[3:])]
             for copy in outs:
                 copy.start()
@@ -844,8 +941,12 @@
                     copy.start()
                     copy.wait()
 
-    pl.run_scoped(back, vm(wt, BF), *[vm(shape, BF) for shape in s.rs_shapes])
+    pl.run_scoped(
+        back, skew, vm((s.length, s.length), BF), vm((8, s.heads, 2 * s.length), F32), *[vm(shape, BF) for shape in s.rs_shapes])
+    put_small = pltpu.make_async_copy(s.small_sum, s.small_out, s.tiny_sems.at[5])
+    put_small.start()
     put_x.wait()
+    put_small.wait()
 
 
 def call_layer(comm, x, c, weights, gains, seg, bucket, table, full):
@@ -856,13 +957,13 @@
     ft, vm, sem = 512, pltpu.VMEM, pltpu.SemaphoreType.DMA
     tw, wt, tiny = (tokens, width), (width, tokens), (2 * (width // 128) + heads, 128)
     s = types.SimpleNamespace(
-        comm=comm, tokens=tokens, width=width, micro=micro, length=length, hidden=hidden, heads=heads, buckets=buckets, ft=ft, gb=256,
+        comm=comm, tokens=tokens, width=width, micro=micro, length=length, hidden=hidden, heads=heads, buckets=buckets, ft=ft, gb=768, rb=512,
         rs_names=[], rs_shapes=[])
     scratch = dict(
         x=vm(tw, BF), c=vm(tw, BF), **{n: vm(shape, BF) for n, shape in zip(NAMES, full)},
         n1t=vm(wt, BF), q=vm(tw, BF), k=vm(tw, BF), v=vm(tw, BF), kt=vm(wt, BF), vt=vm(wt, BF), ot=vm(wt, BF),
-        dn=vm(tw, F32), toep=vm((128, 2 * length), F32), ds=vm((length, length), BF), p=vm((heads * micro * length, length), BF),
-        offs=vm((heads, 2 * length), F32), goff=vm((8, heads, 2 * length), F32), gain=vm((8, width), F32), small=vm((2, width), F32), near_from=vm(tiny, F32),
+        dn=vm(tw, F32), p=vm((heads * micro * length, length), BF),
+        offs=vm((heads, 2 * length), F32), gain=vm((8, width), F32), small=vm((2, width), F32), near_from=vm(tiny, F32),
         turned=vm((1, 2 * length), jnp.int32), io_sems=sem((2,)), load_sems=sem((7,)), out_sems=sem((UNITS,)),
     )
     out_shape = [(tw, BF)] * 2
@@ -870,7 +971,7 @@
         scratch.update(
             gain_from=vm((8, 128), F32), far_from=vm(tiny, F32),
             gain_slots=vm((8, 8, 128), F32), near_slots=vm((8, *tiny), F32), far_slots=vm((4, *tiny), F32),
-            ag_send=sem((UNITS, 9)), ag_recv=sem((UNITS, 9)), own_sems=sem((UNITS, 2)), rs_send=sem((UNITS, 15)), rs_recv=sem((UNITS, 15)),
+            ag_send=sem((UNITS, 9)), ag_recv=sem((UNITS, 9)), own_sems=sem((UNITS, 2)), rs_send=sem((UNITS, 16)), rs_recv=sem((UNITS, 16)),
             gain_send=sem((7,)), gain_recv=sem((8,)), near_send=sem((7,)), near_recv=sem((8,)), far_send=sem((3,)), far_recv=sem((4,)),
             ready=pltpu.SemaphoreType.REGULAR,
         )
@@ -878,6 +979,9 @@
             rb, cb = unit_shape(s, unit)
             hb = rb // 2
             shapes = dict(pr=(2, 2, rb, cb), xa=(2, hb, cb), yb=(2, hb, cb), ya=(hb, cb), xb=(hb, cb), zi=(rb, cb), zx=(hb, cb))
+            if unit == DIRECT:
+                del shapes["zi"], shapes["zx"]
+                shapes["zq"] = (3, rb // 4, cb)
             for name, shape in shapes.items():
                 if unit in EARLY:
                     scratch[f"{name}{unit}"] = vm(shape, BF)
@@ -889,11 +993,15 @@
     else:
         out_shape += [(shape, BF) for shape in full]
         grad_names = [n + "_out" for n in NAMES]
-    ins = ["x_in", "c_in"] + [n + "_in" for n in NAMES] + ["gain_one", "gain_two", "seg", "bucket", "table"]
+    tiny_ins = dict(gain_one=gains[0], gain_two=gains[1], seg=seg, bucket=bucket, table=table)
+    for name, array in tiny_ins.items():
+        scratch[name] = vm(array.shape, array.dtype)
+    scratch.update(tiny_sems=sem((6,)), small_sum=vm(tiny, F32))
+    ins = ["x_in", "c_in"] + [n + "_in" for n in NAMES] + [name + "_in" for name in tiny_ins]
     outs = ["y_out", "gi_out"] + grad_names + ["small_out"]
     out_shape.append((tiny, F32))
     names = ins + outs + list(scratch)
-    far, near = pl.BlockSpec(memory_space=pl.ANY), pl.BlockSpec(memory_space=pltpu.VMEM)
+    far = pl.BlockSpec(memory_space=pl.ANY)
     params = dict(vmem_limit_bytes=67043328)
     if comm:
         params.update(collective_id=0, has_side_effects=True)
@@ -904,34 +1012,37 @@
 
     return pl.pallas_call(
         body, out_shape=[jax.ShapeDtypeStruct(*o) for o in out_shape],
-        in_specs=[far] * 9 + [near] * 5, out_specs=[far] * (len(outs) - 1) + [near], scratch_shapes=list(scratch.values()),
+        in_specs=[far] * len(ins), out_specs=[far] * len(outs), scratch_shapes=list(scratch.values()),
         compiler_params=pltpu.CompilerParams(**params),
     )(x, c, *weights, *gains, seg, bucket, table)
 
 
 def finish_kernel(cfg, *refs):
     s = types.SimpleNamespace(**cfg)
-    small, srcs, outs = refs[0], refs[1 : 3 + UNITS], refs[3 + UNITS : 3 + UNITS + 12]
-    bufs = refs[15 + UNITS : 15 + 2 + 2 * UNITS]
-    wide, (in_sems, out_sems) = refs[17 + 2 * UNITS : -2], refs[-2:]
+    srcs, outs = refs[: 3 + UNITS], refs[3 + UNITS : 3 + UNITS + 12]
+    bufs = refs[15 + UNITS : 15 + 3 + 2 * UNITS]
+    wide, tiny, (in_sems, out_sems) = refs[18 + 2 * UNITS : -5], refs[-5:-2], refs[-2:]
     loads = [pltpu.make_async_copy(src, buf, in_sems.at[i]) for i, (src, buf) in enumerate(zip(srcs, bufs))]
-    for i in list(range(2, len(loads))) + [0, 1]:
+    for i in [len(loads) - 1] + list(range(2, len(loads) - 1)) + [0, 1]:
         loads[i].start()
     row, col = lax.axis_index("row"), lax.axis_index("col")
     y, gi, gain_one, gq, gk, gv, go, table, gain_two, gg, gu, gd = outs
+    small, units = bufs[-1], bufs[2:-1]
+    stores = []
+
+    def leave(buf, out):
+        stores.append(pltpu.make_async_copy(buf, out, out_sems.at[len(stores)]))
+        stores[-1].start()
+
+    loads[-1].wait()
     rows = s.width // 128
     at = lax.rem(s.width - s.gain_count * (2 * row + col), s.width)
     for i, out in enumerate((gain_one, gain_two)):
         full = jnp.concatenate([small[i * rows + j : i * rows + j + 1, :] for j in range(rows)], axis=1)
-        out[...] = pltpu.roll(jnp.broadcast_to(full, (8, s.width)), at, 1)[0:1, 0 : s.gain_count]
-    table[...] = small[2 * rows : 2 * rows + s.heads, 0 : s.buckets]
-    units = bufs[2:]
-    stores = []
-
-    def leave(buf, out):
-        stores.append(pltpu.make_async_copy(buf, out, out_sems.at[len(stores)]))
-        stores[-1].start()
-
+        tiny[i][...] = pltpu.roll(jnp.broadcast_to(full, (8, s.width)), at, 1)[0:1, 0 : s.gain_count]
+        leave(tiny[i], out)
+    tiny[2][...] = small[2 * rows : 2 * rows + s.heads, 0 : s.buckets]
+    leave(tiny[2], table)
     wq, wk, wv, wo, wg, wu, wd = wide
     for unit in range(3):
         loads[2 + unit].wait()
@@ -962,9 +1073,9 @@
         copy.wait()
 
 
-def finish(small, arrays, gain_count, heads, buckets, blocks):
+def finish(arrays, gain_count, heads, buckets, blocks):
     vm, sh = pltpu.VMEM, jax.ShapeDtypeStruct
-    far, near = pl.BlockSpec(memory_space=pl.ANY), pl.BlockSpec(memory_space=pltpu.VMEM)
+    far = pl.BlockSpec(memory_space=pl.ANY)
     y, gi = arrays[:2]
     b = [sh(shape, F32) for shape in blocks]
     gain = sh((1, gain_count), F32)
@@ -972,11 +1083,12 @@
     return pl.pallas_call(
         functools.partial(finish_kernel, cfg),
         out_shape=[sh(y.shape, BF), sh(gi.shape, BF), gain, *b[:4], sh((heads, buckets), F32), gain, *b[4:]],
-        in_specs=[near] + [far] * len(arrays), out_specs=[far, far, near, far, far, far, far, near, near, far, far, far],
-        scratch_shapes=[vm(a.shape, BF) for a in arrays] + [vm(shape, F32) for shape in blocks]
-        + [pltpu.SemaphoreType.DMA((len(arrays),)), pltpu.SemaphoreType.DMA((9,))],
+        in_specs=[far] * len(arrays), out_specs=[far] * 12,
+        scratch_shapes=[vm(a.shape, a.dtype) for a in arrays] + [vm(shape, F32) for shape in blocks]
+        + [vm(gain.shape, F32)] * 2 + [vm((heads, buckets), F32)]
+        + [pltpu.SemaphoreType.DMA((len(arrays),)), pltpu.SemaphoreType.DMA((12,))],
         compiler_params=pltpu.CompilerParams(vmem_limit_bytes=67043328),
-    )(small, *arrays)
+    )(*arrays)
 
 
 def open_block(gathered, row_count, column_count):
@@ -1005,7 +1117,7 @@
     if fits:
         out = call_layer(True, x, c, pieces, gains, segment_ids, bucket[None], bias_table.T, full)
         y, gi, one, gq, gk, gv, go, table, two, gg, gu, gd = finish(
-            out[-1], out[:-1], gain_count, heads, buckets, [p.shape for p in pieces])
+            out, gain_count, heads, buckets, [p.shape for p in pieces])
         return y.reshape(block_input.shape), gi.reshape(block_input.shape), one[0], gq, gk, gv, go, table.T, two[0], gg, gu, gd
     gains = [lax.all_gather(g, plane, axis=1, tiled=True) for g in gains]
     weights = [open_block(lax.all_gather(p[None], plane, axis=0, tiled=True), row_count, column_count) for p in pieces]

time: 193 us -> 178 us (0.922)
  Pallas kernels: 192 us -> 177 us
    pallas_call x1, Pallas kernels: 185 us -> 172 us  [call_layer(): pl.pallas_call(body, out_shape=[jax.ShapeDtypeStruct(*o) for o in out_sha...]
where the time goes in v3:
time: 178 us
  Pallas kernels  177 us (99%)
    pallas_call x1, Pallas kernels, call_layer(): pl.pallas_call(body, out_shape=[jax.ShapeDtypeStruct(*o) for o in out_sha...  172 us
    pallas_call x1, Pallas kernels, finish(): pl.pallas_call(functools.partial(finish_kernel, cfg), out_shape=[sh(y.sha...  5.29 us

profile of v3, /device:TPU:0, one launch (start us, length us, event | category | flops | bytes accessed | tf_op | source)
XLA Modules:
  0.0 177.6 jit_solution(106501618772484457)
XLA Ops:
  0.6 171.5 %shard_map.229 = (bf16[1024,768]{1,0:T(8,128)(2,1)}, bf16[1024,768]{1,0:T(8,128)(2,1)}, bf16[192,384]{1,0:T(8,128)(2,1)}, bf16[192,384]{1,0:T(8,128)(2,1)}, bf16...) custom-call(bf16[1024,768]{1,0:T(8,128)(2,1)} %bitcast.11, ...), custom_call_target="tpu_custom_call" | custom-call | tf_op jit(solution)/shard_map/pallas_call | solution.py:1013
  172.2 5.3 %shard_map.230 = (bf16[1024,768]{1,0:T(8,128)(2,1)}, bf16[1024,768]{1,0:T(8,128)(2,1)}, f32[1,96]{1,0:T(1,128)}, f32[192,384]{1,0:T(8,128)}, f32[192,384]{1,0:T(...) custom-call(bf16[1024,768]{1,0:T(8,128)(2,1)} %get-tuple-element.43., ...), custom_call_target="tpu_custom_call" | custom-call | tf_op jit(solution)/shard_map/pallas_call | solution.py:1083

commit v4 on v3

--- a/solution.py
+++ b/solution.py
@@ -509,6 +509,11 @@
     s.near_from[2 * wide : 2 * wide + s.heads, 0 : s.buckets] = table
 
 
+def small_turn(s, unit):
+    s.far_from[...] = swap_close(s, "near", s.plane, s.plane_ids)
+    swap_open(s, "far", s.stack, s.z)
+
+
 DIRECT = 2
 
 
@@ -686,65 +691,65 @@
     ("start", 0): (("o", 0), ("o", 1), ("o", 2)),
     ("project", 0): (("r", 0), ("n", 0), ("o", 3)),
     ("project", 1): (("r", 1), ("n", 1)),
-    ("project", 2): (("o", 4), ("r", 2), ("n", 2), ("c", 0)),
-    ("attend", 0): (("o", 5),),
-    ("attend", 1): (("r", 3),),
-    ("attend", 2): (("c", 1), ("o", 6)),
-    ("attend", 4): (("r", 4), ("o", 7)),
-    ("attend", 5): (("c", 2),),
-    ("project", 3): (("r", 5), ("f", 0), ("o", 8)),
-    ("project", 4): (("c", 3), ("f", 1)),
-    ("project", 5): (("o", 9), ("r", 6), ("f", 2)),
-    ("attend", 6): (("c", 4), ("o", 10)),
-    ("attend", 7): (("r", 7),),
-    ("attend", 8): (("c", 5),),
-    ("attend", 9): (("o", 11),),
-    ("attend", 10): (("r", 8),),
-    ("attend", 11): (("r", 9),),
-    ("feed_in", 0): (("c", 6), ("o", 12), ("x", 3)),
-    ("feed", 0): (("c", 7), ("r", 10), ("r", 11), ("o", 13), ("x", 4), ("x", 5), ("x", 6)),
-    ("feed", 1): (("c", 8), ("c", 9), ("o", 14), ("o", 15), ("r", 12)),
-    ("feed", 4): (("c", 10), ("c", 11)),
-    ("feed", 5): (("r", 13), ("r", 14), (1, 4), (1, 5), (1, 6), ("x", 7), ("x", 8), ("x", 9)),
-    ("feed", 6): (("c", 12), ("r", 15), (2, 4)),
-    ("feed", 9): (("c", 13), ("c", 14), (2, 5), (2, 6)),
-    ("feed", 10): (("c", 15), (3, 4), (1, 7), (1, 8), (1, 9), ("x", 10), ("x", 11), ("x", 12)),
-    ("feed", 11): ((3, 5), (2, 7), (2, 8), (3, 6)),
-    ("feed", 14): ((4, 4), (2, 9), (4, 5)),
-    ("feed", 15): ((3, 7), ("x", 13), ("x", 14), ("x", 15)),
-    ("feed", 16): ((5, 4), (4, 6), (3, 8), (3, 9), (5, 5)),
-    ("feed", 19): ((4, 7),),
-    ("close", 0): ((6, 4), (6, 5), (5, 6), (4, 8), (4, 9)),
-    ("outback", 0): ((5, 7), (1, 10), (1, 11), (1, 12), (1, 13), (1, 14), (1, 15)),
-    ("outback", 1): ((7, 4),),
-    ("outback", 2): ((7, 5),),
-    ("outback", 3): ((6, 6), (5, 8), (2, 10), (2, 11), (6, 7)),
-    ("outgrad", 0): ((5, 9), (2, 12), (2, 13), (8, 4)),
-    ("outgrad", 1): ((1, 3), (8, 5), (7, 6), (2, 14), (2, 15)),
-    ("back", 1): ((7, 7), (6, 8), (3, 10)),
-    ("back", 2): ((6, 9), (3, 11), (2, 3), (8, 6)),
-    ("back", 3): ((3, 12),),
-    ("chunk", 0): ((1, 0), (8, 7), (7, 8), (7, 9), (3, 13), (3, 14)),
-    ("back", 5): ((3, 15),),
-    ("back", 6): ((4, 10), (4, 11), (2, 0)),
-    ("back", 7): ((8, 8), (8, 9)),
-    ("chunk", 1): ((1, 1), (4, 12), (4, 13), (3, 3), (5, 10), (4, 14)),
-    ("back", 9): ((5, 11), (4, 15)),
-    ("back", 10): ((2, 1),),
-    ("back", 11): ((6, 10), (5, 12), (4, 3), (3, 0)),
-    ("chunk", 2): ((1, 2), (6, 11), (5, 13), (5, 14), (7, 10)),
-    ("input", 1): ((3, 1), (6, 12), (5, 15)),
-    ("input", 2): ((4, 0), (2, 2)),
-    ("input", 3): ((7, 11), (5, 3), (8, 10), (6, 13)),
-    ("input", 4): ((6, 14), (4, 1), (7, 12)),
-    ("tail", 0): ((6, 15), (8, 11), (5, 0), (3, 2), (6, 3), (7, 13), (7, 14), (8, 12), (7, 15), (5, 1), (4, 2), (6, 0), (8, 13), (7, 3), (8, 14), (6, 1), (8, 15), (8, 3), (5, 2), (7, 0), (7, 1), (8, 0), (8, 1), (6, 2)),
+    ("project", 2): (("o", 4), ("r", 2), ("n", 2)),
+    ("attend", 0): (("c", 0),),
+    ("attend", 1): (("o", 5),),
+    ("attend", 2): (("r", 3),),
+    ("attend", 3): (("c", 1),),
+    ("attend", 4): (("o", 6),),
+    ("attend", 5): (("r", 4),),
+    ("project", 3): (("c", 2), ("o", 7), ("f", 0)),
+    ("project", 4): (("r", 5), ("f", 1)),
+    ("project", 5): (("c", 3), ("o", 8), ("f", 2)),
+    ("attend", 6): (("o", 9),),
+    ("attend", 7): (("c", 4), ("r", 6)),
+    ("attend", 9): (("r", 7),),
+    ("attend", 10): (("c", 5), ("o", 10)),
+    ("attend", 11): (("r", 8),),
+    ("feed_in", 0): (("o", 11), ("x", 3)),
+    ("feed", 0): (("c", 6), ("c", 7), ("r", 9), ("o", 12), ("x", 4), ("x", 5), ("x", 6), ("r", 10)),
+    ("feed", 1): (("c", 8), ("r", 11), ("o", 13)),
+    ("feed", 4): (("c", 9), ("r", 12), ("o", 14)),
+    ("feed", 5): (("c", 10), ("c", 11), ("o", 15), (1, 4), (1, 5), (1, 6), ("x", 7), ("x", 8), ("x", 9)),
+    ("feed", 6): (("c", 12), ("r", 13), (2, 4), (2, 5), (2, 6), ("r", 14)),
+    ("feed", 9): (("c", 13), ("r", 15)),
+    ("feed", 10): ((3, 4), (1, 7), (1, 8), (1, 9), ("x", 10), ("x", 11), ("x", 12)),
+    ("feed", 11): ((3, 5), (3, 6), (2, 7), (2, 8), (2, 9), ("c", 14)),
+    ("feed", 14): (("c", 15), (4, 4), (4, 5)),
+    ("feed", 15): ((4, 6), (1, 10), (1, 11), ("x", 13), ("x", 14), ("x", 15), (3, 7)),
+    ("feed", 16): ((5, 4), (3, 8), (2, 10), (2, 11), (5, 5)),
+    ("feed", 19): ((6, 4), (5, 6), (4, 7), (4, 8), (3, 9)),
+    ("close", 0): ((6, 5), (3, 10)),
+    ("outback", 0): ((7, 4), (6, 6), (5, 7), (4, 9), (3, 11), (1, 12), (1, 13), (1, 14), (1, 15)),
+    ("outback", 1): ((7, 5), (5, 8), (4, 10), (2, 12)),
+    ("outback", 2): ((2, 13), (2, 14)),
+    ("outback", 3): ((8, 4), (7, 6), (4, 11), (2, 15)),
+    ("outgrad", 0): ((6, 7), (5, 9)),
+    ("outgrad", 1): ((1, 3), (8, 5), (6, 8), (5, 10), (3, 12)),
+    ("back", 1): ((8, 6),),
+    ("back", 2): ((7, 7), (6, 9), (5, 11), (3, 13), (2, 3)),
+    ("back", 3): ((7, 8), (3, 14), (6, 10)),
+    ("chunk", 0): ((1, 0), (8, 7), (7, 9), (6, 11), (4, 12), (4, 13), (3, 15), (8, 8)),
+    ("back", 5): ((7, 10), (2, 0)),
+    ("back", 6): ((3, 3),),
+    ("back", 7): ((8, 9), (7, 11), (5, 12), (4, 14), (4, 15)),
+    ("chunk", 1): ((1, 1), (8, 10), (5, 13), (3, 0), (8, 11), (6, 12)),
+    ("back", 9): ((5, 14), (4, 3), (2, 1)),
+    ("back", 10): ((5, 15),),
+    ("back", 11): ((7, 12), (6, 13), (4, 0)),
+    ("chunk", 2): ((1, 2), (6, 14), (6, 15), (5, 3), (3, 1), (8, 12), (7, 13)),
+    ("input", 1): ((2, 2),),
+    ("input", 2): ((5, 0),),
+    ("input", 3): ((7, 14), (7, 15), (4, 1)),
+    ("input", 4): ((8, 13), (6, 3)),
+    ("tail", 0): ((6, 0), (3, 2), (8, 14), (8, 15), (7, 3), (5, 1), (7, 0), (4, 2), ("w", 0), (8, 3), (6, 1), (8, 0), (5, 2), (7, 1), (8, 1), (6, 2)),
 }
 
 
 NAMES = ("wq", "wk", "wv", "wo", "wg", "wu", "wd")
 UNITS = OUT + 1 + 3 * CHUNKS
-EARLY = tuple(range(4, 10))
-ACTS = {"o": ag_open, "r": ag_relay, "c": ag_corner, "x": ag_close, "n": ag_near, "f": ag_far, 1: rs_1, 2: rs_2, 3: rs_3, 4: rs_4, 5: rs_5, 6: rs_6, 7: rs_7, 8: rs_8}
+EARLY = tuple(range(4, 12))
+ACTS = {"o": ag_open, "r": ag_relay, "c": ag_corner, "x": ag_close, "n": ag_near, "f": ag_far, "w": small_turn, 1: rs_1, 2: rs_2, 3: rs_3, 4: rs_4, 5: rs_5, 6: rs_6, 7: rs_7, 8: rs_8}
 
 
 def act_all(s, todo):
@@ -800,7 +805,7 @@
     s.pieces = [getattr(s, n + "_in") for n in NAMES]
     comm = s.comm
     s.hook = functools.partial(hook, s)
-    load_x = pltpu.make_async_copy(s.x_in, s.x, s.io_sems.at[0])
+    load_x = pltpu.make_async_copy(s.x_in, s.x, s.io_sems.at[2])
     load_c = pltpu.make_async_copy(s.c_in, s.c, s.io_sems.at[1])
     tiny_loads = [
         pltpu.make_async_copy(getattr(s, name + "_in"), getattr(s, name), s.tiny_sems.at[i])
@@ -812,15 +817,15 @@
         place(s)
         s.unit_out = [getattr(s, f"unit{u}_out") for u in range(UNITS)]
         greet(s)
-        for unit in range(UNITS):
-            for copy in own_copies(s, unit):
-                copy.start()
-        s.hook("start", 0)
         for copy in tiny_loads:
             copy.wait()
         s.gain_from[...] = jnp.zeros_like(s.gain_from)
         gains_in(s)
         swap_open(s, "gain", s.plane, s.me)
+        s.hook("start", 0)
+        for unit in range(UNITS):
+            for copy in own_copies(s, unit):
+                copy.start()
     else:
         weights = [pltpu.make_async_copy(piece, getattr(s, n), s.load_sems.at[i]) for i, (n, piece) in enumerate(zip(NAMES, s.pieces))]
         for copy in weights:
@@ -858,7 +863,8 @@
 
     def feed(act, mid, y, ct):
         s.mid, s.y, s.ct = mid, y, ct
-        s.hid, s.dg, s.du = (act.at[:, i * s.ft : (i + 1) * s.ft] for i in range(3))
+        s.dg, s.du = (act.at[:, i * s.ft : (i + 1) * s.ft] for i in range(2))
+        s.hid = s.x.at[:, 0 : s.ft]
         load_c.wait()
         s.hook("feed_in", 0)
         out_project(s, 256)
@@ -880,10 +886,11 @@
         s.hook("close", 0)
         ffn_close(s, 128)
 
-    pl.run_scoped(feed, vm((s.tokens, 3 * s.ft), BF), vm(tw, F32), vm(tw, F32), vm(wt, BF))
+    pl.run_scoped(feed, vm((s.tokens, 2 * s.ft), BF), vm(tw, F32), vm(tw, F32), vm(wt, BF))
     put_y = pltpu.make_async_copy(s.c, s.y_out, s.io_sems.at[0])
     put_x = pltpu.make_async_copy(s.x, s.gi_out, s.io_sems.at[1])
     put_y.start()
+    load_x.start()
 
     def back(toep, ds, goff, *bufs):
         s.toep, s.ds, s.goff = toep, ds, goff
@@ -914,13 +921,12 @@
         loop(s.heads // 2, step)
         s.hook("input", 0)
         table = table_grad(s)
+        load_x.wait()
         qkv_back_input(s, 256)
         put_x.start()
         small_pack(s, table)
         if comm:
             swap_open(s, "near", s.plane, s.me)
-            s.far_from[...] = swap_close(s, "near", s.plane, s.plane_ids)
-            swap_open(s, "far", s.stack, s.z)
             s.hook("tail", 0)
             s.small_sum[...] = swap_close(s, "far", s.stack, s.stack_ids)
             for unit in range(UNITS):
@@ -964,7 +970,7 @@
         n1t=vm(wt, BF), q=vm(tw, BF), k=vm(tw, BF), v=vm(tw, BF), kt=vm(wt, BF), vt=vm(wt, BF), ot=vm(wt, BF),
         dn=vm(tw, F32), p=vm((heads * micro * length, length), BF),
         offs=vm((heads, 2 * length), F32), gain=vm((8, width), F32), small=vm((2, width), F32), near_from=vm(tiny, F32),
-        turned=vm((1, 2 * length), jnp.int32), io_sems=sem((2,)), load_sems=sem((7,)), out_sems=sem((UNITS,)),
+        turned=vm((1, 2 * length), jnp.int32), io_sems=sem((3,)), load_sems=sem((7,)), out_sems=sem((UNITS,)),
     )
     out_shape = [(tw, BF)] * 2
     if comm:

time: 178 us -> 162 us (0.910)
  Pallas kernels: 177 us -> 161 us
    pallas_call x1, Pallas kernels: 172 us -> 156 us  [call_layer(): pl.pallas_call(body, out_shape=[jax.ShapeDtypeStruct(*o) for o in out_sha...]
where the time goes in v4:
time: 162 us
  Pallas kernels  161 us (99%)
    pallas_call x1, Pallas kernels, call_layer(): pl.pallas_call(body, out_shape=[jax.ShapeDtypeStruct(*o) for o in out_sha...  156 us
    pallas_call x1, Pallas kernels, finish(): pl.pallas_call(functools.partial(finish_kernel, cfg), out_shape=[sh(y.sha...  5.29 us

profile of v4, /device:TPU:0, one launch (start us, length us, event | category | flops | bytes accessed | tf_op | source)
XLA Modules:
  0.0 161.7 jit_solution(15647780229074665423)
XLA Ops:
  0.6 155.6 %shard_map.229 = (bf16[1024,768]{1,0:T(8,128)(2,1)}, bf16[1024,768]{1,0:T(8,128)(2,1)}, bf16[192,384]{1,0:T(8,128)(2,1)}, bf16[192,384]{1,0:T(8,128)(2,1)}, bf16...) custom-call(bf16[1024,768]{1,0:T(8,128)(2,1)} %bitcast.11, ...), custom_call_target="tpu_custom_call" | custom-call | tf_op jit(solution)/shard_map/pallas_call | solution.py:1019
  156.2 5.3 %shard_map.230 = (bf16[1024,768]{1,0:T(8,128)(2,1)}, bf16[1024,768]{1,0:T(8,128)(2,1)}, f32[1,96]{1,0:T(1,128)}, f32[192,384]{1,0:T(8,128)}, f32[192,384]{1,0:T(...) custom-call(bf16[1024,768]{1,0:T(8,128)(2,1)} %get-tuple-element.43., ...), custom_call_target="tpu_custom_call" | custom-call | tf_op jit(solution)/shard_map/pallas_call | solution.py:1089

commit v5 on v4

--- a/solution.py
+++ b/solution.py
@@ -691,58 +691,58 @@
     ("start", 0): (("o", 0), ("o", 1), ("o", 2)),
     ("project", 0): (("r", 0), ("n", 0), ("o", 3)),
     ("project", 1): (("r", 1), ("n", 1)),
-    ("project", 2): (("o", 4), ("r", 2), ("n", 2)),
+    ("project", 2): (("r", 2), ("n", 2), ("o", 4)),
     ("attend", 0): (("c", 0),),
     ("attend", 1): (("o", 5),),
     ("attend", 2): (("r", 3),),
     ("attend", 3): (("c", 1),),
     ("attend", 4): (("o", 6),),
-    ("attend", 5): (("r", 4),),
-    ("project", 3): (("c", 2), ("o", 7), ("f", 0)),
-    ("project", 4): (("r", 5), ("f", 1)),
-    ("project", 5): (("c", 3), ("o", 8), ("f", 2)),
-    ("attend", 6): (("o", 9),),
-    ("attend", 7): (("c", 4), ("r", 6)),
-    ("attend", 9): (("r", 7),),
-    ("attend", 10): (("c", 5), ("o", 10)),
-    ("attend", 11): (("r", 8),),
-    ("feed_in", 0): (("o", 11), ("x", 3)),
-    ("feed", 0): (("c", 6), ("c", 7), ("r", 9), ("o", 12), ("x", 4), ("x", 5), ("x", 6), ("r", 10)),
-    ("feed", 1): (("c", 8), ("r", 11), ("o", 13)),
-    ("feed", 4): (("c", 9), ("r", 12), ("o", 14)),
-    ("feed", 5): (("c", 10), ("c", 11), ("o", 15), (1, 4), (1, 5), (1, 6), ("x", 7), ("x", 8), ("x", 9)),
-    ("feed", 6): (("c", 12), ("r", 13), (2, 4), (2, 5), (2, 6), ("r", 14)),
-    ("feed", 9): (("c", 13), ("r", 15)),
-    ("feed", 10): ((3, 4), (1, 7), (1, 8), (1, 9), ("x", 10), ("x", 11), ("x", 12)),
-    ("feed", 11): ((3, 5), (3, 6), (2, 7), (2, 8), (2, 9), ("c", 14)),
-    ("feed", 14): (("c", 15), (4, 4), (4, 5)),
-    ("feed", 15): ((4, 6), (1, 10), (1, 11), ("x", 13), ("x", 14), ("x", 15), (3, 7)),
-    ("feed", 16): ((5, 4), (3, 8), (2, 10), (2, 11), (5, 5)),
-    ("feed", 19): ((6, 4), (5, 6), (4, 7), (4, 8), (3, 9)),
-    ("close", 0): ((6, 5), (3, 10)),
-    ("outback", 0): ((7, 4), (6, 6), (5, 7), (4, 9), (3, 11), (1, 12), (1, 13), (1, 14), (1, 15)),
-    ("outback", 1): ((7, 5), (5, 8), (4, 10), (2, 12)),
-    ("outback", 2): ((2, 13), (2, 14)),
-    ("outback", 3): ((8, 4), (7, 6), (4, 11), (2, 15)),
-    ("outgrad", 0): ((6, 7), (5, 9)),
-    ("outgrad", 1): ((1, 3), (8, 5), (6, 8), (5, 10), (3, 12)),
-    ("back", 1): ((8, 6),),
-    ("back", 2): ((7, 7), (6, 9), (5, 11), (3, 13), (2, 3)),
-    ("back", 3): ((7, 8), (3, 14), (6, 10)),
-    ("chunk", 0): ((1, 0), (8, 7), (7, 9), (6, 11), (4, 12), (4, 13), (3, 15), (8, 8)),
-    ("back", 5): ((7, 10), (2, 0)),
-    ("back", 6): ((3, 3),),
-    ("back", 7): ((8, 9), (7, 11), (5, 12), (4, 14), (4, 15)),
-    ("chunk", 1): ((1, 1), (8, 10), (5, 13), (3, 0), (8, 11), (6, 12)),
-    ("back", 9): ((5, 14), (4, 3), (2, 1)),
-    ("back", 10): ((5, 15),),
-    ("back", 11): ((7, 12), (6, 13), (4, 0)),
-    ("chunk", 2): ((1, 2), (6, 14), (6, 15), (5, 3), (3, 1), (8, 12), (7, 13)),
-    ("input", 1): ((2, 2),),
-    ("input", 2): ((5, 0),),
-    ("input", 3): ((7, 14), (7, 15), (4, 1)),
-    ("input", 4): ((8, 13), (6, 3)),
-    ("tail", 0): ((6, 0), (3, 2), (8, 14), (8, 15), (7, 3), (5, 1), (7, 0), (4, 2), ("w", 0), (8, 3), (6, 1), (8, 0), (5, 2), (7, 1), (8, 1), (6, 2)),
+    ("attend", 5): (("c", 2),),
+    ("project", 3): (("r", 4), ("o", 7), ("f", 0)),
+    ("project", 4): (("f", 1),),
+    ("project", 5): (("r", 5), ("f", 2)),
+    ("attend", 6): (("o", 8),),
+    ("attend", 7): (("c", 3),),
+    ("attend", 8): (("r", 6),),
+    ("attend", 9): (("c", 4), ("o", 9)),
+    ("attend", 10): (("r", 7),),
+    ("attend", 11): (("c", 5), ("o", 10)),
+    ("feed_in", 0): (("x", 3),),
+    ("feed", 0): (("c", 6), ("r", 8), ("o", 11), ("o", 12), ("r", 9), ("x", 4), ("x", 5), ("x", 6)),
+    ("feed", 1): (("c", 7), ("r", 10), ("o", 13)),
+    ("feed", 4): (("c", 8), ("r", 11)),
+    ("feed", 5): (("c", 9), ("r", 12), ("o", 14), (1, 4), (1, 5), (1, 6), ("x", 7), ("x", 8), ("x", 9), ("c", 10), ("o", 15)),
+    ("feed", 6): (("r", 13), (2, 4), (2, 5), (2, 6), ("c", 11)),
+    ("feed", 9): (("c", 12), ("r", 14)),
+    ("feed", 10): (("r", 15), (1, 7), (1, 8), (1, 9), ("x", 10), ("x", 11), ("x", 12), ("c", 13)),
+    ("feed", 11): ((3, 4), (2, 7), (2, 8), (2, 9)),
+    ("feed", 14): ((3, 5), (3, 6)),
+    ("feed", 15): (("c", 14), ("c", 15), (4, 4), (1, 10), (1, 11), ("x", 13), ("x", 14), ("x", 15)),
+    ("feed", 16): ((3, 7), (3, 8), (2, 10), (2, 11)),
+    ("feed", 19): ((5, 4), (4, 5), (3, 9)),
+    ("close", 0): ((4, 6), (4, 7), (4, 8)),
+    ("outback", 0): ((6, 4), (1, 12), (1, 13), (1, 14), (1, 15), (5, 5), (3, 10)),
+    ("outback", 1): ((2, 12),),
+    ("outback", 2): ((3, 11), (2, 13), (2, 14), (5, 6)),
+    ("outback", 3): ((7, 4), (4, 9), (2, 15)),
+    ("outgrad", 0): ((6, 5), (5, 7), (4, 10)),
+    ("outgrad", 1): ((1, 3),),
+    ("back", 1): ((8, 4), (6, 6), (5, 8), (4, 11), (3, 12)),
+    ("back", 2): ((7, 5), (6, 7), (5, 9), (3, 13), (2, 3)),
+    ("back", 3): ((5, 10), (7, 6)),
+    ("chunk", 0): ((1, 0), (8, 5), (7, 7), (6, 8), (5, 11), (3, 14), (3, 15), (6, 9), (4, 12)),
+    ("back", 5): ((8, 6), (6, 10), (4, 13), (2, 0)),
+    ("back", 6): ((8, 7), (7, 8)),
+    ("back", 7): ((6, 11), (5, 12), (3, 3)),
+    ("chunk", 1): ((1, 1), (8, 8), (7, 9), (7, 10), (5, 13), (4, 14), (4, 15)),
+    ("back", 9): ((7, 11), (6, 12), (3, 0), (2, 1)),
+    ("back", 10): ((4, 3),),
+    ("back", 11): ((8, 9), (8, 10), (6, 13), (5, 14)),
+    ("chunk", 2): ((1, 2), (8, 11), (7, 12), (5, 15), (4, 0)),
+    ("input", 1): ((7, 13), (2, 2), (6, 14), (3, 1), (5, 3)),
+    ("input", 3): ((8, 12), (8, 13), (6, 15)),
+    ("input", 4): ((7, 14), (5, 0), (3, 2), (6, 3)),
+    ("tail", 0): ((7, 15), (4, 1), (8, 14), (6, 0), (4, 2), ("w", 0), (7, 3), (8, 15), (5, 1), (7, 0), (8, 3), (5, 2), (8, 0), (6, 1), (6, 2), (7, 1), (8, 1)),
 }
 
 
@@ -848,13 +848,13 @@
         else:
             for copy in weights:
                 copy.wait()
-        norm_in(s, 128)
+        norm_in(s, 256)
         pairs = s.heads // 4
         for part in range(2):
             side = (s.col if part == 0 else s.col_y) if comm else part
             for w in (Q, K, V):
                 s.hook("project", 3 * part + w)
-                project(s, w, side, 256)
+                project(s, w, side, s.tokens)
             loop(pairs, functools.partial(attend_pair, s, side, 2 * pairs * part))
 
     skew = vm((128, 2 * s.length), F32)
@@ -867,7 +867,7 @@
         s.hid = s.x.at[:, 0 : s.ft]
         load_c.wait()
         s.hook("feed_in", 0)
-        out_project(s, 256)
+        out_project(s, 512)
 
         def step(t):
             ffn_rows(s, t, s.ft, s.rb)
@@ -884,7 +884,7 @@
 
         loop(s.hidden // s.ft, step)
         s.hook("close", 0)
-        ffn_close(s, 128)
+        ffn_close(s, 256)
 
     pl.run_scoped(feed, vm((s.tokens, 2 * s.ft), BF), vm(tw, F32), vm(tw, F32), vm(wt, BF))
     put_y = pltpu.make_async_copy(s.c, s.y_out, s.io_sems.at[0])
@@ -907,7 +907,7 @@
         if comm:
             for unit in range(4):
                 ag_sent(s, unit)
-        out_grads(s, 256)
+        out_grads(s, 768)
         s.hook("outgrad", 1)
 
         def step(i):
@@ -915,7 +915,7 @@
 
             @pl.when(lax.rem(i, 2) == 1)
             def _():
-                chunk_grads(s, lax.div(i, 2), 384)
+                chunk_grads(s, lax.div(i, 2), 768)
                 s.hook("chunk", lax.div(i, 2))
 
         loop(s.heads // 2, step)

time: 162 us -> 161 us (level)
  no operation moved by 1% of the time
where the time goes in v5:
time: 161 us
  Pallas kernels  160 us (99%)
    pallas_call x1, Pallas kernels, call_layer(): pl.pallas_call(body, out_shape=[jax.ShapeDtypeStruct(*o) for o in out_sha...  155 us
    pallas_call x1, Pallas kernels, finish(): pl.pallas_call(functools.partial(finish_kernel, cfg), out_shape=[sh(y.sha...  5.29 us

profile of v5, /device:TPU:0, one launch (start us, length us, event | category | flops | bytes accessed | tf_op | source)
XLA Modules:
  0.0 160.7 jit_solution(10271720777467740270)
XLA Ops:
  0.6 154.5 %shard_map.229 = (bf16[1024,768]{1,0:T(8,128)(2,1)}, bf16[1024,768]{1,0:T(8,128)(2,1)}, bf16[192,384]{1,0:T(8,128)(2,1)}, bf16[192,384]{1,0:T(8,128)(2,1)}, bf16...) custom-call(bf16[1024,768]{1,0:T(8,128)(2,1)} %bitcast.11, ...), custom_call_target="tpu_custom_call" | custom-call | tf_op jit(solution)/shard_map/pallas_call | solution.py:1019
  155.2 5.3 %shard_map.230 = (bf16[1024,768]{1,0:T(8,128)(2,1)}, bf16[1024,768]{1,0:T(8,128)(2,1)}, f32[1,96]{1,0:T(1,128)}, f32[192,384]{1,0:T(8,128)}, f32[192,384]{1,0:T(...) custom-call(bf16[1024,768]{1,0:T(8,128)(2,1)} %get-tuple-element.43., ...), custom_call_target="tpu_custom_call" | custom-call | tf_op jit(solution)/shard_map/pallas_call | solution.py:1089

commit v6 on v5

--- a/solution.py
+++ b/solution.py
@@ -691,58 +691,57 @@
     ("start", 0): (("o", 0), ("o", 1), ("o", 2)),
     ("project", 0): (("r", 0), ("n", 0), ("o", 3)),
     ("project", 1): (("r", 1), ("n", 1)),
-    ("project", 2): (("r", 2), ("n", 2), ("o", 4)),
-    ("attend", 0): (("c", 0),),
+    ("project", 2): (("r", 2), ("n", 2), ("c", 0), ("o", 4)),
     ("attend", 1): (("o", 5),),
     ("attend", 2): (("r", 3),),
     ("attend", 3): (("c", 1),),
-    ("attend", 4): (("o", 6),),
-    ("attend", 5): (("c", 2),),
-    ("project", 3): (("r", 4), ("o", 7), ("f", 0)),
+    ("attend", 4): (("c", 2), ("o", 6)),
+    ("attend", 5): (("o", 7),),
+    ("project", 3): (("r", 4), ("f", 0)),
     ("project", 4): (("f", 1),),
     ("project", 5): (("r", 5), ("f", 2)),
-    ("attend", 6): (("o", 8),),
-    ("attend", 7): (("c", 3),),
+    ("attend", 6): (("c", 3), ("o", 8)),
     ("attend", 8): (("r", 6),),
-    ("attend", 9): (("c", 4), ("o", 9)),
-    ("attend", 10): (("r", 7),),
+    ("attend", 9): (("o", 9), ("r", 7)),
+    ("attend", 10): (("c", 4),),
     ("attend", 11): (("c", 5), ("o", 10)),
-    ("feed_in", 0): (("x", 3),),
-    ("feed", 0): (("c", 6), ("r", 8), ("o", 11), ("o", 12), ("r", 9), ("x", 4), ("x", 5), ("x", 6)),
-    ("feed", 1): (("c", 7), ("r", 10), ("o", 13)),
-    ("feed", 4): (("c", 8), ("r", 11)),
-    ("feed", 5): (("c", 9), ("r", 12), ("o", 14), (1, 4), (1, 5), (1, 6), ("x", 7), ("x", 8), ("x", 9), ("c", 10), ("o", 15)),
-    ("feed", 6): (("r", 13), (2, 4), (2, 5), (2, 6), ("c", 11)),
-    ("feed", 9): (("c", 12), ("r", 14)),
-    ("feed", 10): (("r", 15), (1, 7), (1, 8), (1, 9), ("x", 10), ("x", 11), ("x", 12), ("c", 13)),
+    ("feed_in", 0): (("o", 11), ("x", 3), ("r", 8)),
+    ("feed", 0): (("c", 6), ("r", 9), ("x", 4), ("x", 5), ("x", 6), ("c", 7), ("o", 12)),
+    ("feed", 1): (("r", 10), ("o", 13)),
+    ("feed", 4): (("c", 8), ("c", 9), ("r", 11), ("o", 14)),
+    ("feed", 5): (("r", 12), (1, 4), (1, 5), (1, 6), ("x", 7), ("x", 8), ("x", 9)),
+    ("feed", 6): (("c", 10), ("r", 13), ("o", 15), (2, 4), (2, 5), (2, 6), ("c", 11)),
+    ("feed", 9): (("r", 14),),
+    ("feed", 10): (("c", 12), ("c", 13), (1, 7), (1, 8), (1, 9), ("x", 10), ("x", 11), ("x", 12), ("r", 15)),
     ("feed", 11): ((3, 4), (2, 7), (2, 8), (2, 9)),
     ("feed", 14): ((3, 5), (3, 6)),
-    ("feed", 15): (("c", 14), ("c", 15), (4, 4), (1, 10), (1, 11), ("x", 13), ("x", 14), ("x", 15)),
-    ("feed", 16): ((3, 7), (3, 8), (2, 10), (2, 11)),
+    ("feed", 15): (("c", 14), ("c", 15), (1, 10), (1, 11), ("x", 13), ("x", 14), ("x", 15), (4, 4)),
+    ("feed", 16): ((3, 7), (2, 10), (2, 11), (3, 8)),
     ("feed", 19): ((5, 4), (4, 5), (3, 9)),
-    ("close", 0): ((4, 6), (4, 7), (4, 8)),
-    ("outback", 0): ((6, 4), (1, 12), (1, 13), (1, 14), (1, 15), (5, 5), (3, 10)),
-    ("outback", 1): ((2, 12),),
-    ("outback", 2): ((3, 11), (2, 13), (2, 14), (5, 6)),
-    ("outback", 3): ((7, 4), (4, 9), (2, 15)),
-    ("outgrad", 0): ((6, 5), (5, 7), (4, 10)),
-    ("outgrad", 1): ((1, 3),),
-    ("back", 1): ((8, 4), (6, 6), (5, 8), (4, 11), (3, 12)),
-    ("back", 2): ((7, 5), (6, 7), (5, 9), (3, 13), (2, 3)),
-    ("back", 3): ((5, 10), (7, 6)),
-    ("chunk", 0): ((1, 0), (8, 5), (7, 7), (6, 8), (5, 11), (3, 14), (3, 15), (6, 9), (4, 12)),
-    ("back", 5): ((8, 6), (6, 10), (4, 13), (2, 0)),
-    ("back", 6): ((8, 7), (7, 8)),
-    ("back", 7): ((6, 11), (5, 12), (3, 3)),
-    ("chunk", 1): ((1, 1), (8, 8), (7, 9), (7, 10), (5, 13), (4, 14), (4, 15)),
-    ("back", 9): ((7, 11), (6, 12), (3, 0), (2, 1)),
-    ("back", 10): ((4, 3),),
-    ("back", 11): ((8, 9), (8, 10), (6, 13), (5, 14)),
-    ("chunk", 2): ((1, 2), (8, 11), (7, 12), (5, 15), (4, 0)),
-    ("input", 1): ((7, 13), (2, 2), (6, 14), (3, 1), (5, 3)),
-    ("input", 3): ((8, 12), (8, 13), (6, 15)),
-    ("input", 4): ((7, 14), (5, 0), (3, 2), (6, 3)),
-    ("tail", 0): ((7, 15), (4, 1), (8, 14), (6, 0), (4, 2), ("w", 0), (7, 3), (8, 15), (5, 1), (7, 0), (8, 3), (5, 2), (8, 0), (6, 1), (6, 2), (7, 1), (8, 1)),
+    ("close", 0): ((4, 6), (4, 7)),
+    ("outback", 0): ((6, 4), (3, 10), (1, 12), (1, 13), (1, 14), (1, 15), (5, 5)),
+    ("outback", 1): ((3, 11), (2, 12), (2, 13)),
+    ("outback", 2): ((5, 6), (4, 8), (2, 14), (2, 15), (7, 4), (4, 9)),
+    ("outback", 3): ((6, 5),),
+    ("outgrad", 0): ((5, 7), (4, 10)),
+    ("outgrad", 1): ((1, 3), (6, 6), (4, 11)),
+    ("back", 1): ((8, 4), (7, 5), (5, 8), (3, 12), (2, 3)),
+    ("back", 2): ((6, 7), (5, 9), (3, 13), (7, 6)),
+    ("back", 3): ((8, 5), (6, 8), (5, 10), (3, 14)),
+    ("chunk", 0): ((1, 0), (8, 6), (7, 7), (6, 9), (5, 11), (4, 12), (3, 15)),
+    ("back", 5): ((7, 8), (6, 10), (2, 0)),
+    ("back", 6): ((3, 3), (8, 7), (7, 9)),
+    ("back", 7): ((6, 11), (5, 12), (4, 13), (4, 14)),
+    ("chunk", 1): ((1, 1), (8, 8), (8, 9), (7, 10), (4, 15)),
+    ("back", 9): ((7, 11), (6, 12), (5, 13), (3, 0), (2, 1)),
+    ("back", 10): ((4, 3), (8, 10), (5, 14)),
+    ("back", 11): ((8, 11), (7, 12)),
+    ("chunk", 2): ((1, 2), (6, 13), (6, 14), (5, 15), (4, 0)),
+    ("input", 1): ((8, 12), (5, 3), (3, 1)),
+    ("input", 2): ((2, 2),),
+    ("input", 3): ((7, 13),),
+    ("input", 4): ((7, 14), (6, 15), (5, 0), (4, 1)),
+    ("tail", 0): ((6, 3), (8, 13), (3, 2), (8, 14), (7, 15), (6, 0), (5, 1), (7, 3), (4, 2), ("w", 0), (8, 15), (7, 0), (6, 1), (8, 3), (8, 0), (5, 2), (7, 1), (8, 1), (6, 2)),
 }
 
 

time: 161 us -> 161 us (level)
  no operation moved by 1% of the time
where the time goes in v6:
time: 161 us
  Pallas kernels  160 us (99%)
    pallas_call x1, Pallas kernels, call_layer(): pl.pallas_call(body, out_shape=[jax.ShapeDtypeStruct(*o) for o in out_sha...  155 us
    pallas_call x1, Pallas kernels, finish(): pl.pallas_call(functools.partial(finish_kernel, cfg), out_shape=[sh(y.sha...  5.29 us

profile of v6, /device:TPU:0, one launch (start us, length us, event | category | flops | bytes accessed | tf_op | source)
XLA Modules:
  0.0 161.0 jit_solution(4012720786070396821)
XLA Ops:
  0.6 154.8 %shard_map.229 = (bf16[1024,768]{1,0:T(8,128)(2,1)}, bf16[1024,768]{1,0:T(8,128)(2,1)}, bf16[192,384]{1,0:T(8,128)(2,1)}, bf16[192,384]{1,0:T(8,128)(2,1)}, bf16...) custom-call(bf16[1024,768]{1,0:T(8,128)(2,1)} %bitcast.11, ...), custom_call_target="tpu_custom_call" | custom-call | tf_op jit(solution)/shard_map/pallas_call | solution.py:1018
  155.5 5.3 %shard_map.230 = (bf16[1024,768]{1,0:T(8,128)(2,1)}, bf16[1024,768]{1,0:T(8,128)(2,1)}, f32[1,96]{1,0:T(1,128)}, f32[192,384]{1,0:T(8,128)}, f32[192,384]{1,0:T(...) custom-call(bf16[1024,768]{1,0:T(8,128)(2,1)} %get-tuple-element.43., ...), custom_call_target="tpu_custom_call" | custom-call | tf_op jit(solution)/shard_map/pallas_call | solution.py:1088
